TPU v7x, 32 devices: a whole 2x2x4 slice. The times are simulated.
32 devices in a mesh: groups: 2 (over x), tok: 16 (over z, y, core).
Axes of the slice: x: 2, y: 2, z: 4, core: 2. Of those that a mesh axis runs over, the one named last changes fastest.
Arguments:
- latents: bfloat16 [2304, 1536], P(('groups', 'tok')), parts along dimension 0, may hold values from -6 to 6
- fresh_noise: bfloat16 [2304, 1536], P(('groups', 'tok')), parts along dimension 0, may hold values from -6 to 6
- levels: int32 [4], replicated, may hold values from 50 to 996, as said below
- time_weight: bfloat16 [256, 3072], replicated, may hold values from -0.375 to 0.375
- w_query: bfloat16 [1536, 768], replicated, may hold values from -1 to 1
- w_key: bfloat16 [1536, 768], replicated, may hold values from -10 to 10
- w_value: bfloat16 [1536, 768], replicated, may hold values from -0.15625 to 0.15625
- w_out: bfloat16 [768, 1536], replicated, may hold values from -0.21875 to 0.21875
Outputs:
- stepped: bfloat16 [2, 2304, 1536], P(None, ('groups', 'tok')), parts along dimension 1
- velocity: bfloat16 [2, 2304, 1536], P(None, ('groups', 'tok')), parts along dimension 1
There are 2 independent parts, one for each index of `groups`. A program takes and returns all parts, laid end to end along the dimension named above; an argument that names none is the same for every part. Nothing has to cross between parts.
Inputs may be any that keep to these rules, and one draw needn't show every extreme that they name: `levels`: strictly increasing over sections.
All inputs are finite; a program needn't handle non-finite values.
Results may differ from a plain program's by a relative error of at most 0.0095.
Values may be sent and summed in bfloat16 or wider, within the bound.
No kernel may reach another device: no remote copies, remote signals or barrier semaphores. Data moves between devices by JAX's collectives and lax.ppermute only.
A program may use at most 128 MiB of HBM per device.

v0:
```python
import functools
import math

import jax
import jax.numpy as jnp
from jax import lax
from jax.experimental import pallas as pl
from jax.experimental.pallas import tpu as pltpu
from jax.sharding import PartitionSpec as P


HEAD_DIM = 128
SECTIONS = 4
CORES = 2

epsilon = 1e-06


def permuted(block, axis, move):
    devices = range(lax.axis_size(axis))
    route = [(i, move(i)) for i in devices if move(i) is not None and move(i) in devices]
    return lax.ppermute(block, axis, route)


def level_embedding(levels, half_width):
    frequency = jnp.exp(-math.log(10000.0) * jnp.arange(half_width, dtype=jnp.float32) / half_width)
    angles = levels.astype(jnp.float32)[:, None] * frequency[None, :]
    return jnp.concatenate([jnp.cos(angles), jnp.sin(angles)], axis=1)


def embed_levels(levels, time_weight):
    return jnp.dot(
        level_embedding(levels, time_weight.shape[0] // 2),
        time_weight.astype(jnp.float32),
        precision=lax.Precision.HIGHEST,
    )


def level_steps(levels):
    previous = jnp.concatenate([jnp.zeros((1,), jnp.int32), levels[:-1]])
    return (previous - levels).astype(jnp.float32) / 1000.0


def gathered_body(latents, fresh_noise, levels, time_weight, w_query, w_key, w_value, w_out):
    local_rows = latents.shape[0]
    heads = w_query.shape[1] // HEAD_DIM
    per_section = lax.axis_size("tok") // SECTIONS
    span_rows = local_rows * per_section
    my_block = lax.axis_index("tok") // per_section
    section_ids = jnp.arange(SECTIONS, dtype=jnp.int32)
    mods = embed_levels(levels, time_weight)
    width = mods.shape[1] // 2
    shift_all, scale_all = mods[:, :width], mods[:, width:]
    chosen = section_ids == my_block
    shift_vec = jnp.sum(jnp.where(chosen[:, None], shift_all, 0.0), axis=0)
    scale_vec = jnp.sum(jnp.where(chosen[:, None], scale_all, 0.0), axis=0)
    step_size = jnp.sum(jnp.where(chosen, level_steps(levels), 0.0))

    def denoise_local(rows):
        rows_f = rows.astype(jnp.float32)
        normed = rows_f * lax.rsqrt(jnp.mean(rows_f * rows_f, axis=-1, keepdims=True) + epsilon)
        hidden = (normed * (1.0 + scale_vec) + shift_vec).astype(jnp.bfloat16)

        def project(weight):
            return jnp.dot(hidden, weight, preferred_element_type=jnp.float32).astype(jnp.bfloat16)

        queries = project(w_query).reshape(local_rows, heads, HEAD_DIM)
        keys = lax.all_gather(project(w_key), "tok", axis=0, tiled=True)
        values = lax.all_gather(project(w_value), "tok", axis=0, tiled=True)
        count = keys.shape[0]
        allowed = (jnp.arange(count, dtype=jnp.int32) // span_rows <= my_block)[None, None, :]
        scores = jnp.einsum(
            "rhd,phd->hrp",
            queries,
            keys.reshape(count, heads, HEAD_DIM),
            preferred_element_type=jnp.float32,
        ) / math.sqrt(HEAD_DIM)
        scores = jnp.where(allowed, scores, -1e30)
        best = jnp.max(scores, axis=-1)
        weights = jnp.where(allowed, jnp.exp(scores - best[..., None]), 0.0)
        denominator = jnp.sum(weights, axis=-1)
        summed = jnp.einsum(
            "hrp,phd->hrd",
            weights.astype(jnp.bfloat16),
            values.reshape(count, heads, HEAD_DIM),
            preferred_element_type=jnp.float32,
        )
        attended = (summed / denominator[..., None]).astype(jnp.bfloat16)
        attended = attended.transpose(1, 0, 2).reshape(local_rows, heads * HEAD_DIM)
        moving = jnp.dot(attended, w_out, preferred_element_type=jnp.float32)
        stepped = (rows_f + step_size * moving).astype(jnp.bfloat16)
        return (stepped, moving.astype(jnp.bfloat16))

    first, first_moving = denoise_local(latents)
    incoming = permuted(first, "tok", lambda i: i - per_section)
    second_input = jnp.where(my_block == SECTIONS - 1, fresh_noise, incoming)
    second, second_moving = denoise_local(second_input)
    return (jnp.stack([first, second]), jnp.stack([first_moving, second_moving]))


VMEM = pl.BlockSpec(memory_space=pltpu.VMEM)
SMEM = pl.BlockSpec(memory_space=pltpu.SMEM)
HBM = pl.BlockSpec(memory_space=pltpu.HBM)
LAST = SECTIONS - 1


def modulate(rows_f, scale_row, shift_row):
    normed = rows_f * lax.rsqrt(jnp.mean(rows_f * rows_f, axis=-1, keepdims=True) + epsilon)
    return (normed * (1.0 + scale_row) + shift_row).astype(jnp.bfloat16)


def dot(a, b):
    return jnp.dot(a, b, preferred_element_type=jnp.float32)


def attend(queries, pairs):
    scores = [
        lax.dot_general(queries, keys, (((1,), (1,)), ((), ())), preferred_element_type=jnp.float32)
        for keys, _ in pairs
    ]
    top = functools.reduce(jnp.maximum, [jnp.max(s, axis=-1, keepdims=True) for s in scores])
    total, summed = 0.0, 0.0
    for score, (_, values) in zip(scores, pairs):
        weights = jnp.exp2((score - top) * (math.log2(math.e) / math.sqrt(HEAD_DIM)))
        total = total + jnp.sum(weights, axis=-1, keepdims=True)
        summed = summed + dot(weights.astype(jnp.bfloat16), values)
    return summed / total


def head_columns(width):
    for head in range(width // HEAD_DIM):
        yield slice(head * HEAD_DIM, (head + 1) * HEAD_DIM), slice(
            width + head * HEAD_DIM, width + (head + 1) * HEAD_DIM
        )


def fetch_kernel(*refs, count):
    sources, embedding_ref, time_hbm = refs[:count], refs[count], refs[count + 1]
    outs, mods_ref = refs[count + 2 : 2 * count + 2], refs[2 * count + 2]
    time_ref, sem = refs[2 * count + 3 :]
    time_copy = pltpu.make_async_copy(time_hbm, time_ref, sem.at[count])
    time_copy.start()
    copies = [pltpu.make_async_copy(sources[i], outs[i], sem.at[i]) for i in range(count)]
    for c in copies:
        c.start()
    rest = embedding_ref[...]
    modulated = None
    time_copy.wait()
    for _ in range(3):
        term = rest.astype(jnp.bfloat16)
        rest = rest - term.astype(jnp.float32)
        product = dot(term, time_ref[...])
        modulated = product if modulated is None else modulated + product
    mods_ref[...] = modulated
    for c in copies:
        c.wait()


def fetch(arrays, embedding, time_weight):
    in_hbm = [pltpu.with_memory_space_constraint(a, pltpu.HBM) for a in (*arrays, time_weight)]
    return pl.pallas_call(
        functools.partial(fetch_kernel, count=len(arrays)),
        out_shape=[jax.ShapeDtypeStruct(a.shape, a.dtype) for a in arrays]
        + [jax.ShapeDtypeStruct((embedding.shape[0], time_weight.shape[1]), jnp.float32)],
        in_specs=[HBM] * len(arrays) + [VMEM, HBM],
        out_specs=[VMEM] * (len(arrays) + 1),
        scratch_shapes=[
            pltpu.VMEM(time_weight.shape, time_weight.dtype),
            pltpu.SemaphoreType.DMA((len(arrays) + 1,)),
        ],
        compiler_params=pltpu.CompilerParams(vmem_limit_bytes=6 << 20),
        cost_estimate=pl.CostEstimate(
            flops=0, bytes_accessed=sum(a.size * 2 for a in arrays), transcendentals=0
        ),
        name="fetch",
    )(*in_hbm[:-1], embedding, in_hbm[-1])


def project_kernel(where, *refs, slots):
    refs = list(refs)
    own = [refs.pop(0) for _ in slots]
    across = [refs.pop(0) for _ in slots]
    mods_ref, wk_ref, wv_ref, wq_ref, kv_ref, q_ref = refs
    depth, width = wk_ref.shape
    hidden = []
    for i, slot in enumerate(slots):
        rows_f = jnp.concatenate([own[i][...].astype(jnp.float32), across[i][...].astype(jnp.float32)])
        section = LAST if slot is None else where[0] ^ slot
        row = mods_ref[pl.ds(section, 1), :]
        hidden.append(modulate(rows_f, row[:, depth:], row[:, :depth]))
    hidden = jnp.concatenate(hidden)
    kv_ref[:, :width] = dot(hidden, wk_ref[...]).astype(jnp.bfloat16)
    kv_ref[:, width:] = dot(hidden, wv_ref[...]).astype(jnp.bfloat16)
    q_ref[...] = dot(hidden, wq_ref[...]).astype(jnp.bfloat16)


def project(where, slots, own, across, mods, weights):
    local, depth = own[0].shape
    width = weights[0].shape[1]
    rows = 2 * local * len(slots)
    return pl.pallas_call(
        functools.partial(project_kernel, slots=slots),
        out_shape=(
            jax.ShapeDtypeStruct((rows, 2 * width), jnp.bfloat16),
            jax.ShapeDtypeStruct((rows, width), jnp.bfloat16),
        ),
        in_specs=[SMEM] + [VMEM] * (2 * len(slots) + 4),
        out_specs=(VMEM, VMEM),
        compiler_params=pltpu.CompilerParams(vmem_limit_bytes=12 << 20),
        cost_estimate=pl.CostEstimate(
            flops=6 * rows * depth * width, bytes_accessed=2 << 20, transcendentals=0
        ),
        name="project",
    )(where, *own, *across, mods, *weights)


def first_kernel(where, steps, *refs, groups):
    refs = list(refs)
    take = lambda n: [refs.pop(0) for _ in range(n)]
    slots = [slot for group in groups for slot in group if slot is not None]
    kv_mine, kv_theirs, q_in = take(len(groups)), take(len(groups)), take(len(groups))
    own_in, across_in = take(len(slots)), take(len(slots))
    mods_ref, wk_ref, wv_ref, wq_ref, wo_ref = take(5)
    stepped_hbm, velocity_hbm, kv2_ref, q2_ref, next_ref = take(5)
    kv_ref, q_ref, x_ref, o_ref, v_ref, st_ref, hid_ref, sem = refs
    local = own_in[0].shape[0]
    half = 2 * local
    span = 2 * half
    depth, width = wk_ref.shape
    section = where[0]

    for g, group in enumerate(groups):
        for i, slot in enumerate(group):
            if slot is None:
                continue
            rows = slice(i * half, (i + 1) * half)
            base = pl.multiple_of((section ^ slot) * span, span)
            kv_ref[pl.ds(base, half), :] = kv_mine[g][rows, :]
            kv_ref[pl.ds(base + half, half), :] = kv_theirs[g][rows, :]
            base = pl.multiple_of((section ^ slot) * half, half)
            q_ref[pl.ds(base, half), :] = q_in[g][rows, :]
            n = slots.index(slot)
            x_ref[pl.ds(base, local), :] = own_in[n][...].astype(jnp.float32)
            x_ref[pl.ds(base + local, local), :] = across_in[n][...].astype(jnp.float32)

    def attend_rows(low, count, seen, into):
        for cols, v_cols in head_columns(width):
            out = attend(q_ref[low : low + count, cols], [(kv_ref[0:seen, cols], kv_ref[0:seen, v_cols])])
            o_ref[into : into + count, cols] = out.astype(jnp.bfloat16)

    for s in range(1, SECTIONS):
        attend_rows(s * half, half, (s + 1) * span, (s - 1) * half)
    v_ref[...] = dot(o_ref[0 : LAST * half, :], wo_ref[...])
    for s in range(1, SECTIONS):
        rows = slice((s - 1) * half, s * half)
        stepped = (x_ref[s * half : (s + 1) * half, :] + steps[s] * v_ref[rows, :]).astype(jnp.bfloat16)
        st_ref[rows, :] = stepped
        hid_ref[rows, :] = modulate(
            stepped.astype(jnp.float32), mods_ref[s - 1 : s, depth:], mods_ref[s - 1 : s, :depth]
        )
    kv2_ref[:, :width] = dot(hid_ref[...], wk_ref[...]).astype(jnp.bfloat16)
    kv2_ref[:, width:] = dot(hid_ref[...], wv_ref[...]).astype(jnp.bfloat16)

    @pl.when(section < LAST)
    def _():
        base = pl.multiple_of(section * half, half)
        q2_ref[...] = dot(hid_ref[pl.ds(base, half), :][:local], wq_ref[...]).astype(jnp.bfloat16)
        next_ref[...] = st_ref[pl.ds(base, half), :][:local]

    @pl.when(section == 0)
    def _():
        attend_rows(0, local, span, 0)
        moving = dot(o_ref[0:local, :], wo_ref[...])
        hid_ref[0:local, :] = moving.astype(jnp.bfloat16)
        st_ref[0:local, :] = (x_ref[0:local, :] + steps[0] * moving).astype(jnp.bfloat16)

    @pl.when(section > 0)
    def _():
        base = pl.multiple_of((section - 1) * half, half)
        hid_ref[0:local, :] = v_ref[pl.ds(base, half), :][:local].astype(jnp.bfloat16)
        st_ref[0:local, :] = st_ref[pl.ds(base, half), :][:local]

    copies = [
        pltpu.make_async_copy(st_ref.at[0:local, :], stepped_hbm.at[0], sem.at[0]),
        pltpu.make_async_copy(hid_ref.at[0:local, :], velocity_hbm.at[0], sem.at[1]),
    ]
    for c in copies:
        c.start()
    for c in copies:
        c.wait()


def first_round(where, steps, groups, kv_mine, kv_theirs, q, own, across, mods, weights, w_out):
    local, depth = own[0].shape
    width = weights[0].shape[1]
    half, span = 2 * local, 4 * local
    pair = jax.ShapeDtypeStruct((2, local, depth), jnp.bfloat16)
    args = [*kv_mine, *kv_theirs, *q, *own, *across, mods, *weights, w_out]
    blocks = SECTIONS
    return pl.pallas_call(
        functools.partial(first_kernel, groups=groups),
        out_shape=(
            pair,
            pair,
            jax.ShapeDtypeStruct((LAST * half, 2 * width), jnp.bfloat16),
            jax.ShapeDtypeStruct((local, width), jnp.bfloat16),
            jax.ShapeDtypeStruct((local, depth), jnp.bfloat16),
        ),
        in_specs=[SMEM, SMEM] + [VMEM] * len(args),
        out_specs=(HBM, HBM, VMEM, VMEM, VMEM),
        scratch_shapes=[
            pltpu.VMEM((blocks * span, 2 * width), jnp.bfloat16),
            pltpu.VMEM((blocks * half, width), jnp.bfloat16),
            pltpu.VMEM((blocks * half, depth), jnp.float32),
            pltpu.VMEM((LAST * half, width), jnp.bfloat16),
            pltpu.VMEM((LAST * half, depth), jnp.float32),
            pltpu.VMEM((LAST * half, depth), jnp.bfloat16),
            pltpu.VMEM((LAST * half, depth), jnp.bfloat16),
            pltpu.SemaphoreType.DMA((2,)),
        ],
        compiler_params=pltpu.CompilerParams(vmem_limit_bytes=28 << 20),
        cost_estimate=pl.CostEstimate(
            flops=12 * LAST * half * depth * width, bytes_accessed=4 << 20, transcendentals=0
        ),
        name="first_round",
    )(where, steps, *args)


def second_kernel(
    where, steps, q_ref, old_ref, mine_ref, theirs_ref, fresh_ref, fresh_q_ref, fresh_mine_ref, fresh_theirs_ref,
    wo_ref, _s, _v, stepped_hbm, velocity_hbm, o_ref, st_ref, v_ref, x_ref, sem, *, fresh_row,
):
    local, width = q_ref.shape
    section = where[0]
    for s in range(SECTIONS):

        @pl.when(section == s)
        def _():
            if s < LAST:
                seen = [(mine_ref, (s + 1) * 2 * local), (theirs_ref, (s + 1) * 2 * local)]
                queries = q_ref
                x_ref[...] = old_ref[...]
            else:
                fresh_rows = slice(fresh_row, fresh_row + 2 * local)
                seen = [(r, r.shape[0]) for r in (mine_ref, theirs_ref)]
                seen += [(r.at[fresh_rows], 2 * local) for r in (fresh_mine_ref, fresh_theirs_ref)]
                queries = fresh_q_ref.at[fresh_row : fresh_row + local]
                x_ref[...] = fresh_ref[...]
            for cols, v_cols in head_columns(width):
                out = attend(queries[:, cols], [(r[0:n, cols], r[0:n, v_cols]) for r, n in seen])
                o_ref[:, cols] = out.astype(jnp.bfloat16)

    moving = dot(o_ref[...], wo_ref[...])
    v_ref[...] = moving.astype(jnp.bfloat16)
    st_ref[...] = (x_ref[...].astype(jnp.float32) + steps[section] * moving).astype(jnp.bfloat16)
    copies = [
        pltpu.make_async_copy(st_ref, stepped_hbm.at[1], sem.at[0]),
        pltpu.make_async_copy(v_ref, velocity_hbm.at[1], sem.at[1]),
    ]
    for c in copies:
        c.start()
    for c in copies:
        c.wait()


def second_round(where, steps, q, old, mine, theirs, fresh, fresh_q, fresh_mine, fresh_theirs, fresh_row, w_out, stepped, velocity):
    local, width = q.shape
    pair = jax.ShapeDtypeStruct(stepped.shape, stepped.dtype)
    return pl.pallas_call(
        functools.partial(second_kernel, fresh_row=fresh_row),
        out_shape=(pair, pair),
        in_specs=[SMEM, SMEM] + [VMEM] * 9 + [HBM, HBM],
        out_specs=(HBM, HBM),
        scratch_shapes=[
            pltpu.VMEM((local, width), jnp.bfloat16),
            pltpu.VMEM(old.shape, jnp.bfloat16),
            pltpu.VMEM(old.shape, jnp.bfloat16),
            pltpu.VMEM(old.shape, jnp.bfloat16),
            pltpu.SemaphoreType.DMA((2,)),
        ],
        input_output_aliases={11: 0, 12: 1},
        compiler_params=pltpu.CompilerParams(vmem_limit_bytes=12 << 20),
        cost_estimate=pl.CostEstimate(
            flops=4 * local * old.shape[1] * width, bytes_accessed=4 << 20, transcendentals=0
        ),
        name="second_round",
    )(where, steps, q, old, mine, theirs, fresh, fresh_q, fresh_mine, fresh_theirs, w_out, stepped, velocity)


def chip_body(latents, fresh_noise, levels, time_weight, w_query, w_key, w_value, w_out):
    per_section = lax.axis_size("tok") // SECTIONS
    where = (lax.axis_index("tok") // per_section).astype(jnp.int32).reshape(1)

    def needs(section, source):
        return source <= section + 1

    def from_section(block, slot):
        def move(i):
            section, within = i // per_section, i % per_section
            target = section ^ slot
            return target * per_section + within if needs(target, section) else None

        return permuted(block, "tok", move)

    def chip_swap(block, slot):
        def move(i):
            section = i // per_section
            if slot is None:
                return i ^ CORES if section == LAST else None
            return i ^ CORES if needs(section, section ^ slot) else None

        return permuted(block, "tok", move)

    def core_swap(block):
        return permuted(block, "tok", lambda i: i ^ 1)

    def after(value, *others):
        return lax.optimization_barrier((value, *others))[0]

    embedding, steps = lax.optimization_barrier(
        (level_embedding(levels, time_weight.shape[0] // 2), level_steps(levels))
    )
    w_key, w_value, w_query, w_out, mods = fetch(
        (w_key, w_value, w_query, w_out), embedding, time_weight
    )
    weights = (w_key, w_value, w_query)

    groups = ((0, None), (1, 3), (2,))
    own = {0: latents, None: fresh_noise}
    for slot in (3, 1, 2):
        own[slot] = from_section(latents, slot)
    across = {slot: chip_swap(own[slot], slot) for slot in (0, None, 1, 3)}
    mine, theirs, q = {}, {}, {}

    def work(group):
        mine[group], q[group] = project(
            where, group, [own[x] for x in group], [across[x] for x in group], mods, weights
        )
        theirs[group] = core_swap(mine[group])

    work(groups[0])
    own[2] = after(own[2], own[3], mine[groups[0]])
    across[2] = chip_swap(own[2], 2)
    work(groups[1])
    across[2] = after(across[2], theirs[groups[0]], mine[groups[1]])
    work(groups[2])
    slots = [x for group in groups for x in group if x is not None]
    stepped, velocity, mine2, q2, old = first_round(
        where, steps, groups, [mine[g] for g in groups], [theirs[g] for g in groups], [q[g] for g in groups],
        [own[x] for x in slots], [across[x] for x in slots], mods, weights, w_out,
    )
    theirs2 = core_swap(mine2)
    first = groups[0]
    return second_round(
        where, steps, q2, old, mine2, theirs2, fresh_noise, q[first], mine[first], theirs[first],
        first.index(None) * 2 * latents.shape[0], w_out, stepped, velocity,
    )


def solution(mesh):
    per_section = mesh.shape["tok"] // SECTIONS
    on_chips = per_section == 2 * CORES
    rows = P(("groups", "tok"), None)
    return jax.shard_map(
        chip_body if on_chips else gathered_body,
        mesh=mesh,
        in_specs=(rows, rows, P(), P(), P(), P(), P(), P()),
        out_specs=(P(None, ("groups", "tok"), None), P(None, ("groups", "tok"), None)),
        check_vma=False,
    )
```

profile of v0, /device:TPU:31, one launch (start us, length us, event | category | flops | bytes accessed | tf_op | source)
XLA Modules:
  0.0 67.9 jit_solution(2942844850551495535)
XLA Ops:
  0.6 1.3 %collective-permute-start.3 = (bf16[72,1536]{1,0:T(8,128)(2,1)}, bf16[72,1536]{1,0:T(8,128)(2,1)S(1)}, u32[]{:S(2)}, u32[]{:S(2)}) collective-permute-start(bf16[72,1536]{1,0:T(8,128)(2,1)} %refs_9_.1), channel_id=1, source_target_pairs={{0,12},{1,13},{2,14},{3,15},{4,8},{5,9},{6,10},{7,11},{8,4},{9,5},... | collective-permute-start | bytes 663560 | tf_op jit(solution)/shard_map/ppermute | solution.py:22
  1.9 1.0 %collective-permute-start.2 = (bf16[72,1536]{1,0:T(8,128)(2,1)}, bf16[72,1536]{1,0:T(8,128)(2,1)S(1)}, u32[]{:S(2)}, u32[]{:S(2)}) collective-permute-start(bf16[72,1536]{1,0:T(8,128)(2,1)} %refs_9_.1), channel_id=1, source_target_pairs={{0,4},{1,5},{2,6},{3,7},{4,0},{5,1},{6,2},{7,3},{8,12},{9,13},{10,... | collective-permute-start | bytes 663560 | tf_op jit(solution)/shard_map/ppermute | solution.py:22
  3.0 0.2 collective-permute-start
  3.2 3.1 %collective-permute-start.1 = (bf16[72,1536]{1,0:T(8,128)(2,1)}, bf16[72,1536]{1,0:T(8,128)(2,1)S(1)}, u32[]{:S(2)}, u32[]{:S(2)}) collective-permute-start(bf16[72,1536]{1,0:T(8,128)(2,1)} %fresh_ref.1), channel_id=1, source_target_pairs={{12,14},{13,15},{14,12},{15,13},{28,30},{29,31},{30,28},{31,29}} | collective-permute-start | bytes 663560 | tf_op jit(solution)/shard_map/ppermute | solution.py:22
  6.4 0.7 convert_element_type.6
  7.0 0.1 multiply_cosine_fusion
  7.1 0.8 %fusion.1.steps = f32[4]{0:T(128)S(1)} fusion(s32[4]{0:T(128)} %param.10, s32[3]{0:T(128)} %bitcast.2, s32[1]{0:T(128)} %constant.28.clone.1), kind=kLoop, calls=%fused_computation.5 | loop fusion | flops 16 | bytes 48 | tf_op jit(solution)/shard_map/div | solution.py:41
  8.0 4.3 %fetch.1 = (bf16[1536,768]{1,0:T(8,128)(2,1)S(1)}, bf16[1536,768]{1,0:T(8,128)(2,1)S(1)}, bf16[1536,768]{1,0:T(8,128)(2,1)S(1)}, bf16[768,1536]{1,0:T(8,128)(2,1)S(1)}, f32[4,3072]{1,0:T(4,128)S(1)}) custom-call(bf16[1536,768]{1,0:T(8,128)(2,1)} %refs_0_.2, bf16[1536,768]{1,0:T(8,128)(2,1)} %refs_1_.2, bf16[1536,768]{1,0:T(8,128)(2,1)} %refs_2_.1, ...), custom_call_target="tpu_custom_call" | custom-call | bytes 9437184 | tf_op jit(solution)/shard_map/fetch/pallas_call | solution.py:161
  12.3 1.4 %collective-permute-done.1.refs_3_ = bf16[72,1536]{1,0:T(8,128)(2,1)S(1)} collective-permute-done((bf16[72,1536]{1,0:T(8,128)(2,1)}, bf16[72,1536]{1,0:T(8,128)(2,1)S(1)}, u32[]{:S(2)}, u32[]{:S(2)}) %collective-permute-start.1) | collective-permute-done | bytes 221216 | tf_op jit(solution)/shard_map/ppermute | solution.py:22
  13.7 0.0 collective-permute-done.refs_2_.refs_13_
  13.7 2.4 %project.3 = (bf16[288,1536]{1,0:T(8,128)(2,1)S(1)}, bf16[288,768]{1,0:T(8,128)(2,1)S(1)}) custom-call(s32[1]{0:T(128)} %bitcast.where, bf16[72,1536]{1,0:T(8,128)(2,1)S(1)} %copy-done.1, bf16[72,1536]{1,0:T(8,128)(2,1)S(1)} %copy-done, bf16[72,1536]{1,0:T(8,128)(2,1)S(1)} %collective-permute-done.refs_2_.refs_13_, ...), custom_call_target="tpu_custom_call" | custom-call | flops 2038431744 | bytes 2097152 | tf_op jit(solution)/shard_map/project/pallas_call | solution.py:201
  16.1 2.2 %collective-permute-start.8 = (bf16[288,1536]{1,0:T(8,128)(2,1)S(1)}, bf16[288,1536]{1,0:T(8,128)(2,1)S(1)}, u32[]{:S(2)}, u32[]{:S(2)}) collective-permute-start(bf16[288,1536]{1,0:T(8,128)(2,1)S(1)} %get-tuple-element.28.refs_0_.fresh_mine_ref), channel_id=1, source_target_pairs={{0,1},{1,0},{2,3},{3,2},{4,5},{5,4},{6,7},{7,6},{8,9},{9,8},{10,11... | collective-permute-start | bytes 2654216 | tf_op jit(solution)/shard_map/ppermute | solution.py:22
  18.3 0.0 collective-permute-done.3.refs_1_.refs_11_
  18.3 2.1 %collective-permute-start.5 = (bf16[72,1536]{1,0:T(8,128)(2,1)S(1)}, bf16[72,1536]{1,0:T(8,128)(2,1)S(1)}, u32[]{:S(2)}, u32[]{:S(2)}) collective-permute-start(bf16[72,1536]{1,0:T(8,128)(2,1)S(1)} %collective-permute-done.3.refs_1_.refs_11_), channel_id=1, source_target_pairs={{4,6},{5,7},{6,4},{7,5},{8,10},{9,11},{10,8},{11,9},{12,14},{13,15... | collective-permute-start | bytes 663560 | tf_op jit(solution)/shard_map/ppermute | solution.py:22
  20.4 0.0 collective-permute-done.2.refs_0_.refs_10_
  20.4 1.3 %collective-permute-start.4 = (bf16[72,1536]{1,0:T(8,128)(2,1)S(1)}, bf16[72,1536]{1,0:T(8,128)(2,1)S(1)}, u32[]{:S(2)}, u32[]{:S(2)}) collective-permute-start(bf16[72,1536]{1,0:T(8,128)(2,1)S(1)} %collective-permute-done.2.refs_0_.refs_10_), channel_id=1, source_target_pairs={{0,2},{1,3},{2,0},{3,1},{4,6},{5,7},{6,4},{7,5},{8,10},{9,11},{10,... | collective-permute-start | bytes 663560 | tf_op jit(solution)/shard_map/ppermute | solution.py:22
  21.7 1.3 %collective-permute-start.6 = (bf16[72,1536]{1,0:T(8,128)(2,1)S(1)}, bf16[72,1536]{1,0:T(8,128)(2,1)S(1)}, u32[]{:S(2)}, u32[]{:S(2)}) collective-permute-start(bf16[72,1536]{1,0:T(8,128)(2,1)S(1)} %copy-done.1), channel_id=1, source_target_pairs={{0,8},{1,9},{2,10},{3,11},{4,12},{5,13},{6,14},{7,15},{16,24},{17,... | collective-permute-start | bytes 663560 | tf_op jit(solution)/shard_map/ppermute | solution.py:22
  23.0 4.1 %collective-permute-done.5.refs_3_.refs_15_ = bf16[72,1536]{1,0:T(8,128)(2,1)S(1)} collective-permute-done((bf16[72,1536]{1,0:T(8,128)(2,1)S(1)}, bf16[72,1536]{1,0:T(8,128)(2,1)S(1)}, u32[]{:S(2)}, u32[]{:S(2)}) %collective-permute-start.5) | collective-permute-done | bytes 221216 | tf_op jit(solution)/shard_map/ppermute | solution.py:22
  27.1 4.7 %collective-permute-done.4.refs_2_.refs_14_ = bf16[72,1536]{1,0:T(8,128)(2,1)S(1)} collective-permute-done((bf16[72,1536]{1,0:T(8,128)(2,1)S(1)}, bf16[72,1536]{1,0:T(8,128)(2,1)S(1)}, u32[]{:S(2)}, u32[]{:S(2)}) %collective-permute-start.4) | collective-permute-done | bytes 221216 | tf_op jit(solution)/shard_map/ppermute | solution.py:22
  31.8 2.4 %project.4 = (bf16[288,1536]{1,0:T(8,128)(2,1)S(1)}, bf16[288,768]{1,0:T(8,128)(2,1)S(1)}) custom-call(s32[1]{0:T(128)} %bitcast.where, bf16[72,1536]{1,0:T(8,128)(2,1)S(1)} %collective-permute-done.2.refs_0_.refs_10_, bf16[72,1536]{1,0:T(8,128)(2,1)S(1)} %collective-permute-done.3.refs_1_.refs_11_, ...), custom_call_target="tpu_custom_call" | custom-call | flops 2038431744 | bytes 2097152 | tf_op jit(solution)/shard_map/project/pallas_call | solution.py:201
  34.3 1.0 %collective-permute-start.9 = (bf16[288,1536]{1,0:T(8,128)(2,1)S(1)}, bf16[288,1536]{1,0:T(8,128)(2,1)S(1)}, u32[]{:S(2)}, u32[]{:S(2)}) collective-permute-start(bf16[288,1536]{1,0:T(8,128)(2,1)S(1)} %get-tuple-element.29.refs_1_), channel_id=1, source_target_pairs={{0,1},{1,0},{2,3},{3,2},{4,5},{5,4},{6,7},{7,6},{8,9},{9,8},{10,11... | collective-permute-start | bytes 2654216 | tf_op jit(solution)/shard_map/ppermute | solution.py:22
  35.2 0.0 collective-permute-done.6.refs_0_.refs_12_
  35.2 2.3 %collective-permute-start.7 = (bf16[72,1536]{1,0:T(8,128)(2,1)S(1)}, bf16[72,1536]{1,0:T(8,128)(2,1)S(1)}, u32[]{:S(2)}, u32[]{:S(2)}) collective-permute-start(bf16[72,1536]{1,0:T(8,128)(2,1)S(1)} %collective-permute-done.6.refs_0_.refs_12_), channel_id=1, source_target_pairs={{8,10},{9,11},{10,8},{11,9},{12,14},{13,15},{14,12},{15,13},{24,26... | collective-permute-start | bytes 663560 | tf_op jit(solution)/shard_map/ppermute | solution.py:22
  37.5 6.5 %collective-permute-done.7.refs_1_.refs_16_ = bf16[72,1536]{1,0:T(8,128)(2,1)S(1)} collective-permute-done((bf16[72,1536]{1,0:T(8,128)(2,1)S(1)}, bf16[72,1536]{1,0:T(8,128)(2,1)S(1)}, u32[]{:S(2)}, u32[]{:S(2)}) %collective-permute-start.7) | collective-permute-done | bytes 221216 | tf_op jit(solution)/shard_map/ppermute | solution.py:22
  44.1 0.0 collective-permute-done.8.refs_3_.fresh_theirs_ref
  44.1 1.3 %project.5 = (bf16[144,1536]{1,0:T(8,128)(2,1)S(1)}, bf16[144,768]{1,0:T(8,128)(2,1)S(1)}) custom-call(s32[1]{0:T(128)} %bitcast.where, bf16[72,1536]{1,0:T(8,128)(2,1)S(1)} %collective-permute-done.6.refs_0_.refs_12_, bf16[72,1536]{1,0:T(8,128)(2,1)S(1)} %collective-permute-done.7.refs_1_.refs_16_, ...), custom_call_target="tpu_custom_call" | custom-call | flops 1019215872 | bytes 2097152 | tf_op jit(solution)/shard_map/project/pallas_call | solution.py:201
  45.4 1.0 %collective-permute-start.10 = (bf16[144,1536]{1,0:T(8,128)(2,1)S(1)}, bf16[144,1536]{1,0:T(8,128)(2,1)S(1)}, u32[]{:S(2)}, u32[]{:S(2)}) collective-permute-start(bf16[144,1536]{1,0:T(8,128)(2,1)S(1)} %get-tuple-element.32.refs_2_), channel_id=1, source_target_pairs={{0,1},{1,0},{2,3},{3,2},{4,5},{5,4},{6,7},{7,6},{8,9},{9,8},{10,11... | collective-permute-start | bytes 1327112 | tf_op jit(solution)/shard_map/ppermute | solution.py:22
  46.3 1.4 %collective-permute-done.10.refs_5_ = bf16[144,1536]{1,0:T(8,128)(2,1)S(1)} collective-permute-done((bf16[144,1536]{1,0:T(8,128)(2,1)S(1)}, bf16[144,1536]{1,0:T(8,128)(2,1)S(1)}, u32[]{:S(2)}, u32[]{:S(2)}) %collective-permute-start.10) | collective-permute-done | bytes 442400 | tf_op jit(solution)/shard_map/ppermute | solution.py:22
  47.8 12.0 %first_round.1 = (bf16[2,72,1536]{2,1,0:T(8,128)(2,1)}, bf16[2,72,1536]{2,1,0:T(8,128)(2,1)}, bf16[432,1536]{1,0:T(8,128)(2,1)S(1)}, bf16[72,768]{1,0:T(8,128)(2,1)S(1)}, bf16[72,1536]{1,0:T(8,128)(2,1)S(1)}) custom-call(s32[1]{0:T(128)} %bitcast.where, f32[4]{0:T(128)S(1)} %fusion.1.steps, bf16[288,1536]{1,0:T(8,128)(2,1)S(1)} %get-tuple-element.28.refs_0_.fresh_mine_ref, ...), custom_call_target="tpu_custom_call" | custom-call | flops 6115295232 | bytes 4194304 | tf_op jit(solution)/shard_map/first_round/pallas_call | solution.py:300
  59.8 0.5 collective-permute-start.11
  60.3 2.7 %collective-permute-done.11.theirs_ref = bf16[432,1536]{1,0:T(8,128)(2,1)S(1)} collective-permute-done((bf16[432,1536]{1,0:T(8,128)(2,1)S(1)}, bf16[432,1536]{1,0:T(8,128)(2,1)S(1)}, u32[]{:S(2)}, u32[]{:S(2)}) %collective-permute-start.11) | collective-permute-done | bytes 1327136 | tf_op jit(solution)/shard_map/ppermute | solution.py:22
  63.0 4.8 %second_round.1 = (bf16[2,72,1536]{2,1,0:T(8,128)(2,1)}, bf16[2,72,1536]{2,1,0:T(8,128)(2,1)}) custom-call(s32[1]{0:T(128)} %bitcast.where, f32[4]{0:T(128)S(1)} %fusion.1.steps, bf16[72,768]{1,0:T(8,128)(2,1)S(1)} %get-tuple-element.37.q_ref, bf16[72,1536]{1,0:T(8,128)(2,1)S(1)} %get-tuple-element.38.old_ref, ...), custom_call_target="tpu_custom_call", output_to_operand_aliasing={{0}: (11, {}), {1}: (12, {})} | custom-call | flops 339738624 | bytes 4194304 | tf_op jit(solution)/shard_map/second_round/pallas_call | solution.py:369
  (7 shorter events, 0.0 us)
Async XLA Ops:
  0.6 17.6 %collective-permute-start.3 = (bf16[72,1536]{1,0:T(8,128)(2,1)}, bf16[72,1536]{1,0:T(8,128)(2,1)S(1)}, u32[]{:S(2)}, u32[]{:S(2)}) collective-permute-start(bf16[72,1536]{1,0:T(8,128)(2,1)} %refs_9_.1), channel_id=1, source_target_pairs={{0,12},{1,13},{2,14},{3,15},{4,8},{5,9},{6,10},{7,11},{8,4},{9,5},... | collective-permute-start | bytes 663560 | tf_op jit(solution)/shard_map/ppermute | solution.py:22
  1.9 18.5 %collective-permute-start.2 = (bf16[72,1536]{1,0:T(8,128)(2,1)}, bf16[72,1536]{1,0:T(8,128)(2,1)S(1)}, u32[]{:S(2)}, u32[]{:S(2)}) collective-permute-start(bf16[72,1536]{1,0:T(8,128)(2,1)} %refs_9_.1), channel_id=1, source_target_pairs={{0,4},{1,5},{2,6},{3,7},{4,0},{5,1},{6,2},{7,3},{8,12},{9,13},{10,... | collective-permute-start | bytes 663560 | tf_op jit(solution)/shard_map/ppermute | solution.py:22
  3.0 10.7 %collective-permute-start = (bf16[72,1536]{1,0:T(8,128)(2,1)}, bf16[72,1536]{1,0:T(8,128)(2,1)S(1)}, u32[]{:S(2)}, u32[]{:S(2)}) collective-permute-start(bf16[72,1536]{1,0:T(8,128)(2,1)} %refs_9_.1), channel_id=1, source_target_pairs={{0,2},{1,3},{2,0},{3,1},{4,6},{5,7},{6,4},{7,5},{8,10},{9,11},{10,... | collective-permute-start | bytes 663560 | tf_op jit(solution)/shard_map/ppermute | solution.py:22
  3.2 10.5 %collective-permute-start.1 = (bf16[72,1536]{1,0:T(8,128)(2,1)}, bf16[72,1536]{1,0:T(8,128)(2,1)S(1)}, u32[]{:S(2)}, u32[]{:S(2)}) collective-permute-start(bf16[72,1536]{1,0:T(8,128)(2,1)} %fresh_ref.1), channel_id=1, source_target_pairs={{12,14},{13,15},{14,12},{15,13},{28,30},{29,31},{30,28},{31,29}} | collective-permute-start | bytes 663560 | tf_op jit(solution)/shard_map/ppermute | solution.py:22
  7.9 5.7 %copy-start = (bf16[72,1536]{1,0:T(8,128)(2,1)S(1)}, bf16[72,1536]{1,0:T(8,128)(2,1)}, u32[]{:S(2)}) copy-start(bf16[72,1536]{1,0:T(8,128)(2,1)} %fresh_ref.1) | copy-start | bytes 663556
  8.0 5.7 %copy-start.1 = (bf16[72,1536]{1,0:T(8,128)(2,1)S(1)}, bf16[72,1536]{1,0:T(8,128)(2,1)}, u32[]{:S(2)}) copy-start(bf16[72,1536]{1,0:T(8,128)(2,1)} %refs_9_.1) | copy-start | bytes 663556
  16.1 28.0 %collective-permute-start.8 = (bf16[288,1536]{1,0:T(8,128)(2,1)S(1)}, bf16[288,1536]{1,0:T(8,128)(2,1)S(1)}, u32[]{:S(2)}, u32[]{:S(2)}) collective-permute-start(bf16[288,1536]{1,0:T(8,128)(2,1)S(1)} %get-tuple-element.28.refs_0_.fresh_mine_ref), channel_id=1, source_target_pairs={{0,1},{1,0},{2,3},{3,2},{4,5},{5,4},{6,7},{7,6},{8,9},{9,8},{10,11... | collective-permute-start | bytes 2654216 | tf_op jit(solution)/shard_map/ppermute | solution.py:22
  18.3 8.8 %collective-permute-start.5 = (bf16[72,1536]{1,0:T(8,128)(2,1)S(1)}, bf16[72,1536]{1,0:T(8,128)(2,1)S(1)}, u32[]{:S(2)}, u32[]{:S(2)}) collective-permute-start(bf16[72,1536]{1,0:T(8,128)(2,1)S(1)} %collective-permute-done.3.refs_1_.refs_11_), channel_id=1, source_target_pairs={{4,6},{5,7},{6,4},{7,5},{8,10},{9,11},{10,8},{11,9},{12,14},{13,15... | collective-permute-start | bytes 663560 | tf_op jit(solution)/shard_map/ppermute | solution.py:22
  20.4 11.4 %collective-permute-start.4 = (bf16[72,1536]{1,0:T(8,128)(2,1)S(1)}, bf16[72,1536]{1,0:T(8,128)(2,1)S(1)}, u32[]{:S(2)}, u32[]{:S(2)}) collective-permute-start(bf16[72,1536]{1,0:T(8,128)(2,1)S(1)} %collective-permute-done.2.refs_0_.refs_10_), channel_id=1, source_target_pairs={{0,2},{1,3},{2,0},{3,1},{4,6},{5,7},{6,4},{7,5},{8,10},{9,11},{10,... | collective-permute-start | bytes 663560 | tf_op jit(solution)/shard_map/ppermute | solution.py:22
  21.7 13.5 %collective-permute-start.6 = (bf16[72,1536]{1,0:T(8,128)(2,1)S(1)}, bf16[72,1536]{1,0:T(8,128)(2,1)S(1)}, u32[]{:S(2)}, u32[]{:S(2)}) collective-permute-start(bf16[72,1536]{1,0:T(8,128)(2,1)S(1)} %copy-done.1), channel_id=1, source_target_pairs={{0,8},{1,9},{2,10},{3,11},{4,12},{5,13},{6,14},{7,15},{16,24},{17,... | collective-permute-start | bytes 663560 | tf_op jit(solution)/shard_map/ppermute | solution.py:22
  34.3 12.1 %collective-permute-start.9 = (bf16[288,1536]{1,0:T(8,128)(2,1)S(1)}, bf16[288,1536]{1,0:T(8,128)(2,1)S(1)}, u32[]{:S(2)}, u32[]{:S(2)}) collective-permute-start(bf16[288,1536]{1,0:T(8,128)(2,1)S(1)} %get-tuple-element.29.refs_1_), channel_id=1, source_target_pairs={{0,1},{1,0},{2,3},{3,2},{4,5},{5,4},{6,7},{7,6},{8,9},{9,8},{10,11... | collective-permute-start | bytes 2654216 | tf_op jit(solution)/shard_map/ppermute | solution.py:22
  35.2 8.8 %collective-permute-start.7 = (bf16[72,1536]{1,0:T(8,128)(2,1)S(1)}, bf16[72,1536]{1,0:T(8,128)(2,1)S(1)}, u32[]{:S(2)}, u32[]{:S(2)}) collective-permute-start(bf16[72,1536]{1,0:T(8,128)(2,1)S(1)} %collective-permute-done.6.refs_0_.refs_12_), channel_id=1, source_target_pairs={{8,10},{9,11},{10,8},{11,9},{12,14},{13,15},{14,12},{15,13},{24,26... | collective-permute-start | bytes 663560 | tf_op jit(solution)/shard_map/ppermute | solution.py:22
  45.4 2.4 %collective-permute-start.10 = (bf16[144,1536]{1,0:T(8,128)(2,1)S(1)}, bf16[144,1536]{1,0:T(8,128)(2,1)S(1)}, u32[]{:S(2)}, u32[]{:S(2)}) collective-permute-start(bf16[144,1536]{1,0:T(8,128)(2,1)S(1)} %get-tuple-element.32.refs_2_), channel_id=1, source_target_pairs={{0,1},{1,0},{2,3},{3,2},{4,5},{5,4},{6,7},{7,6},{8,9},{9,8},{10,11... | collective-permute-start | bytes 1327112 | tf_op jit(solution)/shard_map/ppermute | solution.py:22
  59.8 3.2 %collective-permute-start.11 = (bf16[432,1536]{1,0:T(8,128)(2,1)S(1)}, bf16[432,1536]{1,0:T(8,128)(2,1)S(1)}, u32[]{:S(2)}, u32[]{:S(2)}) collective-permute-start(bf16[432,1536]{1,0:T(8,128)(2,1)S(1)} %get-tuple-element.39.mine_ref), channel_id=1, source_target_pairs={{0,1},{1,0},{2,3},{3,2},{4,5},{5,4},{6,7},{7,6},{8,9},{9,8},{10,11... | collective-permute-start | bytes 3981320 | tf_op jit(solution)/shard_map/ppermute | solution.py:22
where the time goes:
time: 68.1 us; the launch traced here: 67.9 us
  Pallas kernels  27.2 us (40%)
  waiting for transfers between devices  20.9 us (31%)
  starting transfers between devices  17.2 us (25%)
  other arithmetic  1.6 us (2%)
  between operations  0.93 us (1%)
    ppermute x12, waiting for transfers between devices, permuted(): return lax.ppermute(block, axis, route)  20.9 us
    ppermute x12, starting transfers between devices, permuted(): return lax.ppermute(block, axis, route)  17.2 us
    pallas_call x1, Pallas kernels, first_round(): pl.pallas_call(functools.partial(first_kernel, groups=groups), out_shape=...  12 us
    pallas_call x3, Pallas kernels, project(): pl.pallas_call(functools.partial(project_kernel, slots=slots), out_shape=...  6.16 us
    pallas_call x1, Pallas kernels, second_round(): pl.pallas_call(functools.partial(second_kernel, fresh_row=fresh_row), out...  4.76 us
    pallas_call x1, Pallas kernels, fetch(): pl.pallas_call(functools.partial(fetch_kernel, count=len(arrays)), out_sh...  4.3 us
  transfers between devices with their start and end apart: 12, of which 6 were waited for; matrix products, arithmetic and copies ran while one was open for 2% of the time, Pallas kernels for 15%

commit v1 on v0

--- a/solution.py
+++ b/solution.py
@@ -113,18 +113,26 @@
     return jnp.dot(a, b, preferred_element_type=jnp.float32)
 
 
-def attend(queries, pairs):
+SHARPNESS = math.log2(math.e) / math.sqrt(HEAD_DIM)
+
+
+def attend(queries, pairs, state=None):
     scores = [
         lax.dot_general(queries, keys, (((1,), (1,)), ((), ())), preferred_element_type=jnp.float32)
         for keys, _ in pairs
     ]
     top = functools.reduce(jnp.maximum, [jnp.max(s, axis=-1, keepdims=True) for s in scores])
     total, summed = 0.0, 0.0
+    if state is not None:
+        old_top, old_total, old_summed = state
+        top = jnp.maximum(top, old_top)
+        fade = jnp.exp2((old_top - top) * SHARPNESS)
+        total, summed = old_total * fade, old_summed * fade
     for score, (_, values) in zip(scores, pairs):
-        weights = jnp.exp2((score - top) * (math.log2(math.e) / math.sqrt(HEAD_DIM)))
+        weights = jnp.exp2((score - top) * SHARPNESS)
         total = total + jnp.sum(weights, axis=-1, keepdims=True)
         summed = summed + dot(weights.astype(jnp.bfloat16), values)
-    return summed / total
+    return top, total, summed
 
 
 def head_columns(width):
@@ -214,43 +222,112 @@
     )(where, *own, *across, mods, *weights)
 
 
-def first_kernel(where, steps, *refs, groups):
+def state_shapes(rows, width):
+    stat = jax.ShapeDtypeStruct((width // HEAD_DIM, rows, 1), jnp.float32)
+    return stat, stat, jax.ShapeDtypeStruct((rows, width), jnp.float32)
+
+
+def split(refs, *counts):
     refs = list(refs)
-    take = lambda n: [refs.pop(0) for _ in range(n)]
+    return [[refs.pop(0) for _ in range(n)] for n in counts] + refs
+
+
+def begin_kernel(where, *refs, groups):
     slots = [slot for group in groups for slot in group if slot is not None]
-    kv_mine, kv_theirs, q_in = take(len(groups)), take(len(groups)), take(len(groups))
-    own_in, across_in = take(len(slots)), take(len(slots))
-    mods_ref, wk_ref, wv_ref, wq_ref, wo_ref = take(5)
-    stepped_hbm, velocity_hbm, kv2_ref, q2_ref, next_ref = take(5)
-    kv_ref, q_ref, x_ref, o_ref, v_ref, st_ref, hid_ref, sem = refs
+    known = len(groups) - 1
+    kv_mine, kv_theirs, q_in, own_in, across_in, *refs = split(
+        refs, known, known, len(groups), len(slots), len(slots)
+    )
+    q_ref, x_ref, top_ref, total_ref, sum_ref, kv_ref = refs
     local = own_in[0].shape[0]
-    half = 2 * local
-    span = 2 * half
-    depth, width = wk_ref.shape
+    half, span = 2 * local, 4 * local
+    width = q_ref.shape[1]
     section = where[0]
-
+    at_last = section == LAST
     for g, group in enumerate(groups):
         for i, slot in enumerate(group):
             if slot is None:
                 continue
             rows = slice(i * half, (i + 1) * half)
-            base = pl.multiple_of((section ^ slot) * span, span)
-            kv_ref[pl.ds(base, half), :] = kv_mine[g][rows, :]
-            kv_ref[pl.ds(base + half, half), :] = kv_theirs[g][rows, :]
-            base = pl.multiple_of((section ^ slot) * half, half)
+            source = section ^ slot
+            base = pl.multiple_of(source * half, half)
             q_ref[pl.ds(base, half), :] = q_in[g][rows, :]
             n = slots.index(slot)
             x_ref[pl.ds(base, local), :] = own_in[n][...].astype(jnp.float32)
             x_ref[pl.ds(base + local, local), :] = across_in[n][...].astype(jnp.float32)
-
-    def attend_rows(low, count, seen, into):
-        for cols, v_cols in head_columns(width):
-            out = attend(q_ref[low : low + count, cols], [(kv_ref[0:seen, cols], kv_ref[0:seen, v_cols])])
-            o_ref[into : into + count, cols] = out.astype(jnp.bfloat16)
-
+            if g < known:
+                swapped = jnp.where(at_last, 1 - source, source)
+                place = jnp.where(source > 1, source - 1, jnp.where(swapped == 1, 0, LAST))
+                base = pl.multiple_of(place * span, span)
+                kv_ref[pl.ds(base, half), :] = kv_mine[g][rows, :]
+                kv_ref[pl.ds(base + half, half), :] = kv_theirs[g][rows, :]
     for s in range(1, SECTIONS):
-        attend_rows(s * half, half, (s + 1) * span, (s - 1) * half)
-    v_ref[...] = dot(o_ref[0 : LAST * half, :], wo_ref[...])
+        rows = slice((s - 1) * half, s * half)
+        for head, (cols, v_cols) in enumerate(head_columns(width)):
+            top, total, summed = attend(
+                q_ref[s * half : (s + 1) * half, cols],
+                [(kv_ref[0 : s * span, cols], kv_ref[0 : s * span, v_cols])],
+            )
+            top_ref[head, rows, :] = top
+            total_ref[head, rows, :] = total
+            sum_ref[rows, cols] = summed
+
+
+def begin_first(where, groups, kv_mine, kv_theirs, q, own, across):
+    local, depth = own[0].shape
+    width = q[0].shape[1]
+    half, span = 2 * local, 4 * local
+    args = [*kv_mine[:-1], *kv_theirs[:-1], *q, *own, *across]
+    return pl.pallas_call(
+        functools.partial(begin_kernel, groups=groups),
+        out_shape=(
+            jax.ShapeDtypeStruct((SECTIONS * half, width), jnp.bfloat16),
+            jax.ShapeDtypeStruct((SECTIONS * half, depth), jnp.float32),
+            *state_shapes(LAST * half, width),
+        ),
+        in_specs=[SMEM] + [VMEM] * len(args),
+        out_specs=(VMEM,) * 5,
+        scratch_shapes=[pltpu.VMEM((SECTIONS * span, 2 * width), jnp.bfloat16)],
+        compiler_params=pltpu.CompilerParams(vmem_limit_bytes=12 << 20),
+        cost_estimate=pl.CostEstimate(
+            flops=24 * half * span * width, bytes_accessed=2 << 20, transcendentals=0
+        ),
+        name="begin_first",
+    )(where, *args)
+
+
+def finish_kernel(where, steps, *refs, groups):
+    known = len(groups)
+    kv_mine, kv_theirs, refs_q = split(refs, known, known, 5)[:3]
+    refs = list(refs)[2 * known + 5 :]
+    q_ref, x_ref, top_ref, total_ref, sum_ref = refs_q
+    mods_ref, wk_ref, wv_ref, wo_ref = refs[:4]
+    stepped_hbm, velocity_hbm, kv2_ref, own2_ref, next_ref = refs[4:9]
+    late_ref, o_ref, v_ref, st_ref, hid_ref, out_ref, sem = refs[9:]
+    local, depth = next_ref.shape
+    half = 2 * local
+    width = wk_ref.shape[1]
+    section = where[0]
+
+    def set_late(slot):
+        for g, group in enumerate(groups):
+            if slot in group:
+                rows = slice(group.index(slot) * half, (group.index(slot) + 1) * half)
+                late_ref[0:half, :] = kv_mine[g][rows, :]
+                late_ref[half:, :] = kv_theirs[g][rows, :]
+
+    for s in range(LAST):
+        pl.when(section == s)(functools.partial(set_late, s))
+    pl.when(section == LAST)(functools.partial(set_late, LAST ^ 1))
+
+    for head, (cols, v_cols) in enumerate(head_columns(width)):
+        _, total, summed = attend(
+            q_ref[half:, cols],
+            [(late_ref[:, cols], late_ref[:, v_cols])],
+            (top_ref[head], total_ref[head], sum_ref[:, cols]),
+        )
+        o_ref[:, cols] = (summed / total).astype(jnp.bfloat16)
+    v_ref[...] = dot(o_ref[...], wo_ref[...])
     for s in range(1, SECTIONS):
         rows = slice((s - 1) * half, s * half)
         stepped = (x_ref[s * half : (s + 1) * half, :] + steps[s] * v_ref[rows, :]).astype(jnp.bfloat16)
@@ -258,31 +335,140 @@
         hid_ref[rows, :] = modulate(
             stepped.astype(jnp.float32), mods_ref[s - 1 : s, depth:], mods_ref[s - 1 : s, :depth]
         )
-    kv2_ref[:, :width] = dot(hid_ref[...], wk_ref[...]).astype(jnp.bfloat16)
-    kv2_ref[:, width:] = dot(hid_ref[...], wv_ref[...]).astype(jnp.bfloat16)
-
-    @pl.when(section < LAST)
-    def _():
-        base = pl.multiple_of(section * half, half)
-        q2_ref[...] = dot(hid_ref[pl.ds(base, half), :][:local], wq_ref[...]).astype(jnp.bfloat16)
-        next_ref[...] = st_ref[pl.ds(base, half), :][:local]
 
     @pl.when(section == 0)
     def _():
-        attend_rows(0, local, span, 0)
+        for cols, v_cols in head_columns(width):
+            _, total, summed = attend(q_ref[0:local, cols], [(late_ref[:, cols], late_ref[:, v_cols])])
+            o_ref[0:local, cols] = (summed / total).astype(jnp.bfloat16)
         moving = dot(o_ref[0:local, :], wo_ref[...])
-        hid_ref[0:local, :] = moving.astype(jnp.bfloat16)
-        st_ref[0:local, :] = (x_ref[0:local, :] + steps[0] * moving).astype(jnp.bfloat16)
+        out_ref[0] = (x_ref[0:local, :] + steps[0] * moving).astype(jnp.bfloat16)
+        out_ref[1] = moving.astype(jnp.bfloat16)
 
     @pl.when(section > 0)
     def _():
         base = pl.multiple_of((section - 1) * half, half)
-        hid_ref[0:local, :] = v_ref[pl.ds(base, half), :][:local].astype(jnp.bfloat16)
-        st_ref[0:local, :] = st_ref[pl.ds(base, half), :][:local]
+        out_ref[0] = st_ref[pl.ds(base, half), :][:local]
+        out_ref[1] = v_ref[pl.ds(base, half), :][:local].astype(jnp.bfloat16)
 
     copies = [
-        pltpu.make_async_copy(st_ref.at[0:local, :], stepped_hbm.at[0], sem.at[0]),
-        pltpu.make_async_copy(hid_ref.at[0:local, :], velocity_hbm.at[0], sem.at[1]),
+        pltpu.make_async_copy(out_ref.at[0], stepped_hbm.at[0], sem.at[0]),
+        pltpu.make_async_copy(out_ref.at[1], velocity_hbm.at[0], sem.at[1]),
+    ]
+    for c in copies:
+        c.start()
+    base = pl.multiple_of(jnp.minimum(section, LAST - 1) * half, half)
+    own2_ref[...] = hid_ref[pl.ds(base, half), :][:local]
+    next_ref[...] = st_ref[pl.ds(base, half), :][:local]
+    kv2_ref[:, :width] = dot(hid_ref[...], wk_ref[...]).astype(jnp.bfloat16)
+    kv2_ref[:, width:] = dot(hid_ref[...], wv_ref[...]).astype(jnp.bfloat16)
+    for c in copies:
+        c.wait()
+
+
+def finish_first(where, steps, groups, kv_mine, kv_theirs, begun, mods, w_key, w_value, w_out):
+    depth, width = w_key.shape
+    half = begun[0].shape[0] // SECTIONS
+    local = half // 2
+    pair = jax.ShapeDtypeStruct((2, local, depth), jnp.bfloat16)
+    one = jax.ShapeDtypeStruct((local, depth), jnp.bfloat16)
+    args = [*kv_mine, *kv_theirs, *begun, mods, w_key, w_value, w_out]
+    return pl.pallas_call(
+        functools.partial(finish_kernel, groups=groups),
+        out_shape=(pair, pair, jax.ShapeDtypeStruct((LAST * half, 2 * width), jnp.bfloat16), one, one),
+        in_specs=[SMEM, SMEM] + [VMEM] * len(args),
+        out_specs=(HBM, HBM, VMEM, VMEM, VMEM),
+        scratch_shapes=[
+            pltpu.VMEM((2 * half, 2 * width), jnp.bfloat16),
+            pltpu.VMEM((LAST * half, width), jnp.bfloat16),
+            pltpu.VMEM((LAST * half, depth), jnp.float32),
+            pltpu.VMEM((LAST * half, depth), jnp.bfloat16),
+            pltpu.VMEM((LAST * half, depth), jnp.bfloat16),
+            pltpu.VMEM((2, local, depth), jnp.bfloat16),
+            pltpu.SemaphoreType.DMA((2,)),
+        ],
+        compiler_params=pltpu.CompilerParams(vmem_limit_bytes=18 << 20),
+        cost_estimate=pl.CostEstimate(
+            flops=8 * LAST * half * depth * width, bytes_accessed=4 << 20, transcendentals=0
+        ),
+        name="finish_first",
+    )(where, steps, *args)
+
+
+def begin_second_kernel(
+    where, own_ref, wq_ref, mine_ref, fresh_q_ref, fresh_mine_ref, fresh_theirs_ref,
+    q_ref, top_ref, total_ref, sum_ref, *, fresh_row,
+):
+    local, width = q_ref.shape
+    half = 2 * local
+    section = where[0]
+
+    def run(seen):
+        for head, (cols, v_cols) in enumerate(head_columns(width)):
+            top_ref[head], total_ref[head], sum_ref[:, cols] = attend(
+                q_ref[:, cols], [(r[rows, cols], r[rows, v_cols]) for r, rows in seen]
+            )
+
+    for s in range(LAST):
+
+        @pl.when(section == s)
+        def _():
+            q_ref[...] = dot(own_ref[...], wq_ref[...]).astype(jnp.bfloat16)
+            run([(mine_ref, slice(0, (s + 1) * half))])
+
+    @pl.when(section == LAST)
+    def _():
+        fresh_rows = slice(fresh_row, fresh_row + half)
+        q_ref[...] = fresh_q_ref[fresh_row : fresh_row + local, :]
+        run([(mine_ref, slice(0, LAST * half)), (fresh_mine_ref, fresh_rows), (fresh_theirs_ref, fresh_rows)])
+
+
+def begin_second(where, own2, w_query, mine2, fresh_q, fresh_mine, fresh_theirs, fresh_row):
+    local, width = own2.shape[0], w_query.shape[1]
+    return pl.pallas_call(
+        functools.partial(begin_second_kernel, fresh_row=fresh_row),
+        out_shape=(jax.ShapeDtypeStruct((local, width), jnp.bfloat16), *state_shapes(local, width)),
+        in_specs=[SMEM] + [VMEM] * 6,
+        out_specs=(VMEM,) * 4,
+        compiler_params=pltpu.CompilerParams(vmem_limit_bytes=8 << 20),
+        cost_estimate=pl.CostEstimate(
+            flops=4 * local * own2.shape[1] * width, bytes_accessed=2 << 20, transcendentals=0
+        ),
+        name="begin_second",
+    )(where, own2, w_query, mine2, fresh_q, fresh_mine, fresh_theirs)
+
+
+def finish_second_kernel(
+    where, steps, q_ref, top_ref, total_ref, sum_ref, theirs_ref, old_ref, fresh_ref, wo_ref, _s, _v,
+    stepped_hbm, velocity_hbm, o_ref, x_ref, out_ref, sem,
+):
+    local, width = q_ref.shape
+    section = where[0]
+
+    def run(seen):
+        for head, (cols, v_cols) in enumerate(head_columns(width)):
+            _, total, summed = attend(
+                q_ref[:, cols],
+                [(theirs_ref[0:seen, cols], theirs_ref[0:seen, v_cols])],
+                (top_ref[head], total_ref[head], sum_ref[:, cols]),
+            )
+            o_ref[:, cols] = (summed / total).astype(jnp.bfloat16)
+
+    for s in range(LAST):
+        reached = (section >= s) if s == LAST - 1 else (section == s)
+        pl.when(reached)(functools.partial(run, (s + 1) * 2 * local))
+    x_ref[...] = old_ref[...]
+
+    @pl.when(section == LAST)
+    def _():
+        x_ref[...] = fresh_ref[...]
+
+    moving = dot(o_ref[...], wo_ref[...])
+    out_ref[0] = (x_ref[...].astype(jnp.float32) + steps[section] * moving).astype(jnp.bfloat16)
+    out_ref[1] = moving.astype(jnp.bfloat16)
+    copies = [
+        pltpu.make_async_copy(out_ref.at[0], stepped_hbm.at[1], sem.at[0]),
+        pltpu.make_async_copy(out_ref.at[1], velocity_hbm.at[1], sem.at[1]),
     ]
     for c in copies:
         c.start()
@@ -290,101 +476,27 @@
         c.wait()
 
 
-def first_round(where, steps, groups, kv_mine, kv_theirs, q, own, across, mods, weights, w_out):
-    local, depth = own[0].shape
-    width = weights[0].shape[1]
-    half, span = 2 * local, 4 * local
-    pair = jax.ShapeDtypeStruct((2, local, depth), jnp.bfloat16)
-    args = [*kv_mine, *kv_theirs, *q, *own, *across, mods, *weights, w_out]
-    blocks = SECTIONS
-    return pl.pallas_call(
-        functools.partial(first_kernel, groups=groups),
-        out_shape=(
-            pair,
-            pair,
-            jax.ShapeDtypeStruct((LAST * half, 2 * width), jnp.bfloat16),
-            jax.ShapeDtypeStruct((local, width), jnp.bfloat16),
-            jax.ShapeDtypeStruct((local, depth), jnp.bfloat16),
-        ),
-        in_specs=[SMEM, SMEM] + [VMEM] * len(args),
-        out_specs=(HBM, HBM, VMEM, VMEM, VMEM),
-        scratch_shapes=[
-            pltpu.VMEM((blocks * span, 2 * width), jnp.bfloat16),
-            pltpu.VMEM((blocks * half, width), jnp.bfloat16),
-            pltpu.VMEM((blocks * half, depth), jnp.float32),
-            pltpu.VMEM((LAST * half, width), jnp.bfloat16),
-            pltpu.VMEM((LAST * half, depth), jnp.float32),
-            pltpu.VMEM((LAST * half, depth), jnp.bfloat16),
-            pltpu.VMEM((LAST * half, depth), jnp.bfloat16),
-            pltpu.SemaphoreType.DMA((2,)),
-        ],
-        compiler_params=pltpu.CompilerParams(vmem_limit_bytes=28 << 20),
-        cost_estimate=pl.CostEstimate(
-            flops=12 * LAST * half * depth * width, bytes_accessed=4 << 20, transcendentals=0
-        ),
-        name="first_round",
-    )(where, steps, *args)
-
-
-def second_kernel(
-    where, steps, q_ref, old_ref, mine_ref, theirs_ref, fresh_ref, fresh_q_ref, fresh_mine_ref, fresh_theirs_ref,
-    wo_ref, _s, _v, stepped_hbm, velocity_hbm, o_ref, st_ref, v_ref, x_ref, sem, *, fresh_row,
-):
-    local, width = q_ref.shape
-    section = where[0]
-    for s in range(SECTIONS):
-
-        @pl.when(section == s)
-        def _():
-            if s < LAST:
-                seen = [(mine_ref, (s + 1) * 2 * local), (theirs_ref, (s + 1) * 2 * local)]
-                queries = q_ref
-                x_ref[...] = old_ref[...]
-            else:
-                fresh_rows = slice(fresh_row, fresh_row + 2 * local)
-                seen = [(r, r.shape[0]) for r in (mine_ref, theirs_ref)]
-                seen += [(r.at[fresh_rows], 2 * local) for r in (fresh_mine_ref, fresh_theirs_ref)]
-                queries = fresh_q_ref.at[fresh_row : fresh_row + local]
-                x_ref[...] = fresh_ref[...]
-            for cols, v_cols in head_columns(width):
-                out = attend(queries[:, cols], [(r[0:n, cols], r[0:n, v_cols]) for r, n in seen])
-                o_ref[:, cols] = out.astype(jnp.bfloat16)
-
-    moving = dot(o_ref[...], wo_ref[...])
-    v_ref[...] = moving.astype(jnp.bfloat16)
-    st_ref[...] = (x_ref[...].astype(jnp.float32) + steps[section] * moving).astype(jnp.bfloat16)
-    copies = [
-        pltpu.make_async_copy(st_ref, stepped_hbm.at[1], sem.at[0]),
-        pltpu.make_async_copy(v_ref, velocity_hbm.at[1], sem.at[1]),
-    ]
-    for c in copies:
-        c.start()
-    for c in copies:
-        c.wait()
-
-
-def second_round(where, steps, q, old, mine, theirs, fresh, fresh_q, fresh_mine, fresh_theirs, fresh_row, w_out, stepped, velocity):
-    local, width = q.shape
+def finish_second(where, steps, begun, theirs2, old, fresh, w_out, stepped, velocity):
+    local, width = begun[0].shape
     pair = jax.ShapeDtypeStruct(stepped.shape, stepped.dtype)
     return pl.pallas_call(
-        functools.partial(second_kernel, fresh_row=fresh_row),
+        finish_second_kernel,
         out_shape=(pair, pair),
-        in_specs=[SMEM, SMEM] + [VMEM] * 9 + [HBM, HBM],
+        in_specs=[SMEM, SMEM] + [VMEM] * 8 + [HBM, HBM],
         out_specs=(HBM, HBM),
         scratch_shapes=[
             pltpu.VMEM((local, width), jnp.bfloat16),
             pltpu.VMEM(old.shape, jnp.bfloat16),
-            pltpu.VMEM(old.shape, jnp.bfloat16),
-            pltpu.VMEM(old.shape, jnp.bfloat16),
+            pltpu.VMEM((2, *old.shape), jnp.bfloat16),
             pltpu.SemaphoreType.DMA((2,)),
         ],
-        input_output_aliases={11: 0, 12: 1},
-        compiler_params=pltpu.CompilerParams(vmem_limit_bytes=12 << 20),
+        input_output_aliases={10: 0, 11: 1},
+        compiler_params=pltpu.CompilerParams(vmem_limit_bytes=8 << 20),
         cost_estimate=pl.CostEstimate(
             flops=4 * local * old.shape[1] * width, bytes_accessed=4 << 20, transcendentals=0
         ),
-        name="second_round",
-    )(where, steps, q, old, mine, theirs, fresh, fresh_q, fresh_mine, fresh_theirs, w_out, stepped, velocity)
+        name="finish_second",
+    )(where, steps, *begun, theirs2, old, fresh, w_out, stepped, velocity)
 
 
 def chip_body(latents, fresh_noise, levels, time_weight, w_query, w_key, w_value, w_out):
@@ -429,7 +541,8 @@
     own = {0: latents, None: fresh_noise}
     for slot in (3, 1, 2):
         own[slot] = from_section(latents, slot)
-    across = {slot: chip_swap(own[slot], slot) for slot in (0, None, 1, 3)}
+    across = {slot: chip_swap(own[slot], slot) for slot in (0, None, 3)}
+    across[1] = from_section(across[0], 1)
     mine, theirs, q = {}, {}, {}
 
     def work(group):
@@ -445,16 +558,21 @@
     across[2] = after(across[2], theirs[groups[0]], mine[groups[1]])
     work(groups[2])
     slots = [x for group in groups for x in group if x is not None]
-    stepped, velocity, mine2, q2, old = first_round(
-        where, steps, groups, [mine[g] for g in groups], [theirs[g] for g in groups], [q[g] for g in groups],
-        [own[x] for x in slots], [across[x] for x in slots], mods, weights, w_out,
+    all_mine, all_theirs = [mine[g] for g in groups], [theirs[g] for g in groups]
+    begun = begin_first(
+        where, groups, all_mine, all_theirs, [q[g] for g in groups],
+        [own[x] for x in slots], [across[x] for x in slots],
+    )
+    stepped, velocity, mine2, own2, old = finish_first(
+        where, steps, groups, all_mine, all_theirs, begun, mods, w_key, w_value, w_out
     )
     theirs2 = core_swap(mine2)
     first = groups[0]
-    return second_round(
-        where, steps, q2, old, mine2, theirs2, fresh_noise, q[first], mine[first], theirs[first],
-        first.index(None) * 2 * latents.shape[0], w_out, stepped, velocity,
-    )
+    begun = begin_second(
+        where, own2, w_query, mine2, q[first], mine[first], theirs[first],
+        first.index(None) * 2 * latents.shape[0],
+    )
+    return finish_second(where, steps, begun, theirs2, old, fresh_noise, w_out, stepped, velocity)
 
 
 def solution(mesh):

time: 68.1 us -> 70.8 us (1.040)
  the two profiles are of different devices: /device:TPU:31 before, /device:TPU:27 now
where the time goes in v1:
time: 70.8 us; the launch traced here: 70.6 us
  Pallas kernels  32.7 us (46%)
  starting transfers between devices  17.7 us (25%)
  waiting for transfers between devices  17.6 us (25%)
  other arithmetic  1.6 us (2%)
  between operations  0.95 us (1%)
    ppermute x12, starting transfers between devices, permuted(): return lax.ppermute(block, axis, route)  17.7 us
    ppermute x12, waiting for transfers between devices, permuted(): return lax.ppermute(block, axis, route)  17.6 us
    pallas_call x1, Pallas kernels, finish_first(): pl.pallas_call(functools.partial(finish_kernel, groups=groups), out_shape...  8.95 us
    pallas_call x1, Pallas kernels, begin_first(): pl.pallas_call(functools.partial(begin_kernel, groups=groups), out_shape=...  6.42 us
    pallas_call x3, Pallas kernels, project(): pl.pallas_call(functools.partial(project_kernel, slots=slots), out_shape=...  6.29 us
    pallas_call x1, Pallas kernels, finish_second(): pl.pallas_call(finish_second_kernel, out_shape=(pair, pair), in_specs=[SM...  4.6 us
    pallas_call x1, Pallas kernels, fetch(): pl.pallas_call(functools.partial(fetch_kernel, count=len(arrays)), out_sh...  4.3 us
    pallas_call x1, Pallas kernels, begin_second(): pl.pallas_call(functools.partial(begin_second_kernel, fresh_row=fresh_row...  2.16 us
  transfers between devices with their start and end apart: 12, of which 7 were waited for; matrix products, arithmetic and copies ran while one was open for 2% of the time, Pallas kernels for 27%

profile of v1, /device:TPU:27, one launch (start us, length us, event | category | flops | bytes accessed | tf_op | source)
XLA Modules:
  0.0 70.6 jit_solution(976729627304423065)
XLA Ops:
  0.6 1.3 %collective-permute-start.3 = (bf16[72,1536]{1,0:T(8,128)(2,1)}, bf16[72,1536]{1,0:T(8,128)(2,1)S(1)}, u32[]{:S(2)}, u32[]{:S(2)}) collective-permute-start(bf16[72,1536]{1,0:T(8,128)(2,1)} %refs_7_.1), channel_id=1, source_target_pairs={{0,12},{1,13},{2,14},{3,15},{4,8},{5,9},{6,10},{7,11},{8,4},{9,5},... | collective-permute-start | bytes 663560 | tf_op jit(solution)/shard_map/ppermute | solution.py:22
  1.9 1.3 %collective-permute-start = (bf16[72,1536]{1,0:T(8,128)(2,1)}, bf16[72,1536]{1,0:T(8,128)(2,1)S(1)}, u32[]{:S(2)}, u32[]{:S(2)}) collective-permute-start(bf16[72,1536]{1,0:T(8,128)(2,1)} %refs_7_.1), channel_id=1, source_target_pairs={{0,2},{1,3},{2,0},{3,1},{4,6},{5,7},{6,4},{7,5},{8,10},{9,11},{10,... | collective-permute-start | bytes 663560 | tf_op jit(solution)/shard_map/ppermute | solution.py:22
  3.2 2.1 %collective-permute-start.1 = (bf16[72,1536]{1,0:T(8,128)(2,1)}, bf16[72,1536]{1,0:T(8,128)(2,1)S(1)}, u32[]{:S(2)}, u32[]{:S(2)}) collective-permute-start(bf16[72,1536]{1,0:T(8,128)(2,1)} %fresh_ref.1), channel_id=1, source_target_pairs={{12,14},{13,15},{14,12},{15,13},{28,30},{29,31},{30,28},{31,29}} | collective-permute-start | bytes 663560 | tf_op jit(solution)/shard_map/ppermute | solution.py:22
  5.4 0.7 convert_element_type.6
  6.1 0.1 multiply_cosine_fusion
  6.2 0.8 %fusion.1.steps = f32[4]{0:T(128)S(1)} fusion(s32[4]{0:T(128)} %param.10, s32[3]{0:T(128)} %bitcast.2, s32[1]{0:T(128)} %constant.28.clone.1), kind=kLoop, calls=%fused_computation.5 | loop fusion | flops 16 | bytes 48 | tf_op jit(solution)/shard_map/div | solution.py:41
  7.0 4.3 %fetch.1 = (bf16[1536,768]{1,0:T(8,128)(2,1)S(1)}, bf16[1536,768]{1,0:T(8,128)(2,1)S(1)}, bf16[1536,768]{1,0:T(8,128)(2,1)S(1)}, bf16[768,1536]{1,0:T(8,128)(2,1)S(1)}, f32[4,3072]{1,0:T(4,128)S(1)}) custom-call(bf16[1536,768]{1,0:T(8,128)(2,1)} %refs_0_.2, bf16[1536,768]{1,0:T(8,128)(2,1)} %refs_1_.2, bf16[1536,768]{1,0:T(8,128)(2,1)} %refs_2_.1, ...), custom_call_target="tpu_custom_call" | custom-call | bytes 9437184 | tf_op jit(solution)/shard_map/fetch/pallas_call | solution.py:169
  11.3 2.0 %collective-permute-done.1.refs_3_ = bf16[72,1536]{1,0:T(8,128)(2,1)S(1)} collective-permute-done((bf16[72,1536]{1,0:T(8,128)(2,1)}, bf16[72,1536]{1,0:T(8,128)(2,1)S(1)}, u32[]{:S(2)}, u32[]{:S(2)}) %collective-permute-start.1) | collective-permute-done | bytes 221216 | tf_op jit(solution)/shard_map/ppermute | solution.py:22
  13.3 0.0 collective-permute-done.refs_2_.refs_11_
  13.3 2.5 %project.3 = (bf16[288,1536]{1,0:T(8,128)(2,1)S(1)}, bf16[288,768]{1,0:T(8,128)(2,1)S(1)}) custom-call(s32[1]{0:T(128)} %bitcast.where, bf16[72,1536]{1,0:T(8,128)(2,1)S(1)} %copy-done, bf16[72,1536]{1,0:T(8,128)(2,1)S(1)} %copy-done.1, bf16[72,1536]{1,0:T(8,128)(2,1)S(1)} %collective-permute-done.refs_2_.refs_11_, ...), custom_call_target="tpu_custom_call" | custom-call | flops 2038431744 | bytes 2097152 | tf_op jit(solution)/shard_map/project/pallas_call | solution.py:209
  15.8 1.6 %collective-permute-start.8 = (bf16[288,1536]{1,0:T(8,128)(2,1)S(1)}, bf16[288,1536]{1,0:T(8,128)(2,1)S(1)}, u32[]{:S(2)}, u32[]{:S(2)}) collective-permute-start(bf16[288,1536]{1,0:T(8,128)(2,1)S(1)} %get-tuple-element.37.refs_0_.fresh_mine_ref), channel_id=1, source_target_pairs={{0,1},{1,0},{2,3},{3,2},{4,5},{5,4},{6,7},{7,6},{8,9},{9,8},{10,11... | collective-permute-start | bytes 2654216 | tf_op jit(solution)/shard_map/ppermute | solution.py:22
  17.3 0.0 collective-permute-start.2
  17.3 0.0 collective-permute-done.3.refs_1_.refs_9_
  17.4 3.1 %collective-permute-start.5 = (bf16[72,1536]{1,0:T(8,128)(2,1)S(1)}, bf16[72,1536]{1,0:T(8,128)(2,1)S(1)}, u32[]{:S(2)}, u32[]{:S(2)}) collective-permute-start(bf16[72,1536]{1,0:T(8,128)(2,1)S(1)} %collective-permute-done.3.refs_1_.refs_9_), channel_id=1, source_target_pairs={{4,6},{5,7},{6,4},{7,5},{8,10},{9,11},{10,8},{11,9},{12,14},{13,15... | collective-permute-start | bytes 663560 | tf_op jit(solution)/shard_map/ppermute | solution.py:22
  20.5 1.5 %collective-permute-start.4 = (bf16[72,1536]{1,0:T(8,128)(2,1)S(1)}, bf16[72,1536]{1,0:T(8,128)(2,1)S(1)}, u32[]{:S(2)}, u32[]{:S(2)}) collective-permute-start(bf16[72,1536]{1,0:T(8,128)(2,1)S(1)} %collective-permute-done.refs_2_.refs_11_), channel_id=1, source_target_pairs={{0,4},{1,5},{2,6},{3,7},{4,0},{5,1},{6,2},{7,3},{8,12},{9,13},{10,... | collective-permute-start | bytes 663560 | tf_op jit(solution)/shard_map/ppermute | solution.py:22
  22.0 1.3 %collective-permute-start.6 = (bf16[72,1536]{1,0:T(8,128)(2,1)S(1)}, bf16[72,1536]{1,0:T(8,128)(2,1)S(1)}, u32[]{:S(2)}, u32[]{:S(2)}) collective-permute-start(bf16[72,1536]{1,0:T(8,128)(2,1)S(1)} %copy-done), channel_id=1, source_target_pairs={{0,8},{1,9},{2,10},{3,11},{4,12},{5,13},{6,14},{7,15},{16,24},{17,... | collective-permute-start | bytes 663560 | tf_op jit(solution)/shard_map/ppermute | solution.py:22
  23.3 0.9 %collective-permute-done.2.refs_0_.refs_8_ = bf16[72,1536]{1,0:T(8,128)(2,1)S(1)} collective-permute-done((bf16[72,1536]{1,0:T(8,128)(2,1)S(1)}, bf16[72,1536]{1,0:T(8,128)(2,1)S(1)}, u32[]{:S(2)}, u32[]{:S(2)}) %collective-permute-start.2) | collective-permute-done | bytes 221216 | tf_op jit(solution)/shard_map/ppermute | solution.py:22
  24.3 1.9 %collective-permute-done.5.refs_3_.refs_13_ = bf16[72,1536]{1,0:T(8,128)(2,1)S(1)} collective-permute-done((bf16[72,1536]{1,0:T(8,128)(2,1)S(1)}, bf16[72,1536]{1,0:T(8,128)(2,1)S(1)}, u32[]{:S(2)}, u32[]{:S(2)}) %collective-permute-start.5) | collective-permute-done | bytes 221216 | tf_op jit(solution)/shard_map/ppermute | solution.py:22
  26.1 3.7 %collective-permute-done.4.refs_2_.refs_12_ = bf16[72,1536]{1,0:T(8,128)(2,1)S(1)} collective-permute-done((bf16[72,1536]{1,0:T(8,128)(2,1)S(1)}, bf16[72,1536]{1,0:T(8,128)(2,1)S(1)}, u32[]{:S(2)}, u32[]{:S(2)}) %collective-permute-start.4) | collective-permute-done | bytes 221216 | tf_op jit(solution)/shard_map/ppermute | solution.py:22
  29.9 2.5 %project.4 = (bf16[288,1536]{1,0:T(8,128)(2,1)S(1)}, bf16[288,768]{1,0:T(8,128)(2,1)S(1)}) custom-call(s32[1]{0:T(128)} %bitcast.where, bf16[72,1536]{1,0:T(8,128)(2,1)S(1)} %collective-permute-done.2.refs_0_.refs_8_, bf16[72,1536]{1,0:T(8,128)(2,1)S(1)} %collective-permute-done.3.refs_1_.refs_9_, ...), custom_call_target="tpu_custom_call" | custom-call | flops 2038431744 | bytes 2097152 | tf_op jit(solution)/shard_map/project/pallas_call | solution.py:209
  32.3 1.0 %collective-permute-start.9 = (bf16[288,1536]{1,0:T(8,128)(2,1)S(1)}, bf16[288,1536]{1,0:T(8,128)(2,1)S(1)}, u32[]{:S(2)}, u32[]{:S(2)}) collective-permute-start(bf16[288,1536]{1,0:T(8,128)(2,1)S(1)} %get-tuple-element.38.refs_1_), channel_id=1, source_target_pairs={{0,1},{1,0},{2,3},{3,2},{4,5},{5,4},{6,7},{7,6},{8,9},{9,8},{10,11... | collective-permute-start | bytes 2654216 | tf_op jit(solution)/shard_map/ppermute | solution.py:22
  33.3 2.8 %collective-permute-done.6.refs_0_.refs_10_ = bf16[72,1536]{1,0:T(8,128)(2,1)S(1)} collective-permute-done((bf16[72,1536]{1,0:T(8,128)(2,1)S(1)}, bf16[72,1536]{1,0:T(8,128)(2,1)S(1)}, u32[]{:S(2)}, u32[]{:S(2)}) %collective-permute-start.6) | collective-permute-done | bytes 221216 | tf_op jit(solution)/shard_map/ppermute | solution.py:22
  36.1 2.2 %collective-permute-start.7 = (bf16[72,1536]{1,0:T(8,128)(2,1)S(1)}, bf16[72,1536]{1,0:T(8,128)(2,1)S(1)}, u32[]{:S(2)}, u32[]{:S(2)}) collective-permute-start(bf16[72,1536]{1,0:T(8,128)(2,1)S(1)} %collective-permute-done.6.refs_0_.refs_10_), channel_id=1, source_target_pairs={{8,10},{9,11},{10,8},{11,9},{12,14},{13,15},{14,12},{15,13},{24,26... | collective-permute-start | bytes 663560 | tf_op jit(solution)/shard_map/ppermute | solution.py:22
  38.3 5.4 %collective-permute-done.7.refs_1_.refs_14_ = bf16[72,1536]{1,0:T(8,128)(2,1)S(1)} collective-permute-done((bf16[72,1536]{1,0:T(8,128)(2,1)S(1)}, bf16[72,1536]{1,0:T(8,128)(2,1)S(1)}, u32[]{:S(2)}, u32[]{:S(2)}) %collective-permute-start.7) | collective-permute-done | bytes 221216 | tf_op jit(solution)/shard_map/ppermute | solution.py:22
  43.8 1.3 %project.5 = (bf16[144,1536]{1,0:T(8,128)(2,1)S(1)}, bf16[144,768]{1,0:T(8,128)(2,1)S(1)}) custom-call(s32[1]{0:T(128)} %bitcast.where, bf16[72,1536]{1,0:T(8,128)(2,1)S(1)} %collective-permute-done.6.refs_0_.refs_10_, bf16[72,1536]{1,0:T(8,128)(2,1)S(1)} %collective-permute-done.7.refs_1_.refs_14_, ...), custom_call_target="tpu_custom_call" | custom-call | flops 1019215872 | bytes 2097152 | tf_op jit(solution)/shard_map/project/pallas_call | solution.py:209
  45.1 2.2 %collective-permute-start.10 = (bf16[144,1536]{1,0:T(8,128)(2,1)S(1)}, bf16[144,1536]{1,0:T(8,128)(2,1)S(1)}, u32[]{:S(2)}, u32[]{:S(2)}) collective-permute-start(bf16[144,1536]{1,0:T(8,128)(2,1)S(1)} %get-tuple-element.41.refs_2_), channel_id=1, source_target_pairs={{0,1},{1,0},{2,3},{3,2},{4,5},{5,4},{6,7},{7,6},{8,9},{9,8},{10,11... | collective-permute-start | bytes 1327112 | tf_op jit(solution)/shard_map/ppermute | solution.py:22
  47.3 6.4 %begin_first.1 = (bf16[576,768]{1,0:T(8,128)(2,1)S(1)}, f32[576,1536]{1,0:T(8,128)S(1)}, f32[6,432,1]{2,1,0:T(8,128)S(1)}, f32[6,432,1]{2,1,0:T(8,128)S(1)}, f32[432,768]{1,0:T(8,128)S(1)}) custom-call(s32[1]{0:T(128)} %bitcast.where, bf16[288,1536]{1,0:T(8,128)(2,1)S(1)} %get-tuple-element.37.refs_0_.fresh_mine_ref, ...), custom_call_target="tpu_custom_call" | custom-call | flops 764411904 | bytes 2097152 | tf_op jit(solution)/shard_map/begin_first/pallas_call | solution.py:281
  53.7 8.9 %finish_first.1 = (bf16[2,72,1536]{2,1,0:T(8,128)(2,1)}, bf16[2,72,1536]{2,1,0:T(8,128)(2,1)}, bf16[432,1536]{1,0:T(8,128)(2,1)S(1)}, bf16[72,1536]{1,0:T(8,128)(2,1)S(1)}, bf16[72,1536]{1,0:T(8,128)(2,1)S(1)}) custom-call(s32[1]{0:T(128)} %bitcast.where, f32[4]{0:T(128)S(1)} %fusion.1.steps, bf16[288,1536]{1,0:T(8,128)(2,1)S(1)} %get-tuple-element.37.refs_0_.fresh_mine_ref, ...), custom_call_target="tpu_custom_call" | custom-call | flops 4076863488 | bytes 4194304 | tf_op jit(solution)/shard_map/finish_first/pallas_call | solution.py:376
  62.7 0.1 collective-permute-start.11
  62.8 2.2 %begin_second.1 = (bf16[72,768]{1,0:T(8,128)(2,1)S(1)}, f32[6,72,1]{2,1,0:T(8,128)S(1)}, f32[6,72,1]{2,1,0:T(8,128)S(1)}, f32[72,768]{1,0:T(8,128)S(1)}) custom-call(s32[1]{0:T(128)} %bitcast.where, bf16[72,1536]{1,0:T(8,128)(2,1)S(1)} %get-tuple-element.51.own_ref, bf16[1536,768]{1,0:T(8,128)(2,1)S(1)} %get-tuple-element.36.refs_7_.refs_5_.wq_ref, ...), custom_call_target="tpu_custom_call" | custom-call | flops 339738624 | bytes 2097152 | tf_op jit(solution)/shard_map/begin_second/pallas_call | solution.py:428
  64.9 0.9 %collective-permute-done.11.theirs_ref = bf16[432,1536]{1,0:T(8,128)(2,1)S(1)} collective-permute-done((bf16[432,1536]{1,0:T(8,128)(2,1)S(1)}, bf16[432,1536]{1,0:T(8,128)(2,1)S(1)}, u32[]{:S(2)}, u32[]{:S(2)}) %collective-permute-start.11) | collective-permute-done | bytes 1327136 | tf_op jit(solution)/shard_map/ppermute | solution.py:22
  65.8 4.6 %finish_second.1 = (bf16[2,72,1536]{2,1,0:T(8,128)(2,1)}, bf16[2,72,1536]{2,1,0:T(8,128)(2,1)}) custom-call(s32[1]{0:T(128)} %bitcast.where, f32[4]{0:T(128)S(1)} %fusion.1.steps, bf16[72,768]{1,0:T(8,128)(2,1)S(1)} %get-tuple-element.53.q_ref, f32[6,72,1]{2,1,0:T(8,128)S(1)} %get-tuple-element.54.top_ref, ...), custom_call_target="tpu_custom_call", output_to_operand_aliasing={{0}: (10, {}), {1}: (11, {})} | custom-call | flops 339738624 | bytes 4194304 | tf_op jit(solution)/shard_map/finish_second/pallas_call | solution.py:482
  (9 shorter events, 0.0 us)
Async XLA Ops:
  0.6 16.7 %collective-permute-start.3 = (bf16[72,1536]{1,0:T(8,128)(2,1)}, bf16[72,1536]{1,0:T(8,128)(2,1)S(1)}, u32[]{:S(2)}, u32[]{:S(2)}) collective-permute-start(bf16[72,1536]{1,0:T(8,128)(2,1)} %refs_7_.1), channel_id=1, source_target_pairs={{0,12},{1,13},{2,14},{3,15},{4,8},{5,9},{6,10},{7,11},{8,4},{9,5},... | collective-permute-start | bytes 663560 | tf_op jit(solution)/shard_map/ppermute | solution.py:22
  1.9 11.3 %collective-permute-start = (bf16[72,1536]{1,0:T(8,128)(2,1)}, bf16[72,1536]{1,0:T(8,128)(2,1)S(1)}, u32[]{:S(2)}, u32[]{:S(2)}) collective-permute-start(bf16[72,1536]{1,0:T(8,128)(2,1)} %refs_7_.1), channel_id=1, source_target_pairs={{0,2},{1,3},{2,0},{3,1},{4,6},{5,7},{6,4},{7,5},{8,10},{9,11},{10,... | collective-permute-start | bytes 663560 | tf_op jit(solution)/shard_map/ppermute | solution.py:22
  3.2 10.0 %collective-permute-start.1 = (bf16[72,1536]{1,0:T(8,128)(2,1)}, bf16[72,1536]{1,0:T(8,128)(2,1)S(1)}, u32[]{:S(2)}, u32[]{:S(2)}) collective-permute-start(bf16[72,1536]{1,0:T(8,128)(2,1)} %fresh_ref.1), channel_id=1, source_target_pairs={{12,14},{13,15},{14,12},{15,13},{28,30},{29,31},{30,28},{31,29}} | collective-permute-start | bytes 663560 | tf_op jit(solution)/shard_map/ppermute | solution.py:22
  7.0 6.3 %copy-start = (bf16[72,1536]{1,0:T(8,128)(2,1)S(1)}, bf16[72,1536]{1,0:T(8,128)(2,1)}, u32[]{:S(2)}) copy-start(bf16[72,1536]{1,0:T(8,128)(2,1)} %refs_7_.1) | copy-start | bytes 663556
  7.0 6.3 %copy-start.1 = (bf16[72,1536]{1,0:T(8,128)(2,1)S(1)}, bf16[72,1536]{1,0:T(8,128)(2,1)}, u32[]{:S(2)}) copy-start(bf16[72,1536]{1,0:T(8,128)(2,1)} %fresh_ref.1) | copy-start | bytes 663556
  15.8 28.0 %collective-permute-start.8 = (bf16[288,1536]{1,0:T(8,128)(2,1)S(1)}, bf16[288,1536]{1,0:T(8,128)(2,1)S(1)}, u32[]{:S(2)}, u32[]{:S(2)}) collective-permute-start(bf16[288,1536]{1,0:T(8,128)(2,1)S(1)} %get-tuple-element.37.refs_0_.fresh_mine_ref), channel_id=1, source_target_pairs={{0,1},{1,0},{2,3},{3,2},{4,5},{5,4},{6,7},{7,6},{8,9},{9,8},{10,11... | collective-permute-start | bytes 2654216 | tf_op jit(solution)/shard_map/ppermute | solution.py:22
  17.3 6.9 %collective-permute-start.2 = (bf16[72,1536]{1,0:T(8,128)(2,1)S(1)}, bf16[72,1536]{1,0:T(8,128)(2,1)S(1)}, u32[]{:S(2)}, u32[]{:S(2)}) collective-permute-start(bf16[72,1536]{1,0:T(8,128)(2,1)S(1)} %copy-done), channel_id=1, source_target_pairs={{0,4},{1,5},{2,6},{3,7},{4,0},{5,1},{6,2},{7,3},{8,12},{9,13},{10,... | collective-permute-start | bytes 663560 | tf_op jit(solution)/shard_map/ppermute | solution.py:22
  17.4 8.8 %collective-permute-start.5 = (bf16[72,1536]{1,0:T(8,128)(2,1)S(1)}, bf16[72,1536]{1,0:T(8,128)(2,1)S(1)}, u32[]{:S(2)}, u32[]{:S(2)}) collective-permute-start(bf16[72,1536]{1,0:T(8,128)(2,1)S(1)} %collective-permute-done.3.refs_1_.refs_9_), channel_id=1, source_target_pairs={{4,6},{5,7},{6,4},{7,5},{8,10},{9,11},{10,8},{11,9},{12,14},{13,15... | collective-permute-start | bytes 663560 | tf_op jit(solution)/shard_map/ppermute | solution.py:22
  20.5 9.4 %collective-permute-start.4 = (bf16[72,1536]{1,0:T(8,128)(2,1)S(1)}, bf16[72,1536]{1,0:T(8,128)(2,1)S(1)}, u32[]{:S(2)}, u32[]{:S(2)}) collective-permute-start(bf16[72,1536]{1,0:T(8,128)(2,1)S(1)} %collective-permute-done.refs_2_.refs_11_), channel_id=1, source_target_pairs={{0,4},{1,5},{2,6},{3,7},{4,0},{5,1},{6,2},{7,3},{8,12},{9,13},{10,... | collective-permute-start | bytes 663560 | tf_op jit(solution)/shard_map/ppermute | solution.py:22
  22.0 14.1 %collective-permute-start.6 = (bf16[72,1536]{1,0:T(8,128)(2,1)S(1)}, bf16[72,1536]{1,0:T(8,128)(2,1)S(1)}, u32[]{:S(2)}, u32[]{:S(2)}) collective-permute-start(bf16[72,1536]{1,0:T(8,128)(2,1)S(1)} %copy-done), channel_id=1, source_target_pairs={{0,8},{1,9},{2,10},{3,11},{4,12},{5,13},{6,14},{7,15},{16,24},{17,... | collective-permute-start | bytes 663560 | tf_op jit(solution)/shard_map/ppermute | solution.py:22
  32.3 15.0 %collective-permute-start.9 = (bf16[288,1536]{1,0:T(8,128)(2,1)S(1)}, bf16[288,1536]{1,0:T(8,128)(2,1)S(1)}, u32[]{:S(2)}, u32[]{:S(2)}) collective-permute-start(bf16[288,1536]{1,0:T(8,128)(2,1)S(1)} %get-tuple-element.38.refs_1_), channel_id=1, source_target_pairs={{0,1},{1,0},{2,3},{3,2},{4,5},{5,4},{6,7},{7,6},{8,9},{9,8},{10,11... | collective-permute-start | bytes 2654216 | tf_op jit(solution)/shard_map/ppermute | solution.py:22
  36.1 7.6 %collective-permute-start.7 = (bf16[72,1536]{1,0:T(8,128)(2,1)S(1)}, bf16[72,1536]{1,0:T(8,128)(2,1)S(1)}, u32[]{:S(2)}, u32[]{:S(2)}) collective-permute-start(bf16[72,1536]{1,0:T(8,128)(2,1)S(1)} %collective-permute-done.6.refs_0_.refs_10_), channel_id=1, source_target_pairs={{8,10},{9,11},{10,8},{11,9},{12,14},{13,15},{14,12},{15,13},{24,26... | collective-permute-start | bytes 663560 | tf_op jit(solution)/shard_map/ppermute | solution.py:22
  45.1 8.6 %collective-permute-start.10 = (bf16[144,1536]{1,0:T(8,128)(2,1)S(1)}, bf16[144,1536]{1,0:T(8,128)(2,1)S(1)}, u32[]{:S(2)}, u32[]{:S(2)}) collective-permute-start(bf16[144,1536]{1,0:T(8,128)(2,1)S(1)} %get-tuple-element.41.refs_2_), channel_id=1, source_target_pairs={{0,1},{1,0},{2,3},{3,2},{4,5},{5,4},{6,7},{7,6},{8,9},{9,8},{10,11... | collective-permute-start | bytes 1327112 | tf_op jit(solution)/shard_map/ppermute | solution.py:22
  62.7 3.1 %collective-permute-start.11 = (bf16[432,1536]{1,0:T(8,128)(2,1)S(1)}, bf16[432,1536]{1,0:T(8,128)(2,1)S(1)}, u32[]{:S(2)}, u32[]{:S(2)}) collective-permute-start(bf16[432,1536]{1,0:T(8,128)(2,1)S(1)} %get-tuple-element.52.mine_ref), channel_id=1, source_target_pairs={{0,1},{1,0},{2,3},{3,2},{4,5},{5,4},{6,7},{7,6},{8,9},{9,8},{10,11... | collective-permute-start | bytes 3981320 | tf_op jit(solution)/shard_map/ppermute | solution.py:22

commit v2 on v1

--- a/solution.py
+++ b/solution.py
@@ -116,23 +116,41 @@
 SHARPNESS = math.log2(math.e) / math.sqrt(HEAD_DIM)
 
 
-def attend(queries, pairs, state=None):
-    scores = [
-        lax.dot_general(queries, keys, (((1,), (1,)), ((), ())), preferred_element_type=jnp.float32)
+def score(queries, pairs):
+    return [
+        lax.dot_general(queries(), keys(), (((1,), (1,)), ((), ())), preferred_element_type=jnp.float32)
         for keys, _ in pairs
     ]
+
+
+def weigh(scores, pairs, state=None):
     top = functools.reduce(jnp.maximum, [jnp.max(s, axis=-1, keepdims=True) for s in scores])
     total, summed = 0.0, 0.0
     if state is not None:
-        old_top, old_total, old_summed = state
+        old_top, old_total, old_summed = state()
         top = jnp.maximum(top, old_top)
         fade = jnp.exp2((old_top - top) * SHARPNESS)
         total, summed = old_total * fade, old_summed * fade
-    for score, (_, values) in zip(scores, pairs):
-        weights = jnp.exp2((score - top) * SHARPNESS)
+    for part, (_, values) in zip(scores, pairs):
+        weights = jnp.exp2((part - top) * SHARPNESS)
         total = total + jnp.sum(weights, axis=-1, keepdims=True)
-        summed = summed + dot(weights.astype(jnp.bfloat16), values)
+        summed = summed + dot(weights.astype(jnp.bfloat16), values())
     return top, total, summed
+
+
+AHEAD = 3
+
+
+def attend_all(jobs):
+    pending = [score(*job[:2]) for job in jobs[:AHEAD]]
+    for i, (_, pairs, state, emit) in enumerate(jobs):
+        if i + AHEAD < len(jobs):
+            pending.append(score(*jobs[i + AHEAD][:2]))
+        emit(*weigh(pending.pop(0), pairs, state))
+
+
+def view(ref, *where):
+    return lambda: ref[where]
 
 
 def head_columns(width):
@@ -261,16 +279,19 @@
                 base = pl.multiple_of(place * span, span)
                 kv_ref[pl.ds(base, half), :] = kv_mine[g][rows, :]
                 kv_ref[pl.ds(base + half, half), :] = kv_theirs[g][rows, :]
+    jobs = []
     for s in range(1, SECTIONS):
-        rows = slice((s - 1) * half, s * half)
+        rows, seen = slice((s - 1) * half, s * half), slice(0, s * span)
         for head, (cols, v_cols) in enumerate(head_columns(width)):
-            top, total, summed = attend(
-                q_ref[s * half : (s + 1) * half, cols],
-                [(kv_ref[0 : s * span, cols], kv_ref[0 : s * span, v_cols])],
-            )
-            top_ref[head, rows, :] = top
-            total_ref[head, rows, :] = total
-            sum_ref[rows, cols] = summed
+
+            def emit(top, total, summed, head=head, rows=rows, cols=cols):
+                top_ref[head, rows, :] = top
+                total_ref[head, rows, :] = total
+                sum_ref[rows, cols] = summed
+
+            queries = view(q_ref, slice(s * half, (s + 1) * half), cols)
+            jobs.append((queries, [(view(kv_ref, seen, cols), view(kv_ref, seen, v_cols))], None, emit))
+    attend_all(jobs)
 
 
 def begin_first(where, groups, kv_mine, kv_theirs, q, own, across):
@@ -320,13 +341,21 @@
         pl.when(section == s)(functools.partial(set_late, s))
     pl.when(section == LAST)(functools.partial(set_late, LAST ^ 1))
 
-    for head, (cols, v_cols) in enumerate(head_columns(width)):
-        _, total, summed = attend(
-            q_ref[half:, cols],
-            [(late_ref[:, cols], late_ref[:, v_cols])],
-            (top_ref[head], total_ref[head], sum_ref[:, cols]),
-        )
-        o_ref[:, cols] = (summed / total).astype(jnp.bfloat16)
+    everything = slice(None)
+
+    def late_jobs(queries, into, with_state):
+        for head, (cols, v_cols) in enumerate(head_columns(width)):
+
+            def emit(_, total, summed, cols=cols):
+                o_ref[into, cols] = (summed / total).astype(jnp.bfloat16)
+
+            def state(head=head, cols=cols):
+                return top_ref[head, into], total_ref[head, into], sum_ref[into, cols]
+
+            pairs = [(view(late_ref, everything, cols), view(late_ref, everything, v_cols))]
+            yield view(q_ref, queries, cols), pairs, state if with_state else None, emit
+
+    attend_all(list(late_jobs(slice(half, SECTIONS * half), slice(0, LAST * half), True)))
     v_ref[...] = dot(o_ref[...], wo_ref[...])
     for s in range(1, SECTIONS):
         rows = slice((s - 1) * half, s * half)
@@ -338,9 +367,7 @@
 
     @pl.when(section == 0)
     def _():
-        for cols, v_cols in head_columns(width):
-            _, total, summed = attend(q_ref[0:local, cols], [(late_ref[:, cols], late_ref[:, v_cols])])
-            o_ref[0:local, cols] = (summed / total).astype(jnp.bfloat16)
+        attend_all(list(late_jobs(slice(0, local), slice(0, local), False)))
         moving = dot(o_ref[0:local, :], wo_ref[...])
         out_ref[0] = (x_ref[0:local, :] + steps[0] * moving).astype(jnp.bfloat16)
         out_ref[1] = moving.astype(jnp.bfloat16)
@@ -404,10 +431,15 @@
     section = where[0]
 
     def run(seen):
+        jobs = []
         for head, (cols, v_cols) in enumerate(head_columns(width)):
-            top_ref[head], total_ref[head], sum_ref[:, cols] = attend(
-                q_ref[:, cols], [(r[rows, cols], r[rows, v_cols]) for r, rows in seen]
-            )
+
+            def emit(top, total, summed, head=head, cols=cols):
+                top_ref[head], total_ref[head], sum_ref[:, cols] = top, total, summed
+
+            pairs = [(view(r, rows, cols), view(r, rows, v_cols)) for r, rows in seen]
+            jobs.append((view(q_ref, slice(None), cols), pairs, None, emit))
+        attend_all(jobs)
 
     for s in range(LAST):
 
@@ -446,13 +478,18 @@
     section = where[0]
 
     def run(seen):
+        jobs = []
         for head, (cols, v_cols) in enumerate(head_columns(width)):
-            _, total, summed = attend(
-                q_ref[:, cols],
-                [(theirs_ref[0:seen, cols], theirs_ref[0:seen, v_cols])],
-                (top_ref[head], total_ref[head], sum_ref[:, cols]),
-            )
-            o_ref[:, cols] = (summed / total).astype(jnp.bfloat16)
+
+            def emit(_, total, summed, cols=cols):
+                o_ref[:, cols] = (summed / total).astype(jnp.bfloat16)
+
+            def state(head=head, cols=cols):
+                return top_ref[head], total_ref[head], sum_ref[:, cols]
+
+            pairs = [(view(theirs_ref, slice(0, seen), cols), view(theirs_ref, slice(0, seen), v_cols))]
+            jobs.append((view(q_ref, slice(None), cols), pairs, state, emit))
+        attend_all(jobs)
 
     for s in range(LAST):
         reached = (section >= s) if s == LAST - 1 else (section == s)

time: 70.8 us -> 65.4 us (0.924)
  Pallas kernels: 32.7 us -> 26.3 us
  waiting for transfers between devices: 17.6 us -> 18.6 us
    pallas_call x1, Pallas kernels: 6.42 us -> 3.14 us  [begin_first(): pl.pallas_call(functools.partial(begin_kernel, groups=groups), out_shape=...]
    pallas_call x1, Pallas kernels: 4.6 us -> 3.07 us  [finish_second(): pl.pallas_call(finish_second_kernel, out_shape=(pair, pair), in_specs=[SM...]
    pallas_call x1, Pallas kernels: 2.16 us -> 1.13 us  [begin_second(): pl.pallas_call(functools.partial(begin_second_kernel, fresh_row=fresh_row...]
    ppermute x12, waiting for transfers between devices: 17.6 us -> 18.6 us  [permuted(): return lax.ppermute(block, axis, route)]
  transfers between devices with their start and end apart: 12 -> 12, of which waited for: 7 -> 7; matrix products, arithmetic and copies ran while one was open for 2% -> 2% of each run, Pallas kernels for 27% -> 23%
where the time goes in v2:
time: 65.4 us; the launch traced here: 65.2 us
  Pallas kernels  26.3 us (40%)
  waiting for transfers between devices  18.6 us (28%)
  starting transfers between devices  17.7 us (27%)
  other arithmetic  1.6 us (2%)
  between operations  0.92 us (1%)
    ppermute x12, waiting for transfers between devices, permuted(): return lax.ppermute(block, axis, route)  18.6 us
    ppermute x12, starting transfers between devices, permuted(): return lax.ppermute(block, axis, route)  17.7 us
    pallas_call x1, Pallas kernels, finish_first(): pl.pallas_call(functools.partial(finish_kernel, groups=groups), out_shape...  8.38 us
    pallas_call x3, Pallas kernels, project(): pl.pallas_call(functools.partial(project_kernel, slots=slots), out_shape=...  6.29 us
    pallas_call x1, Pallas kernels, fetch(): pl.pallas_call(functools.partial(fetch_kernel, count=len(arrays)), out_sh...  4.3 us
    pallas_call x1, Pallas kernels, begin_first(): pl.pallas_call(functools.partial(begin_kernel, groups=groups), out_shape=...  3.14 us
    pallas_call x1, Pallas kernels, finish_second(): pl.pallas_call(finish_second_kernel, out_shape=(pair, pair), in_specs=[SM...  3.07 us
  transfers between devices with their start and end apart: 12, of which 7 were waited for; matrix products, arithmetic and copies ran while one was open for 2% of the time, Pallas kernels for 23%

profile of v2, /device:TPU:27, one launch (start us, length us, event | category | flops | bytes accessed | tf_op | source)
XLA Modules:
  0.0 65.2 jit_solution(14378540491702156187)
XLA Ops:
  0.6 1.3 %collective-permute-start.3 = (bf16[72,1536]{1,0:T(8,128)(2,1)}, bf16[72,1536]{1,0:T(8,128)(2,1)S(1)}, u32[]{:S(2)}, u32[]{:S(2)}) collective-permute-start(bf16[72,1536]{1,0:T(8,128)(2,1)} %refs_7_.1), channel_id=1, source_target_pairs={{0,12},{1,13},{2,14},{3,15},{4,8},{5,9},{6,10},{7,11},{8,4},{9,5},... | collective-permute-start | bytes 663560 | tf_op jit(solution)/shard_map/ppermute | solution.py:22
  1.9 1.3 %collective-permute-start = (bf16[72,1536]{1,0:T(8,128)(2,1)}, bf16[72,1536]{1,0:T(8,128)(2,1)S(1)}, u32[]{:S(2)}, u32[]{:S(2)}) collective-permute-start(bf16[72,1536]{1,0:T(8,128)(2,1)} %refs_7_.1), channel_id=1, source_target_pairs={{0,2},{1,3},{2,0},{3,1},{4,6},{5,7},{6,4},{7,5},{8,10},{9,11},{10,... | collective-permute-start | bytes 663560 | tf_op jit(solution)/shard_map/ppermute | solution.py:22
  3.2 2.1 %collective-permute-start.1 = (bf16[72,1536]{1,0:T(8,128)(2,1)}, bf16[72,1536]{1,0:T(8,128)(2,1)S(1)}, u32[]{:S(2)}, u32[]{:S(2)}) collective-permute-start(bf16[72,1536]{1,0:T(8,128)(2,1)} %fresh_ref.1), channel_id=1, source_target_pairs={{12,14},{13,15},{14,12},{15,13},{28,30},{29,31},{30,28},{31,29}} | collective-permute-start | bytes 663560 | tf_op jit(solution)/shard_map/ppermute | solution.py:22
  5.4 0.7 %convert_element_type.6 = f32[4]{0:T(128)S(1)} convert(s32[4]{0:T(128)} %param.10) | non-fusion elementwise | flops 4 | bytes 32 | tf_op jit(solution)/shard_map/convert_element_type | solution.py:27
  6.1 0.1 multiply_cosine_fusion
  6.2 0.8 %fusion.1.steps = f32[4]{0:T(128)S(1)} fusion(s32[4]{0:T(128)} %param.10, s32[3]{0:T(128)} %bitcast.2, s32[1]{0:T(128)} %constant.28.clone.1), kind=kLoop, calls=%fused_computation.5 | loop fusion | flops 16 | bytes 48 | tf_op jit(solution)/shard_map/div | solution.py:41
  7.0 4.3 %fetch.1 = (bf16[1536,768]{1,0:T(8,128)(2,1)S(1)}, bf16[1536,768]{1,0:T(8,128)(2,1)S(1)}, bf16[1536,768]{1,0:T(8,128)(2,1)S(1)}, bf16[768,1536]{1,0:T(8,128)(2,1)S(1)}, f32[4,3072]{1,0:T(4,128)S(1)}) custom-call(bf16[1536,768]{1,0:T(8,128)(2,1)} %refs_0_.2, bf16[1536,768]{1,0:T(8,128)(2,1)} %refs_1_.2, bf16[1536,768]{1,0:T(8,128)(2,1)} %refs_2_.1, ...), custom_call_target="tpu_custom_call" | custom-call | bytes 9437184 | tf_op jit(solution)/shard_map/fetch/pallas_call | solution.py:187
  11.3 2.0 %collective-permute-done.1.refs_3_ = bf16[72,1536]{1,0:T(8,128)(2,1)S(1)} collective-permute-done((bf16[72,1536]{1,0:T(8,128)(2,1)}, bf16[72,1536]{1,0:T(8,128)(2,1)S(1)}, u32[]{:S(2)}, u32[]{:S(2)}) %collective-permute-start.1) | collective-permute-done | bytes 221216 | tf_op jit(solution)/shard_map/ppermute | solution.py:22
  13.3 0.0 collective-permute-done.refs_2_.refs_11_
  13.3 2.5 %project.3 = (bf16[288,1536]{1,0:T(8,128)(2,1)S(1)}, bf16[288,768]{1,0:T(8,128)(2,1)S(1)}) custom-call(s32[1]{0:T(128)} %bitcast.where, bf16[72,1536]{1,0:T(8,128)(2,1)S(1)} %copy-done, bf16[72,1536]{1,0:T(8,128)(2,1)S(1)} %copy-done.1, bf16[72,1536]{1,0:T(8,128)(2,1)S(1)} %collective-permute-done.refs_2_.refs_11_, ...), custom_call_target="tpu_custom_call" | custom-call | flops 2038431744 | bytes 2097152 | tf_op jit(solution)/shard_map/project/pallas_call | solution.py:227
  15.8 1.6 %collective-permute-start.8 = (bf16[288,1536]{1,0:T(8,128)(2,1)S(1)}, bf16[288,1536]{1,0:T(8,128)(2,1)S(1)}, u32[]{:S(2)}, u32[]{:S(2)}) collective-permute-start(bf16[288,1536]{1,0:T(8,128)(2,1)S(1)} %get-tuple-element.37.refs_0_.fresh_mine_ref), channel_id=1, source_target_pairs={{0,1},{1,0},{2,3},{3,2},{4,5},{5,4},{6,7},{7,6},{8,9},{9,8},{10,11... | collective-permute-start | bytes 2654216 | tf_op jit(solution)/shard_map/ppermute | solution.py:22
  17.3 0.0 collective-permute-start.2
  17.3 0.0 collective-permute-done.3.refs_1_.refs_9_
  17.4 3.1 %collective-permute-start.5 = (bf16[72,1536]{1,0:T(8,128)(2,1)S(1)}, bf16[72,1536]{1,0:T(8,128)(2,1)S(1)}, u32[]{:S(2)}, u32[]{:S(2)}) collective-permute-start(bf16[72,1536]{1,0:T(8,128)(2,1)S(1)} %collective-permute-done.3.refs_1_.refs_9_), channel_id=1, source_target_pairs={{4,6},{5,7},{6,4},{7,5},{8,10},{9,11},{10,8},{11,9},{12,14},{13,15... | collective-permute-start | bytes 663560 | tf_op jit(solution)/shard_map/ppermute | solution.py:22
  20.5 1.5 %collective-permute-start.4 = (bf16[72,1536]{1,0:T(8,128)(2,1)S(1)}, bf16[72,1536]{1,0:T(8,128)(2,1)S(1)}, u32[]{:S(2)}, u32[]{:S(2)}) collective-permute-start(bf16[72,1536]{1,0:T(8,128)(2,1)S(1)} %collective-permute-done.refs_2_.refs_11_), channel_id=1, source_target_pairs={{0,4},{1,5},{2,6},{3,7},{4,0},{5,1},{6,2},{7,3},{8,12},{9,13},{10,... | collective-permute-start | bytes 663560 | tf_op jit(solution)/shard_map/ppermute | solution.py:22
  22.0 1.3 %collective-permute-start.6 = (bf16[72,1536]{1,0:T(8,128)(2,1)S(1)}, bf16[72,1536]{1,0:T(8,128)(2,1)S(1)}, u32[]{:S(2)}, u32[]{:S(2)}) collective-permute-start(bf16[72,1536]{1,0:T(8,128)(2,1)S(1)} %copy-done), channel_id=1, source_target_pairs={{0,8},{1,9},{2,10},{3,11},{4,12},{5,13},{6,14},{7,15},{16,24},{17,... | collective-permute-start | bytes 663560 | tf_op jit(solution)/shard_map/ppermute | solution.py:22
  23.3 0.9 %collective-permute-done.2.refs_0_.refs_8_ = bf16[72,1536]{1,0:T(8,128)(2,1)S(1)} collective-permute-done((bf16[72,1536]{1,0:T(8,128)(2,1)S(1)}, bf16[72,1536]{1,0:T(8,128)(2,1)S(1)}, u32[]{:S(2)}, u32[]{:S(2)}) %collective-permute-start.2) | collective-permute-done | bytes 221216 | tf_op jit(solution)/shard_map/ppermute | solution.py:22
  24.3 1.9 %collective-permute-done.5.refs_3_.refs_13_ = bf16[72,1536]{1,0:T(8,128)(2,1)S(1)} collective-permute-done((bf16[72,1536]{1,0:T(8,128)(2,1)S(1)}, bf16[72,1536]{1,0:T(8,128)(2,1)S(1)}, u32[]{:S(2)}, u32[]{:S(2)}) %collective-permute-start.5) | collective-permute-done | bytes 221216 | tf_op jit(solution)/shard_map/ppermute | solution.py:22
  26.1 3.7 %collective-permute-done.4.refs_2_.refs_12_ = bf16[72,1536]{1,0:T(8,128)(2,1)S(1)} collective-permute-done((bf16[72,1536]{1,0:T(8,128)(2,1)S(1)}, bf16[72,1536]{1,0:T(8,128)(2,1)S(1)}, u32[]{:S(2)}, u32[]{:S(2)}) %collective-permute-start.4) | collective-permute-done | bytes 221216 | tf_op jit(solution)/shard_map/ppermute | solution.py:22
  29.9 2.5 %project.4 = (bf16[288,1536]{1,0:T(8,128)(2,1)S(1)}, bf16[288,768]{1,0:T(8,128)(2,1)S(1)}) custom-call(s32[1]{0:T(128)} %bitcast.where, bf16[72,1536]{1,0:T(8,128)(2,1)S(1)} %collective-permute-done.2.refs_0_.refs_8_, bf16[72,1536]{1,0:T(8,128)(2,1)S(1)} %collective-permute-done.3.refs_1_.refs_9_, ...), custom_call_target="tpu_custom_call" | custom-call | flops 2038431744 | bytes 2097152 | tf_op jit(solution)/shard_map/project/pallas_call | solution.py:227
  32.3 1.0 %collective-permute-start.9 = (bf16[288,1536]{1,0:T(8,128)(2,1)S(1)}, bf16[288,1536]{1,0:T(8,128)(2,1)S(1)}, u32[]{:S(2)}, u32[]{:S(2)}) collective-permute-start(bf16[288,1536]{1,0:T(8,128)(2,1)S(1)} %get-tuple-element.38.refs_1_), channel_id=1, source_target_pairs={{0,1},{1,0},{2,3},{3,2},{4,5},{5,4},{6,7},{7,6},{8,9},{9,8},{10,11... | collective-permute-start | bytes 2654216 | tf_op jit(solution)/shard_map/ppermute | solution.py:22
  33.3 2.8 %collective-permute-done.6.refs_0_.refs_10_ = bf16[72,1536]{1,0:T(8,128)(2,1)S(1)} collective-permute-done((bf16[72,1536]{1,0:T(8,128)(2,1)S(1)}, bf16[72,1536]{1,0:T(8,128)(2,1)S(1)}, u32[]{:S(2)}, u32[]{:S(2)}) %collective-permute-start.6) | collective-permute-done | bytes 221216 | tf_op jit(solution)/shard_map/ppermute | solution.py:22
  36.1 2.2 %collective-permute-start.7 = (bf16[72,1536]{1,0:T(8,128)(2,1)S(1)}, bf16[72,1536]{1,0:T(8,128)(2,1)S(1)}, u32[]{:S(2)}, u32[]{:S(2)}) collective-permute-start(bf16[72,1536]{1,0:T(8,128)(2,1)S(1)} %collective-permute-done.6.refs_0_.refs_10_), channel_id=1, source_target_pairs={{8,10},{9,11},{10,8},{11,9},{12,14},{13,15},{14,12},{15,13},{24,26... | collective-permute-start | bytes 663560 | tf_op jit(solution)/shard_map/ppermute | solution.py:22
  38.3 5.4 %collective-permute-done.7.refs_1_.refs_14_ = bf16[72,1536]{1,0:T(8,128)(2,1)S(1)} collective-permute-done((bf16[72,1536]{1,0:T(8,128)(2,1)S(1)}, bf16[72,1536]{1,0:T(8,128)(2,1)S(1)}, u32[]{:S(2)}, u32[]{:S(2)}) %collective-permute-start.7) | collective-permute-done | bytes 221216 | tf_op jit(solution)/shard_map/ppermute | solution.py:22
  43.8 1.3 %project.5 = (bf16[144,1536]{1,0:T(8,128)(2,1)S(1)}, bf16[144,768]{1,0:T(8,128)(2,1)S(1)}) custom-call(s32[1]{0:T(128)} %bitcast.where, bf16[72,1536]{1,0:T(8,128)(2,1)S(1)} %collective-permute-done.6.refs_0_.refs_10_, bf16[72,1536]{1,0:T(8,128)(2,1)S(1)} %collective-permute-done.7.refs_1_.refs_14_, ...), custom_call_target="tpu_custom_call" | custom-call | flops 1019215872 | bytes 2097152 | tf_op jit(solution)/shard_map/project/pallas_call | solution.py:227
  45.1 2.2 %collective-permute-start.10 = (bf16[144,1536]{1,0:T(8,128)(2,1)S(1)}, bf16[144,1536]{1,0:T(8,128)(2,1)S(1)}, u32[]{:S(2)}, u32[]{:S(2)}) collective-permute-start(bf16[144,1536]{1,0:T(8,128)(2,1)S(1)} %get-tuple-element.41.refs_2_), channel_id=1, source_target_pairs={{0,1},{1,0},{2,3},{3,2},{4,5},{5,4},{6,7},{7,6},{8,9},{9,8},{10,11... | collective-permute-start | bytes 1327112 | tf_op jit(solution)/shard_map/ppermute | solution.py:22
  47.3 3.1 %begin_first.1 = (bf16[576,768]{1,0:T(8,128)(2,1)S(1)}, f32[576,1536]{1,0:T(8,128)S(1)}, f32[6,432,1]{2,1,0:T(8,128)S(1)}, f32[6,432,1]{2,1,0:T(8,128)S(1)}, f32[432,768]{1,0:T(8,128)S(1)}) custom-call(s32[1]{0:T(128)} %bitcast.where, bf16[288,1536]{1,0:T(8,128)(2,1)S(1)} %get-tuple-element.37.refs_0_.fresh_mine_ref, ...), custom_call_target="tpu_custom_call" | custom-call | flops 764411904 | bytes 2097152 | tf_op jit(solution)/shard_map/begin_first/pallas_call | solution.py:302
  50.4 8.4 %finish_first.1 = (bf16[2,72,1536]{2,1,0:T(8,128)(2,1)}, bf16[2,72,1536]{2,1,0:T(8,128)(2,1)}, bf16[432,1536]{1,0:T(8,128)(2,1)S(1)}, bf16[72,1536]{1,0:T(8,128)(2,1)S(1)}, bf16[72,1536]{1,0:T(8,128)(2,1)S(1)}) custom-call(s32[1]{0:T(128)} %bitcast.where, f32[4]{0:T(128)S(1)} %fusion.1.steps, bf16[288,1536]{1,0:T(8,128)(2,1)S(1)} %get-tuple-element.37.refs_0_.fresh_mine_ref, ...), custom_call_target="tpu_custom_call" | custom-call | flops 4076863488 | bytes 4194304 | tf_op jit(solution)/shard_map/finish_first/pallas_call | solution.py:403
  58.8 0.1 collective-permute-start.11
  58.9 1.1 %begin_second.1 = (bf16[72,768]{1,0:T(8,128)(2,1)S(1)}, f32[6,72,1]{2,1,0:T(8,128)S(1)}, f32[6,72,1]{2,1,0:T(8,128)S(1)}, f32[72,768]{1,0:T(8,128)S(1)}) custom-call(s32[1]{0:T(128)} %bitcast.where, bf16[72,1536]{1,0:T(8,128)(2,1)S(1)} %get-tuple-element.51.own_ref, bf16[1536,768]{1,0:T(8,128)(2,1)S(1)} %get-tuple-element.36.refs_7_.refs_5_.wq_ref, ...), custom_call_target="tpu_custom_call" | custom-call | flops 339738624 | bytes 2097152 | tf_op jit(solution)/shard_map/begin_second/pallas_call | solution.py:460
  60.1 1.9 %collective-permute-done.11.theirs_ref = bf16[432,1536]{1,0:T(8,128)(2,1)S(1)} collective-permute-done((bf16[432,1536]{1,0:T(8,128)(2,1)S(1)}, bf16[432,1536]{1,0:T(8,128)(2,1)S(1)}, u32[]{:S(2)}, u32[]{:S(2)}) %collective-permute-start.11) | collective-permute-done | bytes 1327136 | tf_op jit(solution)/shard_map/ppermute | solution.py:22
  62.0 3.1 %finish_second.1 = (bf16[2,72,1536]{2,1,0:T(8,128)(2,1)}, bf16[2,72,1536]{2,1,0:T(8,128)(2,1)}) custom-call(s32[1]{0:T(128)} %bitcast.where, f32[4]{0:T(128)S(1)} %fusion.1.steps, bf16[72,768]{1,0:T(8,128)(2,1)S(1)} %get-tuple-element.53.q_ref, f32[6,72,1]{2,1,0:T(8,128)S(1)} %get-tuple-element.54.top_ref, ...), custom_call_target="tpu_custom_call", output_to_operand_aliasing={{0}: (10, {}), {1}: (11, {})} | custom-call | flops 339738624 | bytes 4194304 | tf_op jit(solution)/shard_map/finish_second/pallas_call | solution.py:519
  (9 shorter events, 0.0 us)
Async XLA Ops:
  0.6 16.7 %collective-permute-start.3 = (bf16[72,1536]{1,0:T(8,128)(2,1)}, bf16[72,1536]{1,0:T(8,128)(2,1)S(1)}, u32[]{:S(2)}, u32[]{:S(2)}) collective-permute-start(bf16[72,1536]{1,0:T(8,128)(2,1)} %refs_7_.1), channel_id=1, source_target_pairs={{0,12},{1,13},{2,14},{3,15},{4,8},{5,9},{6,10},{7,11},{8,4},{9,5},... | collective-permute-start | bytes 663560 | tf_op jit(solution)/shard_map/ppermute | solution.py:22
  1.9 11.3 %collective-permute-start = (bf16[72,1536]{1,0:T(8,128)(2,1)}, bf16[72,1536]{1,0:T(8,128)(2,1)S(1)}, u32[]{:S(2)}, u32[]{:S(2)}) collective-permute-start(bf16[72,1536]{1,0:T(8,128)(2,1)} %refs_7_.1), channel_id=1, source_target_pairs={{0,2},{1,3},{2,0},{3,1},{4,6},{5,7},{6,4},{7,5},{8,10},{9,11},{10,... | collective-permute-start | bytes 663560 | tf_op jit(solution)/shard_map/ppermute | solution.py:22
  3.2 10.0 %collective-permute-start.1 = (bf16[72,1536]{1,0:T(8,128)(2,1)}, bf16[72,1536]{1,0:T(8,128)(2,1)S(1)}, u32[]{:S(2)}, u32[]{:S(2)}) collective-permute-start(bf16[72,1536]{1,0:T(8,128)(2,1)} %fresh_ref.1), channel_id=1, source_target_pairs={{12,14},{13,15},{14,12},{15,13},{28,30},{29,31},{30,28},{31,29}} | collective-permute-start | bytes 663560 | tf_op jit(solution)/shard_map/ppermute | solution.py:22
  7.0 6.3 %copy-start = (bf16[72,1536]{1,0:T(8,128)(2,1)S(1)}, bf16[72,1536]{1,0:T(8,128)(2,1)}, u32[]{:S(2)}) copy-start(bf16[72,1536]{1,0:T(8,128)(2,1)} %refs_7_.1) | copy-start | bytes 663556
  7.0 6.3 %copy-start.1 = (bf16[72,1536]{1,0:T(8,128)(2,1)S(1)}, bf16[72,1536]{1,0:T(8,128)(2,1)}, u32[]{:S(2)}) copy-start(bf16[72,1536]{1,0:T(8,128)(2,1)} %fresh_ref.1) | copy-start | bytes 663556
  15.8 28.0 %collective-permute-start.8 = (bf16[288,1536]{1,0:T(8,128)(2,1)S(1)}, bf16[288,1536]{1,0:T(8,128)(2,1)S(1)}, u32[]{:S(2)}, u32[]{:S(2)}) collective-permute-start(bf16[288,1536]{1,0:T(8,128)(2,1)S(1)} %get-tuple-element.37.refs_0_.fresh_mine_ref), channel_id=1, source_target_pairs={{0,1},{1,0},{2,3},{3,2},{4,5},{5,4},{6,7},{7,6},{8,9},{9,8},{10,11... | collective-permute-start | bytes 2654216 | tf_op jit(solution)/shard_map/ppermute | solution.py:22
  17.3 6.9 %collective-permute-start.2 = (bf16[72,1536]{1,0:T(8,128)(2,1)S(1)}, bf16[72,1536]{1,0:T(8,128)(2,1)S(1)}, u32[]{:S(2)}, u32[]{:S(2)}) collective-permute-start(bf16[72,1536]{1,0:T(8,128)(2,1)S(1)} %copy-done), channel_id=1, source_target_pairs={{0,4},{1,5},{2,6},{3,7},{4,0},{5,1},{6,2},{7,3},{8,12},{9,13},{10,... | collective-permute-start | bytes 663560 | tf_op jit(solution)/shard_map/ppermute | solution.py:22
  17.4 8.8 %collective-permute-start.5 = (bf16[72,1536]{1,0:T(8,128)(2,1)S(1)}, bf16[72,1536]{1,0:T(8,128)(2,1)S(1)}, u32[]{:S(2)}, u32[]{:S(2)}) collective-permute-start(bf16[72,1536]{1,0:T(8,128)(2,1)S(1)} %collective-permute-done.3.refs_1_.refs_9_), channel_id=1, source_target_pairs={{4,6},{5,7},{6,4},{7,5},{8,10},{9,11},{10,8},{11,9},{12,14},{13,15... | collective-permute-start | bytes 663560 | tf_op jit(solution)/shard_map/ppermute | solution.py:22
  20.5 9.4 %collective-permute-start.4 = (bf16[72,1536]{1,0:T(8,128)(2,1)S(1)}, bf16[72,1536]{1,0:T(8,128)(2,1)S(1)}, u32[]{:S(2)}, u32[]{:S(2)}) collective-permute-start(bf16[72,1536]{1,0:T(8,128)(2,1)S(1)} %collective-permute-done.refs_2_.refs_11_), channel_id=1, source_target_pairs={{0,4},{1,5},{2,6},{3,7},{4,0},{5,1},{6,2},{7,3},{8,12},{9,13},{10,... | collective-permute-start | bytes 663560 | tf_op jit(solution)/shard_map/ppermute | solution.py:22
  22.0 14.1 %collective-permute-start.6 = (bf16[72,1536]{1,0:T(8,128)(2,1)S(1)}, bf16[72,1536]{1,0:T(8,128)(2,1)S(1)}, u32[]{:S(2)}, u32[]{:S(2)}) collective-permute-start(bf16[72,1536]{1,0:T(8,128)(2,1)S(1)} %copy-done), channel_id=1, source_target_pairs={{0,8},{1,9},{2,10},{3,11},{4,12},{5,13},{6,14},{7,15},{16,24},{17,... | collective-permute-start | bytes 663560 | tf_op jit(solution)/shard_map/ppermute | solution.py:22
  32.3 15.0 %collective-permute-start.9 = (bf16[288,1536]{1,0:T(8,128)(2,1)S(1)}, bf16[288,1536]{1,0:T(8,128)(2,1)S(1)}, u32[]{:S(2)}, u32[]{:S(2)}) collective-permute-start(bf16[288,1536]{1,0:T(8,128)(2,1)S(1)} %get-tuple-element.38.refs_1_), channel_id=1, source_target_pairs={{0,1},{1,0},{2,3},{3,2},{4,5},{5,4},{6,7},{7,6},{8,9},{9,8},{10,11... | collective-permute-start | bytes 2654216 | tf_op jit(solution)/shard_map/ppermute | solution.py:22
  36.1 7.6 %collective-permute-start.7 = (bf16[72,1536]{1,0:T(8,128)(2,1)S(1)}, bf16[72,1536]{1,0:T(8,128)(2,1)S(1)}, u32[]{:S(2)}, u32[]{:S(2)}) collective-permute-start(bf16[72,1536]{1,0:T(8,128)(2,1)S(1)} %collective-permute-done.6.refs_0_.refs_10_), channel_id=1, source_target_pairs={{8,10},{9,11},{10,8},{11,9},{12,14},{13,15},{14,12},{15,13},{24,26... | collective-permute-start | bytes 663560 | tf_op jit(solution)/shard_map/ppermute | solution.py:22
  45.1 5.3 %collective-permute-start.10 = (bf16[144,1536]{1,0:T(8,128)(2,1)S(1)}, bf16[144,1536]{1,0:T(8,128)(2,1)S(1)}, u32[]{:S(2)}, u32[]{:S(2)}) collective-permute-start(bf16[144,1536]{1,0:T(8,128)(2,1)S(1)} %get-tuple-element.41.refs_2_), channel_id=1, source_target_pairs={{0,1},{1,0},{2,3},{3,2},{4,5},{5,4},{6,7},{7,6},{8,9},{9,8},{10,11... | collective-permute-start | bytes 1327112 | tf_op jit(solution)/shard_map/ppermute | solution.py:22
  58.8 3.1 %collective-permute-start.11 = (bf16[432,1536]{1,0:T(8,128)(2,1)S(1)}, bf16[432,1536]{1,0:T(8,128)(2,1)S(1)}, u32[]{:S(2)}, u32[]{:S(2)}) collective-permute-start(bf16[432,1536]{1,0:T(8,128)(2,1)S(1)} %get-tuple-element.52.mine_ref), channel_id=1, source_target_pairs={{0,1},{1,0},{2,3},{3,2},{4,5},{5,4},{6,7},{7,6},{8,9},{9,8},{10,11... | collective-permute-start | bytes 3981320 | tf_op jit(solution)/shard_map/ppermute | solution.py:22

commit v3 on v2

--- a/solution.py
+++ b/solution.py
@@ -125,16 +125,28 @@
 
 def weigh(scores, pairs, state=None):
     top = functools.reduce(jnp.maximum, [jnp.max(s, axis=-1, keepdims=True) for s in scores])
-    total, summed = 0.0, 0.0
+    rows = top.shape[0]
+    top = jnp.broadcast_to(top, (rows, HEAD_DIM))
     if state is not None:
         old_top, old_total, old_summed = state()
         top = jnp.maximum(top, old_top)
+    total, summed = 0.0, 0.0
+    for part, (_, values) in zip(scores, pairs):
+        rounded = []
+        sums = []
+        for low in range(0, part.shape[1], HEAD_DIM):
+            piece = part[:, low : low + HEAD_DIM]
+            weights = jnp.exp2((piece - top[:, : piece.shape[1]]) * SHARPNESS)
+            sums.append(jnp.sum(weights, axis=-1, keepdims=True) if piece.shape[1] < HEAD_DIM else weights)
+            rounded.append(weights.astype(jnp.bfloat16))
+        full = [w for w in sums if w.shape[1] == HEAD_DIM]
+        for w in [functools.reduce(jnp.add, full)] * (len(full) > 0) + [w for w in sums if w.shape[1] < HEAD_DIM]:
+            total = total + jnp.sum(w, axis=-1, keepdims=True)
+        summed = summed + dot(jnp.concatenate(rounded, axis=1), values())
+    total = jnp.broadcast_to(total, (rows, HEAD_DIM))
+    if state is not None:
         fade = jnp.exp2((old_top - top) * SHARPNESS)
-        total, summed = old_total * fade, old_summed * fade
-    for part, (_, values) in zip(scores, pairs):
-        weights = jnp.exp2((part - top) * SHARPNESS)
-        total = total + jnp.sum(weights, axis=-1, keepdims=True)
-        summed = summed + dot(weights.astype(jnp.bfloat16), values())
+        total, summed = old_total * fade + total, old_summed * fade + summed
     return top, total, summed
 
 
@@ -202,15 +214,14 @@
     )(*in_hbm[:-1], embedding, in_hbm[-1])
 
 
-def project_kernel(where, *refs, slots):
+def project_kernel(where, *refs, slots, counts):
     refs = list(refs)
-    own = [refs.pop(0) for _ in slots]
-    across = [refs.pop(0) for _ in slots]
+    parts = [[refs.pop(0) for _ in range(n)] for n in counts]
     mods_ref, wk_ref, wv_ref, wq_ref, kv_ref, q_ref = refs
     depth, width = wk_ref.shape
     hidden = []
     for i, slot in enumerate(slots):
-        rows_f = jnp.concatenate([own[i][...].astype(jnp.float32), across[i][...].astype(jnp.float32)])
+        rows_f = jnp.concatenate([part[...].astype(jnp.float32) for part in parts[i]])
         section = LAST if slot is None else where[0] ^ slot
         row = mods_ref[pl.ds(section, 1), :]
         hidden.append(modulate(rows_f, row[:, depth:], row[:, :depth]))
@@ -220,28 +231,28 @@
     q_ref[...] = dot(hidden, wq_ref[...]).astype(jnp.bfloat16)
 
 
-def project(where, slots, own, across, mods, weights):
-    local, depth = own[0].shape
-    width = weights[0].shape[1]
-    rows = 2 * local * len(slots)
+def project(where, slots, parts, mods, weights):
+    args = [p for rows in parts for p in rows]
+    depth, width = weights[0].shape
+    rows = sum(p.shape[0] for p in args)
     return pl.pallas_call(
-        functools.partial(project_kernel, slots=slots),
+        functools.partial(project_kernel, slots=slots, counts=[len(p) for p in parts]),
         out_shape=(
             jax.ShapeDtypeStruct((rows, 2 * width), jnp.bfloat16),
             jax.ShapeDtypeStruct((rows, width), jnp.bfloat16),
         ),
-        in_specs=[SMEM] + [VMEM] * (2 * len(slots) + 4),
+        in_specs=[SMEM] + [VMEM] * (len(args) + 4),
         out_specs=(VMEM, VMEM),
         compiler_params=pltpu.CompilerParams(vmem_limit_bytes=12 << 20),
         cost_estimate=pl.CostEstimate(
             flops=6 * rows * depth * width, bytes_accessed=2 << 20, transcendentals=0
         ),
         name="project",
-    )(where, *own, *across, mods, *weights)
+    )(where, *args, mods, *weights)
 
 
 def state_shapes(rows, width):
-    stat = jax.ShapeDtypeStruct((width // HEAD_DIM, rows, 1), jnp.float32)
+    stat = jax.ShapeDtypeStruct((width // HEAD_DIM, rows, HEAD_DIM), jnp.float32)
     return stat, stat, jax.ShapeDtypeStruct((rows, width), jnp.float32)
 
 
@@ -250,35 +261,73 @@
     return [[refs.pop(0) for _ in range(n)] for n in counts] + refs
 
 
-def begin_kernel(where, *refs, groups):
+def key_place(section, slot):
+    source = section ^ slot
+    swapped = jnp.where(section == LAST, 1 - source, source)
+    return jnp.where(source > 1, source - 1, jnp.where(swapped == 1, 0, LAST))
+
+
+def set_keys(kv_ref, section, slot, offset, block):
+    base = key_place(section, slot) * (kv_ref.shape[0] // SECTIONS) + offset
+    kv_ref[pl.ds(pl.multiple_of(base, 16), block.shape[0]), :] = block
+
+
+def set_rows(x_ref, q_ref, section, slot, parts, queries):
+    half = q_ref.shape[0] // SECTIONS
+    base = pl.multiple_of((section ^ slot) * half, half)
+    q_ref[pl.ds(base, half), :] = queries
+    low = 0
+    for part in parts:
+        x_ref[pl.ds(pl.multiple_of(base + low, 8), part.shape[0]), :] = part[...].astype(jnp.float32)
+        low += part.shape[0]
+
+
+def place_kernel(where, *refs, groups, swapped):
     slots = [slot for group in groups for slot in group if slot is not None]
-    known = len(groups) - 1
-    kv_mine, kv_theirs, q_in, own_in, across_in, *refs = split(
-        refs, known, known, len(groups), len(slots), len(slots)
-    )
-    q_ref, x_ref, top_ref, total_ref, sum_ref, kv_ref = refs
-    local = own_in[0].shape[0]
-    half, span = 2 * local, 4 * local
-    width = q_ref.shape[1]
+    kv_mine, kv_theirs, q_in, *refs = split(refs, len(groups), swapped, len(groups))
+    *x_in, out = split(refs, *[2] * len(slots), 3)
+    kv_ref, x_ref, q_ref = out
+    half = q_ref.shape[0] // SECTIONS
     section = where[0]
-    at_last = section == LAST
     for g, group in enumerate(groups):
         for i, slot in enumerate(group):
             if slot is None:
                 continue
             rows = slice(i * half, (i + 1) * half)
-            source = section ^ slot
-            base = pl.multiple_of(source * half, half)
-            q_ref[pl.ds(base, half), :] = q_in[g][rows, :]
-            n = slots.index(slot)
-            x_ref[pl.ds(base, local), :] = own_in[n][...].astype(jnp.float32)
-            x_ref[pl.ds(base + local, local), :] = across_in[n][...].astype(jnp.float32)
-            if g < known:
-                swapped = jnp.where(at_last, 1 - source, source)
-                place = jnp.where(source > 1, source - 1, jnp.where(swapped == 1, 0, LAST))
-                base = pl.multiple_of(place * span, span)
-                kv_ref[pl.ds(base, half), :] = kv_mine[g][rows, :]
-                kv_ref[pl.ds(base + half, half), :] = kv_theirs[g][rows, :]
+            set_rows(x_ref, q_ref, section, slot, x_in[slots.index(slot)], q_in[g][rows, :])
+            set_keys(kv_ref, section, slot, 0, kv_mine[g][rows, :])
+            if g < swapped:
+                set_keys(kv_ref, section, slot, half, kv_theirs[g][rows, :])
+
+
+def place(where, groups, kv_mine, kv_theirs, q, parts):
+    local, depth = parts[0][0].shape
+    half, width = 2 * local, q[0].shape[1]
+    args = [*kv_mine, *kv_theirs, *q, *(p for rows in parts for p in rows)]
+    return pl.pallas_call(
+        functools.partial(place_kernel, groups=groups, swapped=len(kv_theirs)),
+        out_shape=(
+            jax.ShapeDtypeStruct((SECTIONS * 2 * half, 2 * width), jnp.bfloat16),
+            jax.ShapeDtypeStruct((SECTIONS * half, depth), jnp.float32),
+            jax.ShapeDtypeStruct((SECTIONS * half, width), jnp.bfloat16),
+        ),
+        in_specs=[SMEM] + [VMEM] * len(args),
+        out_specs=(VMEM,) * 3,
+        compiler_params=pltpu.CompilerParams(vmem_limit_bytes=4 << 20),
+        cost_estimate=pl.CostEstimate(flops=0, bytes_accessed=4 << 20, transcendentals=0),
+        name="place",
+    )(where, *args)
+
+
+def begin_kernel(where, theirs_ref, late_q_ref, own_ref, across_ref, kv_in, x_in, q_in,
+                 kv_ref, x_ref, q_ref, top_ref, total_ref, sum_ref, *, groups):
+    half = q_ref.shape[0] // SECTIONS
+    span = 2 * half
+    width = q_ref.shape[1]
+    section = where[0]
+    for i, slot in enumerate(groups[1]):
+        set_keys(kv_ref, section, slot, half, theirs_ref[i * half : (i + 1) * half, :])
+    set_rows(x_ref, q_ref, section, groups[2][0], (own_ref, across_ref), late_q_ref[...])
     jobs = []
     for s in range(1, SECTIONS):
         rows, seen = slice((s - 1) * half, s * half), slice(0, s * span)
@@ -294,34 +343,28 @@
     attend_all(jobs)
 
 
-def begin_first(where, groups, kv_mine, kv_theirs, q, own, across):
-    local, depth = own[0].shape
-    width = q[0].shape[1]
-    half, span = 2 * local, 4 * local
-    args = [*kv_mine[:-1], *kv_theirs[:-1], *q, *own, *across]
+def begin_first(where, groups, placed, theirs, late_q, late_parts):
+    half, width = placed[2].shape[0] // SECTIONS, late_q.shape[1]
+    same = [jax.ShapeDtypeStruct(p.shape, p.dtype) for p in placed]
     return pl.pallas_call(
         functools.partial(begin_kernel, groups=groups),
-        out_shape=(
-            jax.ShapeDtypeStruct((SECTIONS * half, width), jnp.bfloat16),
-            jax.ShapeDtypeStruct((SECTIONS * half, depth), jnp.float32),
-            *state_shapes(LAST * half, width),
-        ),
-        in_specs=[SMEM] + [VMEM] * len(args),
-        out_specs=(VMEM,) * 5,
-        scratch_shapes=[pltpu.VMEM((SECTIONS * span, 2 * width), jnp.bfloat16)],
+        out_shape=(*same, *state_shapes(LAST * half, width)),
+        in_specs=[SMEM] + [VMEM] * 7,
+        out_specs=(VMEM,) * 6,
+        input_output_aliases={5: 0, 6: 1, 7: 2},
         compiler_params=pltpu.CompilerParams(vmem_limit_bytes=12 << 20),
         cost_estimate=pl.CostEstimate(
-            flops=24 * half * span * width, bytes_accessed=2 << 20, transcendentals=0
+            flops=24 * half * 2 * half * width, bytes_accessed=2 << 20, transcendentals=0
         ),
         name="begin_first",
-    )(where, *args)
+    )(where, theirs, late_q, *late_parts, *placed)[1:]
 
 
 def finish_kernel(where, steps, *refs, groups):
     known = len(groups)
     kv_mine, kv_theirs, refs_q = split(refs, known, known, 5)[:3]
     refs = list(refs)[2 * known + 5 :]
-    q_ref, x_ref, top_ref, total_ref, sum_ref = refs_q
+    x_ref, q_ref, top_ref, total_ref, sum_ref = refs_q
     mods_ref, wk_ref, wv_ref, wo_ref = refs[:4]
     stepped_hbm, velocity_hbm, kv2_ref, own2_ref, next_ref = refs[4:9]
     late_ref, o_ref, v_ref, st_ref, hid_ref, out_ref, sem = refs[9:]
@@ -578,27 +621,28 @@
     own = {0: latents, None: fresh_noise}
     for slot in (3, 1, 2):
         own[slot] = from_section(latents, slot)
-    across = {slot: chip_swap(own[slot], slot) for slot in (0, None, 3)}
-    across[1] = from_section(across[0], 1)
+    parts = {slot: [own[slot], chip_swap(own[slot], slot)] for slot in (0, None, 3)}
+    parts[1] = [own[1], from_section(parts[0][1], 1)]
     mine, theirs, q = {}, {}, {}
 
     def work(group):
-        mine[group], q[group] = project(
-            where, group, [own[x] for x in group], [across[x] for x in group], mods, weights
-        )
+        mine[group], q[group] = project(where, group, [parts[x] for x in group], mods, weights)
         theirs[group] = core_swap(mine[group])
 
     work(groups[0])
     own[2] = after(own[2], own[3], mine[groups[0]])
-    across[2] = chip_swap(own[2], 2)
+    parts[2] = [own[2], chip_swap(own[2], 2)]
     work(groups[1])
-    across[2] = after(across[2], theirs[groups[0]], mine[groups[1]])
+    early = groups[:-1]
+    placed = place(
+        where, early, [mine[g] for g in early], [theirs[groups[0]]], [q[g] for g in early],
+        [parts[x] for g in early for x in g if x is not None],
+    )
+    parts[2][1] = after(parts[2][1], *placed)
     work(groups[2])
-    slots = [x for group in groups for x in group if x is not None]
     all_mine, all_theirs = [mine[g] for g in groups], [theirs[g] for g in groups]
     begun = begin_first(
-        where, groups, all_mine, all_theirs, [q[g] for g in groups],
-        [own[x] for x in slots], [across[x] for x in slots],
+        where, groups, placed, theirs[groups[1]], q[groups[2]], parts[groups[2][0]]
     )
     stepped, velocity, mine2, own2, old = finish_first(
         where, steps, groups, all_mine, all_theirs, begun, mods, w_key, w_value, w_out

time: 65.4 us -> 63.6 us (0.972)
  the two profiles are of different devices: /device:TPU:27 before, /device:TPU:25 now
where the time goes in v3:
time: 63.6 us; the launch traced here: 63.4 us
  Pallas kernels  24.9 us (39%)
  waiting for transfers between devices  18.2 us (29%)
  starting transfers between devices  17.7 us (28%)
  other arithmetic  1.6 us (3%)
  between operations  0.94 us (1%)
    ppermute x12, waiting for transfers between devices, permuted(): return lax.ppermute(block, axis, route)  18.2 us
    ppermute x12, starting transfers between devices, permuted(): return lax.ppermute(block, axis, route)  17.7 us
    pallas_call x1, Pallas kernels, finish_first(): pl.pallas_call(functools.partial(finish_kernel, groups=groups), out_shape...  6.98 us
    pallas_call x3, Pallas kernels, project(): pl.pallas_call(functools.partial(project_kernel, slots=slots, counts=[len...  6.3 us
    pallas_call x1, Pallas kernels, fetch(): pl.pallas_call(functools.partial(fetch_kernel, count=len(arrays)), out_sh...  4.3 us
    pallas_call x1, Pallas kernels, begin_first(): pl.pallas_call(functools.partial(begin_kernel, groups=groups), out_shape=...  3.1 us
    pallas_call x1, Pallas kernels, finish_second(): pl.pallas_call(finish_second_kernel, out_shape=(pair, pair), in_specs=[SM...  2.71 us
  transfers between devices with their start and end apart: 12, of which 7 were waited for; matrix products, arithmetic and copies ran while one was open for 3% of the time, Pallas kernels for 24%

profile of v3, /device:TPU:25, one launch (start us, length us, event | category | flops | bytes accessed | tf_op | source)
XLA Modules:
  0.0 63.4 jit_solution(11636079176329220992)
XLA Ops:
  0.6 1.3 %collective-permute-start.4 = (bf16[72,1536]{1,0:T(8,128)(2,1)}, bf16[72,1536]{1,0:T(8,128)(2,1)S(1)}, u32[]{:S(2)}, u32[]{:S(2)}) collective-permute-start(bf16[72,1536]{1,0:T(8,128)(2,1)} %refs_5_.3), channel_id=1, source_target_pairs={{0,12},{1,13},{2,14},{3,15},{4,8},{5,9},{6,10},{7,11},{8,4},{9,5},... | collective-permute-start | bytes 663560 | tf_op jit(solution)/shard_map/ppermute | solution.py:22
  1.9 1.3 %collective-permute-start = (bf16[72,1536]{1,0:T(8,128)(2,1)}, bf16[72,1536]{1,0:T(8,128)(2,1)S(1)}, u32[]{:S(2)}, u32[]{:S(2)}) collective-permute-start(bf16[72,1536]{1,0:T(8,128)(2,1)} %refs_5_.3), channel_id=1, source_target_pairs={{0,2},{1,3},{2,0},{3,1},{4,6},{5,7},{6,4},{7,5},{8,10},{9,11},{10,... | collective-permute-start | bytes 663560 | tf_op jit(solution)/shard_map/ppermute | solution.py:22
  3.2 2.1 %collective-permute-start.1 = (bf16[72,1536]{1,0:T(8,128)(2,1)}, bf16[72,1536]{1,0:T(8,128)(2,1)S(1)}, u32[]{:S(2)}, u32[]{:S(2)}) collective-permute-start(bf16[72,1536]{1,0:T(8,128)(2,1)} %fresh_ref.1), channel_id=1, source_target_pairs={{12,14},{13,15},{14,12},{15,13},{28,30},{29,31},{30,28},{31,29}} | collective-permute-start | bytes 663560 | tf_op jit(solution)/shard_map/ppermute | solution.py:22
  5.4 0.7 %convert_element_type.6 = f32[4]{0:T(128)S(1)} convert(s32[4]{0:T(128)} %param.10) | non-fusion elementwise | flops 4 | bytes 32 | tf_op jit(solution)/shard_map/convert_element_type | solution.py:27
  6.1 0.1 multiply_cosine_fusion
  6.2 0.8 %fusion.1.steps = f32[4]{0:T(128)S(1)} fusion(s32[4]{0:T(128)} %param.10, s32[3]{0:T(128)} %bitcast.2, s32[1]{0:T(128)} %constant.28.clone.1), kind=kLoop, calls=%fused_computation.5 | loop fusion | flops 16 | bytes 48 | tf_op jit(solution)/shard_map/div | solution.py:41
  7.0 4.3 %fetch.1 = (bf16[1536,768]{1,0:T(8,128)(2,1)S(1)}, bf16[1536,768]{1,0:T(8,128)(2,1)S(1)}, bf16[1536,768]{1,0:T(8,128)(2,1)S(1)}, bf16[768,1536]{1,0:T(8,128)(2,1)S(1)}, f32[4,3072]{1,0:T(4,128)S(1)}) custom-call(bf16[1536,768]{1,0:T(8,128)(2,1)} %refs_0_.2, bf16[1536,768]{1,0:T(8,128)(2,1)} %refs_1_.1, bf16[1536,768]{1,0:T(8,128)(2,1)} %refs_2_.2, ...), custom_call_target="tpu_custom_call" | custom-call | bytes 9437184 | tf_op jit(solution)/shard_map/fetch/pallas_call | solution.py:199
  11.3 1.9 %collective-permute-done.1.refs_3_ = bf16[72,1536]{1,0:T(8,128)(2,1)S(1)} collective-permute-done((bf16[72,1536]{1,0:T(8,128)(2,1)}, bf16[72,1536]{1,0:T(8,128)(2,1)S(1)}, u32[]{:S(2)}, u32[]{:S(2)}) %collective-permute-start.1) | collective-permute-done | bytes 221216 | tf_op jit(solution)/shard_map/ppermute | solution.py:22
  13.3 2.5 %project.3 = (bf16[288,1536]{1,0:T(8,128)(2,1)S(1)}, bf16[288,768]{1,0:T(8,128)(2,1)S(1)}) custom-call(s32[1]{0:T(128)} %bitcast.where, bf16[72,1536]{1,0:T(8,128)(2,1)S(1)} %copy-done, bf16[72,1536]{1,0:T(8,128)(2,1)S(1)} %collective-permute-done.refs_1_.refs_6_, bf16[72,1536]{1,0:T(8,128)(2,1)S(1)} %copy-done.1, ...), custom_call_target="tpu_custom_call" | custom-call | flops 2038431744 | bytes 2097152 | tf_op jit(solution)/shard_map/project/pallas_call | solution.py:238
  15.8 1.6 %collective-permute-start.8 = (bf16[288,1536]{1,0:T(8,128)(2,1)S(1)}, bf16[288,1536]{1,0:T(8,128)(2,1)S(1)}, u32[]{:S(2)}, u32[]{:S(2)}) collective-permute-start(bf16[288,1536]{1,0:T(8,128)(2,1)S(1)} %get-tuple-element.40.refs_0_.fresh_mine_ref), channel_id=1, source_target_pairs={{0,1},{1,0},{2,3},{3,2},{4,5},{5,4},{6,7},{7,6},{8,9},{9,8},{10,11... | collective-permute-start | bytes 2654216 | tf_op jit(solution)/shard_map/ppermute | solution.py:22
  17.3 0.0 collective-permute-start.2
  17.4 3.1 %collective-permute-start.5 = (bf16[72,1536]{1,0:T(8,128)(2,1)S(1)}, bf16[72,1536]{1,0:T(8,128)(2,1)S(1)}, u32[]{:S(2)}, u32[]{:S(2)}) collective-permute-start(bf16[72,1536]{1,0:T(8,128)(2,1)S(1)} %collective-permute-done.4.refs_2_.refs_9_), channel_id=1, source_target_pairs={{4,6},{5,7},{6,4},{7,5},{8,10},{9,11},{10,8},{11,9},{12,14},{13,15... | collective-permute-start | bytes 663560 | tf_op jit(solution)/shard_map/ppermute | solution.py:22
  20.5 1.5 %collective-permute-start.3 = (bf16[72,1536]{1,0:T(8,128)(2,1)S(1)}, bf16[72,1536]{1,0:T(8,128)(2,1)S(1)}, u32[]{:S(2)}, u32[]{:S(2)}) collective-permute-start(bf16[72,1536]{1,0:T(8,128)(2,1)S(1)} %collective-permute-done.refs_1_.refs_6_), channel_id=1, source_target_pairs={{0,4},{1,5},{2,6},{3,7},{4,0},{5,1},{6,2},{7,3},{8,12},{9,13},{10,... | collective-permute-start | bytes 663560 | tf_op jit(solution)/shard_map/ppermute | solution.py:22
  22.0 1.3 %collective-permute-start.6 = (bf16[72,1536]{1,0:T(8,128)(2,1)S(1)}, bf16[72,1536]{1,0:T(8,128)(2,1)S(1)}, u32[]{:S(2)}, u32[]{:S(2)}) collective-permute-start(bf16[72,1536]{1,0:T(8,128)(2,1)S(1)} %copy-done), channel_id=1, source_target_pairs={{0,8},{1,9},{2,10},{3,11},{4,12},{5,13},{6,14},{7,15},{16,24},{17,... | collective-permute-start | bytes 663560 | tf_op jit(solution)/shard_map/ppermute | solution.py:22
  23.3 0.9 %collective-permute-done.2.refs_0_.refs_7_ = bf16[72,1536]{1,0:T(8,128)(2,1)S(1)} collective-permute-done((bf16[72,1536]{1,0:T(8,128)(2,1)S(1)}, bf16[72,1536]{1,0:T(8,128)(2,1)S(1)}, u32[]{:S(2)}, u32[]{:S(2)}) %collective-permute-start.2) | collective-permute-done | bytes 221216 | tf_op jit(solution)/shard_map/ppermute | solution.py:22
  24.3 1.9 %collective-permute-done.5.refs_3_.refs_10_ = bf16[72,1536]{1,0:T(8,128)(2,1)S(1)} collective-permute-done((bf16[72,1536]{1,0:T(8,128)(2,1)S(1)}, bf16[72,1536]{1,0:T(8,128)(2,1)S(1)}, u32[]{:S(2)}, u32[]{:S(2)}) %collective-permute-start.5) | collective-permute-done | bytes 221216 | tf_op jit(solution)/shard_map/ppermute | solution.py:22
  26.1 3.8 %collective-permute-done.3.refs_1_.refs_8_ = bf16[72,1536]{1,0:T(8,128)(2,1)S(1)} collective-permute-done((bf16[72,1536]{1,0:T(8,128)(2,1)S(1)}, bf16[72,1536]{1,0:T(8,128)(2,1)S(1)}, u32[]{:S(2)}, u32[]{:S(2)}) %collective-permute-start.3) | collective-permute-done | bytes 221216 | tf_op jit(solution)/shard_map/ppermute | solution.py:22
  29.9 2.5 %project.4 = (bf16[288,1536]{1,0:T(8,128)(2,1)S(1)}, bf16[288,768]{1,0:T(8,128)(2,1)S(1)}) custom-call(s32[1]{0:T(128)} %bitcast.where, bf16[72,1536]{1,0:T(8,128)(2,1)S(1)} %collective-permute-done.2.refs_0_.refs_7_, bf16[72,1536]{1,0:T(8,128)(2,1)S(1)} %collective-permute-done.3.refs_1_.refs_8_, ...), custom_call_target="tpu_custom_call" | custom-call | flops 2038431744 | bytes 2097152 | tf_op jit(solution)/shard_map/project/pallas_call | solution.py:238
  32.4 1.0 %collective-permute-start.9 = (bf16[288,1536]{1,0:T(8,128)(2,1)S(1)}, bf16[288,1536]{1,0:T(8,128)(2,1)S(1)}, u32[]{:S(2)}, u32[]{:S(2)}) collective-permute-start(bf16[288,1536]{1,0:T(8,128)(2,1)S(1)} %get-tuple-element.41.refs_1_), channel_id=1, source_target_pairs={{0,1},{1,0},{2,3},{3,2},{4,5},{5,4},{6,7},{7,6},{8,9},{9,8},{10,11... | collective-permute-start | bytes 2654216 | tf_op jit(solution)/shard_map/ppermute | solution.py:22
  33.4 2.8 %collective-permute-done.6.refs_0_.own_ref = bf16[72,1536]{1,0:T(8,128)(2,1)S(1)} collective-permute-done((bf16[72,1536]{1,0:T(8,128)(2,1)S(1)}, bf16[72,1536]{1,0:T(8,128)(2,1)S(1)}, u32[]{:S(2)}, u32[]{:S(2)}) %collective-permute-start.6) | collective-permute-done | bytes 221216 | tf_op jit(solution)/shard_map/ppermute | solution.py:22
  36.1 2.2 %collective-permute-start.7 = (bf16[72,1536]{1,0:T(8,128)(2,1)S(1)}, bf16[72,1536]{1,0:T(8,128)(2,1)S(1)}, u32[]{:S(2)}, u32[]{:S(2)}) collective-permute-start(bf16[72,1536]{1,0:T(8,128)(2,1)S(1)} %collective-permute-done.6.refs_0_.own_ref), channel_id=1, source_target_pairs={{8,10},{9,11},{10,8},{11,9},{12,14},{13,15},{14,12},{15,13},{24,26... | collective-permute-start | bytes 663560 | tf_op jit(solution)/shard_map/ppermute | solution.py:22
  38.3 0.0 collective-permute-done.8.refs_2_.refs_3_.fresh_theirs_ref
  38.3 0.3 place.1
  38.7 5.1 %collective-permute-done.7.refs_1_.across_ref = bf16[72,1536]{1,0:T(8,128)(2,1)S(1)} collective-permute-done((bf16[72,1536]{1,0:T(8,128)(2,1)S(1)}, bf16[72,1536]{1,0:T(8,128)(2,1)S(1)}, u32[]{:S(2)}, u32[]{:S(2)}) %collective-permute-start.7) | collective-permute-done | bytes 221216 | tf_op jit(solution)/shard_map/ppermute | solution.py:22
  43.7 1.3 %project.5 = (bf16[144,1536]{1,0:T(8,128)(2,1)S(1)}, bf16[144,768]{1,0:T(8,128)(2,1)S(1)}) custom-call(s32[1]{0:T(128)} %bitcast.where, bf16[72,1536]{1,0:T(8,128)(2,1)S(1)} %collective-permute-done.6.refs_0_.own_ref, bf16[72,1536]{1,0:T(8,128)(2,1)S(1)} %collective-permute-done.7.refs_1_.across_ref, ...), custom_call_target="tpu_custom_call" | custom-call | flops 1019215872 | bytes 2097152 | tf_op jit(solution)/shard_map/project/pallas_call | solution.py:238
  45.1 2.2 %collective-permute-start.10 = (bf16[144,1536]{1,0:T(8,128)(2,1)S(1)}, bf16[144,1536]{1,0:T(8,128)(2,1)S(1)}, u32[]{:S(2)}, u32[]{:S(2)}) collective-permute-start(bf16[144,1536]{1,0:T(8,128)(2,1)S(1)} %get-tuple-element.49.refs_2_), channel_id=1, source_target_pairs={{0,1},{1,0},{2,3},{3,2},{4,5},{5,4},{6,7},{7,6},{8,9},{9,8},{10,11... | collective-permute-start | bytes 1327112 | tf_op jit(solution)/shard_map/ppermute | solution.py:22
  47.3 3.1 %begin_first.1 = (bf16[1152,1536]{1,0:T(8,128)(2,1)S(1)}, f32[576,1536]{1,0:T(8,128)S(1)}, bf16[576,768]{1,0:T(8,128)(2,1)S(1)}, f32[6,432,128]{2,1,0:T(8,128)S(...) custom-call(s32[1]{0:T(128)} %bitcast.where, ...), custom_call_target="tpu_custom_call", output_to_operand_aliasing={{0}: (5, {}), {1}: (6, {}), {2}: (7, {})} | custom-call | flops 764411904 | bytes 2097152 | tf_op jit(solution)/shard_map/begin_first/pallas_call | solution.py:349
  50.4 7.0 %finish_first.1 = (bf16[2,72,1536]{2,1,0:T(8,128)(2,1)}, bf16[2,72,1536]{2,1,0:T(8,128)(2,1)}, bf16[432,1536]{1,0:T(8,128)(2,1)S(1)}, bf16[72,1536]{1,0:T(8,128)(2,1)S(1)}, bf16[72,1536]{1,0:T(8,128)(2,1)S(1)}) custom-call(s32[1]{0:T(128)} %bitcast.where, f32[4]{0:T(128)S(1)} %fusion.1.steps, bf16[288,1536]{1,0:T(8,128)(2,1)S(1)} %get-tuple-element.40.refs_0_.fresh_mine_ref, ...), custom_call_target="tpu_custom_call" | custom-call | flops 4076863488 | bytes 4194304 | tf_op jit(solution)/shard_map/finish_first/pallas_call | solution.py:446
  57.4 0.1 collective-permute-start.11
  57.5 1.1 %begin_second.1 = (bf16[72,768]{1,0:T(8,128)(2,1)S(1)}, f32[6,72,128]{2,1,0:T(8,128)S(1)}, f32[6,72,128]{2,1,0:T(8,128)S(1)}, f32[72,768]{1,0:T(8,128)S(1)}) custom-call(s32[1]{0:T(128)} %bitcast.where, bf16[72,1536]{1,0:T(8,128)(2,1)S(1)} %get-tuple-element.57.own_ref, bf16[1536,768]{1,0:T(8,128)(2,1)S(1)} %get-tuple-element.39.refs_7_.refs_5_.wq_ref, ...), custom_call_target="tpu_custom_call" | custom-call | flops 339738624 | bytes 2097152 | tf_op jit(solution)/shard_map/begin_second/pallas_call | solution.py:503
  58.6 1.9 %collective-permute-done.11.theirs_ref = bf16[432,1536]{1,0:T(8,128)(2,1)S(1)} collective-permute-done((bf16[432,1536]{1,0:T(8,128)(2,1)S(1)}, bf16[432,1536]{1,0:T(8,128)(2,1)S(1)}, u32[]{:S(2)}, u32[]{:S(2)}) %collective-permute-start.11) | collective-permute-done | bytes 1327136 | tf_op jit(solution)/shard_map/ppermute | solution.py:22
  60.5 2.7 %finish_second.1 = (bf16[2,72,1536]{2,1,0:T(8,128)(2,1)}, bf16[2,72,1536]{2,1,0:T(8,128)(2,1)}) custom-call(s32[1]{0:T(128)} %bitcast.where, f32[4]{0:T(128)S(1)} %fusion.1.steps, bf16[72,768]{1,0:T(8,128)(2,1)S(1)} %get-tuple-element.59.q_ref, f32[6,72,128]{2,1,0:T(8,128)S(1)} %get-tuple-element.60.top_ref, ...), custom_call_target="tpu_custom_call", output_to_operand_aliasing={{0}: (10, {}), {1}: (11, {})} | custom-call | flops 339738624 | bytes 4194304 | tf_op jit(solution)/shard_map/finish_second/pallas_call | solution.py:562
  (10 shorter events, 0.0 us)
Async XLA Ops:
  0.6 16.7 %collective-permute-start.4 = (bf16[72,1536]{1,0:T(8,128)(2,1)}, bf16[72,1536]{1,0:T(8,128)(2,1)S(1)}, u32[]{:S(2)}, u32[]{:S(2)}) collective-permute-start(bf16[72,1536]{1,0:T(8,128)(2,1)} %refs_5_.3), channel_id=1, source_target_pairs={{0,12},{1,13},{2,14},{3,15},{4,8},{5,9},{6,10},{7,11},{8,4},{9,5},... | collective-permute-start | bytes 663560 | tf_op jit(solution)/shard_map/ppermute | solution.py:22
  1.9 9.4 %collective-permute-start = (bf16[72,1536]{1,0:T(8,128)(2,1)}, bf16[72,1536]{1,0:T(8,128)(2,1)S(1)}, u32[]{:S(2)}, u32[]{:S(2)}) collective-permute-start(bf16[72,1536]{1,0:T(8,128)(2,1)} %refs_5_.3), channel_id=1, source_target_pairs={{0,2},{1,3},{2,0},{3,1},{4,6},{5,7},{6,4},{7,5},{8,10},{9,11},{10,... | collective-permute-start | bytes 663560 | tf_op jit(solution)/shard_map/ppermute | solution.py:22
  3.2 10.0 %collective-permute-start.1 = (bf16[72,1536]{1,0:T(8,128)(2,1)}, bf16[72,1536]{1,0:T(8,128)(2,1)S(1)}, u32[]{:S(2)}, u32[]{:S(2)}) collective-permute-start(bf16[72,1536]{1,0:T(8,128)(2,1)} %fresh_ref.1), channel_id=1, source_target_pairs={{12,14},{13,15},{14,12},{15,13},{28,30},{29,31},{30,28},{31,29}} | collective-permute-start | bytes 663560 | tf_op jit(solution)/shard_map/ppermute | solution.py:22
  7.0 6.3 %copy-start = (bf16[72,1536]{1,0:T(8,128)(2,1)S(1)}, bf16[72,1536]{1,0:T(8,128)(2,1)}, u32[]{:S(2)}) copy-start(bf16[72,1536]{1,0:T(8,128)(2,1)} %refs_5_.3) | copy-start | bytes 663556
  7.0 6.3 %copy-start.1 = (bf16[72,1536]{1,0:T(8,128)(2,1)S(1)}, bf16[72,1536]{1,0:T(8,128)(2,1)}, u32[]{:S(2)}) copy-start(bf16[72,1536]{1,0:T(8,128)(2,1)} %fresh_ref.1) | copy-start | bytes 663556
  15.8 22.6 %collective-permute-start.8 = (bf16[288,1536]{1,0:T(8,128)(2,1)S(1)}, bf16[288,1536]{1,0:T(8,128)(2,1)S(1)}, u32[]{:S(2)}, u32[]{:S(2)}) collective-permute-start(bf16[288,1536]{1,0:T(8,128)(2,1)S(1)} %get-tuple-element.40.refs_0_.fresh_mine_ref), channel_id=1, source_target_pairs={{0,1},{1,0},{2,3},{3,2},{4,5},{5,4},{6,7},{7,6},{8,9},{9,8},{10,11... | collective-permute-start | bytes 2654216 | tf_op jit(solution)/shard_map/ppermute | solution.py:22
  17.3 6.9 %collective-permute-start.2 = (bf16[72,1536]{1,0:T(8,128)(2,1)S(1)}, bf16[72,1536]{1,0:T(8,128)(2,1)S(1)}, u32[]{:S(2)}, u32[]{:S(2)}) collective-permute-start(bf16[72,1536]{1,0:T(8,128)(2,1)S(1)} %copy-done), channel_id=1, source_target_pairs={{0,4},{1,5},{2,6},{3,7},{4,0},{5,1},{6,2},{7,3},{8,12},{9,13},{10,... | collective-permute-start | bytes 663560 | tf_op jit(solution)/shard_map/ppermute | solution.py:22
  17.4 8.8 %collective-permute-start.5 = (bf16[72,1536]{1,0:T(8,128)(2,1)S(1)}, bf16[72,1536]{1,0:T(8,128)(2,1)S(1)}, u32[]{:S(2)}, u32[]{:S(2)}) collective-permute-start(bf16[72,1536]{1,0:T(8,128)(2,1)S(1)} %collective-permute-done.4.refs_2_.refs_9_), channel_id=1, source_target_pairs={{4,6},{5,7},{6,4},{7,5},{8,10},{9,11},{10,8},{11,9},{12,14},{13,15... | collective-permute-start | bytes 663560 | tf_op jit(solution)/shard_map/ppermute | solution.py:22
  20.5 9.4 %collective-permute-start.3 = (bf16[72,1536]{1,0:T(8,128)(2,1)S(1)}, bf16[72,1536]{1,0:T(8,128)(2,1)S(1)}, u32[]{:S(2)}, u32[]{:S(2)}) collective-permute-start(bf16[72,1536]{1,0:T(8,128)(2,1)S(1)} %collective-permute-done.refs_1_.refs_6_), channel_id=1, source_target_pairs={{0,4},{1,5},{2,6},{3,7},{4,0},{5,1},{6,2},{7,3},{8,12},{9,13},{10,... | collective-permute-start | bytes 663560 | tf_op jit(solution)/shard_map/ppermute | solution.py:22
  22.0 14.1 %collective-permute-start.6 = (bf16[72,1536]{1,0:T(8,128)(2,1)S(1)}, bf16[72,1536]{1,0:T(8,128)(2,1)S(1)}, u32[]{:S(2)}, u32[]{:S(2)}) collective-permute-start(bf16[72,1536]{1,0:T(8,128)(2,1)S(1)} %copy-done), channel_id=1, source_target_pairs={{0,8},{1,9},{2,10},{3,11},{4,12},{5,13},{6,14},{7,15},{16,24},{17,... | collective-permute-start | bytes 663560 | tf_op jit(solution)/shard_map/ppermute | solution.py:22
  32.4 14.9 %collective-permute-start.9 = (bf16[288,1536]{1,0:T(8,128)(2,1)S(1)}, bf16[288,1536]{1,0:T(8,128)(2,1)S(1)}, u32[]{:S(2)}, u32[]{:S(2)}) collective-permute-start(bf16[288,1536]{1,0:T(8,128)(2,1)S(1)} %get-tuple-element.41.refs_1_), channel_id=1, source_target_pairs={{0,1},{1,0},{2,3},{3,2},{4,5},{5,4},{6,7},{7,6},{8,9},{9,8},{10,11... | collective-permute-start | bytes 2654216 | tf_op jit(solution)/shard_map/ppermute | solution.py:22
  36.1 7.6 %collective-permute-start.7 = (bf16[72,1536]{1,0:T(8,128)(2,1)S(1)}, bf16[72,1536]{1,0:T(8,128)(2,1)S(1)}, u32[]{:S(2)}, u32[]{:S(2)}) collective-permute-start(bf16[72,1536]{1,0:T(8,128)(2,1)S(1)} %collective-permute-done.6.refs_0_.own_ref), channel_id=1, source_target_pairs={{8,10},{9,11},{10,8},{11,9},{12,14},{13,15},{14,12},{15,13},{24,26... | collective-permute-start | bytes 663560 | tf_op jit(solution)/shard_map/ppermute | solution.py:22
  45.1 5.3 %collective-permute-start.10 = (bf16[144,1536]{1,0:T(8,128)(2,1)S(1)}, bf16[144,1536]{1,0:T(8,128)(2,1)S(1)}, u32[]{:S(2)}, u32[]{:S(2)}) collective-permute-start(bf16[144,1536]{1,0:T(8,128)(2,1)S(1)} %get-tuple-element.49.refs_2_), channel_id=1, source_target_pairs={{0,1},{1,0},{2,3},{3,2},{4,5},{5,4},{6,7},{7,6},{8,9},{9,8},{10,11... | collective-permute-start | bytes 1327112 | tf_op jit(solution)/shard_map/ppermute | solution.py:22
  57.4 3.1 %collective-permute-start.11 = (bf16[432,1536]{1,0:T(8,128)(2,1)S(1)}, bf16[432,1536]{1,0:T(8,128)(2,1)S(1)}, u32[]{:S(2)}, u32[]{:S(2)}) collective-permute-start(bf16[432,1536]{1,0:T(8,128)(2,1)S(1)} %get-tuple-element.58.mine_ref), channel_id=1, source_target_pairs={{0,1},{1,0},{2,3},{3,2},{4,5},{5,4},{6,7},{7,6},{8,9},{9,8},{10,11... | collective-permute-start | bytes 3981320 | tf_op jit(solution)/shard_map/ppermute | solution.py:22

commit v4 on v3

--- a/solution.py
+++ b/solution.py
@@ -214,15 +214,43 @@
     )(*in_hbm[:-1], embedding, in_hbm[-1])
 
 
-def project_kernel(where, *refs, slots, counts):
+OWN, NEXT, EARLY, LATE = range(4)
+
+
+def source_of(section, slot):
+    if slot == EARLY:
+        return jnp.where(section == LAST, 1, jnp.where(section == LAST - 1, 0, 2))
+    if slot == LATE:
+        return jnp.where(section == LAST, 0, jnp.where(section == LAST - 1, 1, LAST))
+    return section ^ slot
+
+
+def arrived(section, parts):
+    for part in parts:
+        if isinstance(part, tuple):
+            direct, relayed = (ref[...].astype(jnp.float32) for ref in part)
+            yield jnp.where(section == LAST, relayed, direct)
+        else:
+            yield part[...].astype(jnp.float32)
+
+
+def flat(parts):
+    return [x for part in parts for x in (part if isinstance(part, tuple) else (part,))]
+
+
+def like(parts, refs):
+    return [tuple(refs.pop(0) for _ in part) if isinstance(part, tuple) else refs.pop(0) for part in parts]
+
+
+def project_kernel(where, *refs, slots, forms):
     refs = list(refs)
-    parts = [[refs.pop(0) for _ in range(n)] for n in counts]
+    parts = [like(form, refs) for form in forms]
     mods_ref, wk_ref, wv_ref, wq_ref, kv_ref, q_ref = refs
     depth, width = wk_ref.shape
     hidden = []
     for i, slot in enumerate(slots):
-        rows_f = jnp.concatenate([part[...].astype(jnp.float32) for part in parts[i]])
-        section = LAST if slot is None else where[0] ^ slot
+        rows_f = jnp.concatenate(list(arrived(where[0], parts[i])))
+        section = LAST if slot is None else source_of(where[0], slot)
         row = mods_ref[pl.ds(section, 1), :]
         hidden.append(modulate(rows_f, row[:, depth:], row[:, :depth]))
     hidden = jnp.concatenate(hidden)
@@ -232,11 +260,12 @@
 
 
 def project(where, slots, parts, mods, weights):
-    args = [p for rows in parts for p in rows]
+    args = [p for rows in parts for p in flat(rows)]
     depth, width = weights[0].shape
-    rows = sum(p.shape[0] for p in args)
+    rows = 2 * args[0].shape[0] * len(slots)
+    forms = [[tuple(None for _ in p) if isinstance(p, tuple) else None for p in rows] for rows in parts]
     return pl.pallas_call(
-        functools.partial(project_kernel, slots=slots, counts=[len(p) for p in parts]),
+        functools.partial(project_kernel, slots=slots, forms=forms),
         out_shape=(
             jax.ShapeDtypeStruct((rows, 2 * width), jnp.bfloat16),
             jax.ShapeDtypeStruct((rows, width), jnp.bfloat16),
@@ -262,8 +291,8 @@
 
 
 def key_place(section, slot):
-    source = section ^ slot
-    swapped = jnp.where(section == LAST, 1 - source, source)
+    source = source_of(section, slot)
+    swapped = jnp.where(section == LAST - 1, 1 - source, source)
     return jnp.where(source > 1, source - 1, jnp.where(swapped == 1, 0, LAST))
 
 
@@ -274,12 +303,12 @@
 
 def set_rows(x_ref, q_ref, section, slot, parts, queries):
     half = q_ref.shape[0] // SECTIONS
-    base = pl.multiple_of((section ^ slot) * half, half)
+    base = pl.multiple_of(source_of(section, slot) * half, half)
     q_ref[pl.ds(base, half), :] = queries
     low = 0
-    for part in parts:
-        x_ref[pl.ds(pl.multiple_of(base + low, 8), part.shape[0]), :] = part[...].astype(jnp.float32)
-        low += part.shape[0]
+    for rows_f in arrived(section, parts):
+        x_ref[pl.ds(pl.multiple_of(base + low, 8), rows_f.shape[0]), :] = rows_f
+        low += rows_f.shape[0]
 
 
 def place_kernel(where, *refs, groups, swapped):
@@ -319,7 +348,7 @@
     )(where, *args)
 
 
-def begin_kernel(where, theirs_ref, late_q_ref, own_ref, across_ref, kv_in, x_in, q_in,
+def begin_kernel(where, theirs_ref, late_q_ref, direct_ref, relayed_ref, direct2_ref, relayed2_ref, kv_in, x_in, q_in,
                  kv_ref, x_ref, q_ref, top_ref, total_ref, sum_ref, *, groups):
     half = q_ref.shape[0] // SECTIONS
     span = 2 * half
@@ -327,7 +356,7 @@
     section = where[0]
     for i, slot in enumerate(groups[1]):
         set_keys(kv_ref, section, slot, half, theirs_ref[i * half : (i + 1) * half, :])
-    set_rows(x_ref, q_ref, section, groups[2][0], (own_ref, across_ref), late_q_ref[...])
+    set_rows(x_ref, q_ref, section, LATE, [(direct_ref, relayed_ref), (direct2_ref, relayed2_ref)], late_q_ref[...])
     jobs = []
     for s in range(1, SECTIONS):
         rows, seen = slice((s - 1) * half, s * half), slice(0, s * span)
@@ -349,15 +378,15 @@
     return pl.pallas_call(
         functools.partial(begin_kernel, groups=groups),
         out_shape=(*same, *state_shapes(LAST * half, width)),
-        in_specs=[SMEM] + [VMEM] * 7,
+        in_specs=[SMEM] + [VMEM] * 9,
         out_specs=(VMEM,) * 6,
-        input_output_aliases={5: 0, 6: 1, 7: 2},
+        input_output_aliases={7: 0, 8: 1, 9: 2},
         compiler_params=pltpu.CompilerParams(vmem_limit_bytes=12 << 20),
         cost_estimate=pl.CostEstimate(
             flops=24 * half * 2 * half * width, bytes_accessed=2 << 20, transcendentals=0
         ),
         name="begin_first",
-    )(where, theirs, late_q, *late_parts, *placed)[1:]
+    )(where, theirs, late_q, *flat(late_parts), *placed)[1:]
 
 
 def finish_kernel(where, steps, *refs, groups):
@@ -380,9 +409,9 @@
                 late_ref[0:half, :] = kv_mine[g][rows, :]
                 late_ref[half:, :] = kv_theirs[g][rows, :]
 
-    for s in range(LAST):
+    for s in range(LAST - 1):
         pl.when(section == s)(functools.partial(set_late, s))
-    pl.when(section == LAST)(functools.partial(set_late, LAST ^ 1))
+    pl.when(section >= LAST - 1)(functools.partial(set_late, LATE))
 
     everything = slice(None)
 
@@ -583,25 +612,17 @@
     per_section = lax.axis_size("tok") // SECTIONS
     where = (lax.axis_index("tok") // per_section).astype(jnp.int32).reshape(1)
 
-    def needs(section, source):
-        return source <= section + 1
-
-    def from_section(block, slot):
+    def between(block, pairs):
+        target = dict(pairs)
+
         def move(i):
             section, within = i // per_section, i % per_section
-            target = section ^ slot
-            return target * per_section + within if needs(target, section) else None
+            return target[section] * per_section + within if section in target else None
 
         return permuted(block, "tok", move)
 
-    def chip_swap(block, slot):
-        def move(i):
-            section = i // per_section
-            if slot is None:
-                return i ^ CORES if section == LAST else None
-            return i ^ CORES if needs(section, section ^ slot) else None
-
-        return permuted(block, "tok", move)
+    def chip_swap(block, sections):
+        return permuted(block, "tok", lambda i: i ^ CORES if i // per_section in sections else None)
 
     def core_swap(block):
         return permuted(block, "tok", lambda i: i ^ 1)
@@ -617,12 +638,21 @@
     )
     weights = (w_key, w_value, w_query)
 
-    groups = ((0, None), (1, 3), (2,))
-    own = {0: latents, None: fresh_noise}
-    for slot in (3, 1, 2):
-        own[slot] = from_section(latents, slot)
-    parts = {slot: [own[slot], chip_swap(own[slot], slot)] for slot in (0, None, 3)}
-    parts[1] = [own[1], from_section(parts[0][1], 1)]
+    groups = ((OWN, None), (NEXT, EARLY), (LATE,))
+    neighbours = [(s, s ^ 1) for s in range(SECTIONS)]
+    early_in = between(latents, [(0, 2), (1, 3), (2, 1)])
+    own_across = chip_swap(latents, range(SECTIONS))
+    next_in = between(latents, neighbours)
+    direct = between(latents, [(LAST - 2, LAST - 1)])
+    fresh_across = chip_swap(fresh_noise, (LAST,))
+    next_across = between(own_across, neighbours)
+    relayed = between(early_in, [(LAST - 1, LAST)])
+    parts = {
+        OWN: [latents, own_across],
+        None: [fresh_noise, fresh_across],
+        NEXT: [next_in, next_across],
+        EARLY: [early_in, chip_swap(early_in, range(1, SECTIONS))],
+    }
     mine, theirs, q = {}, {}, {}
 
     def work(group):
@@ -630,15 +660,18 @@
         theirs[group] = core_swap(mine[group])
 
     work(groups[0])
-    own[2] = after(own[2], own[3], mine[groups[0]])
-    parts[2] = [own[2], chip_swap(own[2], 2)]
+    direct = after(direct, early_in, mine[groups[0]])
+    relayed = after(relayed, direct)
+    direct_across = chip_swap(direct, (LAST - 1,))
+    relayed_across = chip_swap(relayed, (LAST,))
     work(groups[1])
     early = groups[:-1]
     placed = place(
         where, early, [mine[g] for g in early], [theirs[groups[0]]], [q[g] for g in early],
         [parts[x] for g in early for x in g if x is not None],
     )
-    parts[2][1] = after(parts[2][1], *placed)
+    relayed_across = after(relayed_across, *placed)
+    parts[LATE] = [(direct, relayed), (direct_across, relayed_across)]
     work(groups[2])
     all_mine, all_theirs = [mine[g] for g in groups], [theirs[g] for g in groups]
     begun = begin_first(

time: 63.6 us -> 60.6 us (0.953)
  the two profiles are of different devices: /device:TPU:25 before, /device:TPU:27 now
where the time goes in v4:
time: 60.6 us; the launch traced here: 60.4 us
  Pallas kernels  25 us (41%)
  starting transfers between devices  20.9 us (34%)
  waiting for transfers between devices  11.9 us (20%)
  other arithmetic  1.6 us (3%)
  between operations  0.96 us (2%)
    ppermute x14, starting transfers between devices, permuted(): return lax.ppermute(block, axis, route)  20.9 us
    ppermute x14, waiting for transfers between devices, permuted(): return lax.ppermute(block, axis, route)  11.9 us
    pallas_call x1, Pallas kernels, finish_first(): pl.pallas_call(functools.partial(finish_kernel, groups=groups), out_shape...  7 us
    pallas_call x3, Pallas kernels, project(): pl.pallas_call(functools.partial(project_kernel, slots=slots, forms=forms...  6.36 us
    pallas_call x1, Pallas kernels, fetch(): pl.pallas_call(functools.partial(fetch_kernel, count=len(arrays)), out_sh...  4.3 us
    pallas_call x1, Pallas kernels, begin_first(): pl.pallas_call(functools.partial(begin_kernel, groups=groups), out_shape=...  3.14 us
    pallas_call x1, Pallas kernels, finish_second(): pl.pallas_call(finish_second_kernel, out_shape=(pair, pair), in_specs=[SM...  2.71 us
  transfers between devices with their start and end apart: 14, of which 6 were waited for; matrix products, arithmetic and copies ran while one was open for 3% of the time, Pallas kernels for 25%

profile of v4, /device:TPU:27, one launch (start us, length us, event | category | flops | bytes accessed | tf_op | source)
XLA Modules:
  0.0 60.4 jit_solution(13154153255489333680)
XLA Ops:
  0.6 1.3 %collective-permute-start.4 = (bf16[72,1536]{1,0:T(8,128)(2,1)}, bf16[72,1536]{1,0:T(8,128)(2,1)S(1)}, u32[]{:S(2)}, u32[]{:S(2)}) collective-permute-start(bf16[72,1536]{1,0:T(8,128)(2,1)} %refs_5_.3), channel_id=1, source_target_pairs={{0,8},{1,9},{2,10},{3,11},{4,12},{5,13},{6,14},{7,15},{8,4},{9,5},... | collective-permute-start | bytes 663560 | tf_op jit(solution)/shard_map/ppermute | solution.py:22
  1.9 1.3 %collective-permute-start = (bf16[72,1536]{1,0:T(8,128)(2,1)}, bf16[72,1536]{1,0:T(8,128)(2,1)S(1)}, u32[]{:S(2)}, u32[]{:S(2)}) collective-permute-start(bf16[72,1536]{1,0:T(8,128)(2,1)} %refs_5_.3), channel_id=1, source_target_pairs={{0,2},{1,3},{2,0},{3,1},{4,6},{5,7},{6,4},{7,5},{8,10},{9,11},{10,... | collective-permute-start | bytes 663560 | tf_op jit(solution)/shard_map/ppermute | solution.py:22
  3.2 2.1 %collective-permute-start.1 = (bf16[72,1536]{1,0:T(8,128)(2,1)}, bf16[72,1536]{1,0:T(8,128)(2,1)S(1)}, u32[]{:S(2)}, u32[]{:S(2)}) collective-permute-start(bf16[72,1536]{1,0:T(8,128)(2,1)} %fresh_ref.1), channel_id=1, source_target_pairs={{12,14},{13,15},{14,12},{15,13},{28,30},{29,31},{30,28},{31,29}} | collective-permute-start | bytes 663560 | tf_op jit(solution)/shard_map/ppermute | solution.py:22
  5.4 0.7 %convert_element_type.6 = f32[4]{0:T(128)S(1)} convert(s32[4]{0:T(128)} %param.10) | non-fusion elementwise | flops 4 | bytes 32 | tf_op jit(solution)/shard_map/convert_element_type | solution.py:27
  6.1 0.1 multiply_cosine_fusion
  6.2 0.8 %fusion.1.steps = f32[4]{0:T(128)S(1)} fusion(s32[4]{0:T(128)} %param.10, s32[3]{0:T(128)} %bitcast.2, s32[1]{0:T(128)} %constant.28.clone.1), kind=kLoop, calls=%fused_computation.5 | loop fusion | flops 16 | bytes 48 | tf_op jit(solution)/shard_map/div | solution.py:41
  7.0 4.3 %fetch.1 = (bf16[1536,768]{1,0:T(8,128)(2,1)S(1)}, bf16[1536,768]{1,0:T(8,128)(2,1)S(1)}, bf16[1536,768]{1,0:T(8,128)(2,1)S(1)}, bf16[768,1536]{1,0:T(8,128)(2,1)S(1)}, f32[4,3072]{1,0:T(4,128)S(1)}) custom-call(bf16[1536,768]{1,0:T(8,128)(2,1)} %refs_0_.2, bf16[1536,768]{1,0:T(8,128)(2,1)} %refs_1_.1, bf16[1536,768]{1,0:T(8,128)(2,1)} %refs_2_.2, ...), custom_call_target="tpu_custom_call" | custom-call | bytes 9437184 | tf_op jit(solution)/shard_map/fetch/pallas_call | solution.py:199
  11.3 1.9 %collective-permute-done.1.refs_3_ = bf16[72,1536]{1,0:T(8,128)(2,1)S(1)} collective-permute-done((bf16[72,1536]{1,0:T(8,128)(2,1)}, bf16[72,1536]{1,0:T(8,128)(2,1)S(1)}, u32[]{:S(2)}, u32[]{:S(2)}) %collective-permute-start.1) | collective-permute-done | bytes 221216 | tf_op jit(solution)/shard_map/ppermute | solution.py:22
  13.3 2.5 %project.3 = (bf16[288,1536]{1,0:T(8,128)(2,1)S(1)}, bf16[288,768]{1,0:T(8,128)(2,1)S(1)}) custom-call(s32[1]{0:T(128)} %bitcast.where, bf16[72,1536]{1,0:T(8,128)(2,1)S(1)} %copy-done, bf16[72,1536]{1,0:T(8,128)(2,1)S(1)} %collective-permute-done.refs_1_.refs_6_, bf16[72,1536]{1,0:T(8,128)(2,1)S(1)} %copy-done.1, ...), custom_call_target="tpu_custom_call" | custom-call | flops 2038431744 | bytes 2097152 | tf_op jit(solution)/shard_map/project/pallas_call | solution.py:267
  15.8 1.6 %collective-permute-start.10 = (bf16[288,1536]{1,0:T(8,128)(2,1)S(1)}, bf16[288,1536]{1,0:T(8,128)(2,1)S(1)}, u32[]{:S(2)}, u32[]{:S(2)}) collective-permute-start(bf16[288,1536]{1,0:T(8,128)(2,1)S(1)} %get-tuple-element.41.refs_0_.fresh_mine_ref), channel_id=1, source_target_pairs={{0,1},{1,0},{2,3},{3,2},{4,5},{5,4},{6,7},{7,6},{8,9},{9,8},{10,11... | collective-permute-start | bytes 2654216 | tf_op jit(solution)/shard_map/ppermute | solution.py:22
  17.4 3.1 %collective-permute-start.5 = (bf16[72,1536]{1,0:T(8,128)(2,1)S(1)}, bf16[72,1536]{1,0:T(8,128)(2,1)S(1)}, u32[]{:S(2)}, u32[]{:S(2)}) collective-permute-start(bf16[72,1536]{1,0:T(8,128)(2,1)S(1)} %collective-permute-done.4.refs_2_.refs_9_), channel_id=1, source_target_pairs={{4,6},{5,7},{6,4},{7,5},{8,10},{9,11},{10,8},{11,9},{12,14},{13,15... | collective-permute-start | bytes 663560 | tf_op jit(solution)/shard_map/ppermute | solution.py:22
  20.5 1.5 %collective-permute-start.3 = (bf16[72,1536]{1,0:T(8,128)(2,1)S(1)}, bf16[72,1536]{1,0:T(8,128)(2,1)S(1)}, u32[]{:S(2)}, u32[]{:S(2)}) collective-permute-start(bf16[72,1536]{1,0:T(8,128)(2,1)S(1)} %collective-permute-done.refs_1_.refs_6_), channel_id=1, source_target_pairs={{0,4},{1,5},{2,6},{3,7},{4,0},{5,1},{6,2},{7,3},{8,12},{9,13},{10,... | collective-permute-start | bytes 663560 | tf_op jit(solution)/shard_map/ppermute | solution.py:22
  22.0 0.7 %collective-permute-start.6 = (bf16[72,1536]{1,0:T(8,128)(2,1)S(1)}, bf16[72,1536]{1,0:T(8,128)(2,1)S(1)}, u32[]{:S(2)}, u32[]{:S(2)}) collective-permute-start(bf16[72,1536]{1,0:T(8,128)(2,1)S(1)} %copy-done), channel_id=1, source_target_pairs={{4,8},{5,9},{6,10},{7,11},{20,24},{21,25},{22,26},{23,27}} | collective-permute-start | bytes 663560 | tf_op jit(solution)/shard_map/ppermute | solution.py:22
  22.7 1.6 %collective-permute-done.2.refs_0_.refs_7_ = bf16[72,1536]{1,0:T(8,128)(2,1)S(1)} collective-permute-done((bf16[72,1536]{1,0:T(8,128)(2,1)S(1)}, bf16[72,1536]{1,0:T(8,128)(2,1)S(1)}, u32[]{:S(2)}, u32[]{:S(2)}) %collective-permute-start.2) | collective-permute-done | bytes 221216 | tf_op jit(solution)/shard_map/ppermute | solution.py:22
  24.3 1.3 %collective-permute-start.7 = (bf16[72,1536]{1,0:T(8,128)(2,1)S(1)}, bf16[72,1536]{1,0:T(8,128)(2,1)S(1)}, u32[]{:S(2)}, u32[]{:S(2)}) collective-permute-start(bf16[72,1536]{1,0:T(8,128)(2,1)S(1)} %collective-permute-done.4.refs_2_.refs_9_), channel_id=1, source_target_pairs={{8,12},{9,13},{10,14},{11,15},{24,28},{25,29},{26,30},{27,31}} | collective-permute-start | bytes 663560 | tf_op jit(solution)/shard_map/ppermute | solution.py:22
  25.5 0.6 collective-permute-done.5.refs_3_.refs_10_
  26.1 2.9 %collective-permute-done.3.refs_1_.refs_8_ = bf16[72,1536]{1,0:T(8,128)(2,1)S(1)} collective-permute-done((bf16[72,1536]{1,0:T(8,128)(2,1)S(1)}, bf16[72,1536]{1,0:T(8,128)(2,1)S(1)}, u32[]{:S(2)}, u32[]{:S(2)}) %collective-permute-start.3) | collective-permute-done | bytes 221216 | tf_op jit(solution)/shard_map/ppermute | solution.py:22
  29.0 2.5 %project.4 = (bf16[288,1536]{1,0:T(8,128)(2,1)S(1)}, bf16[288,768]{1,0:T(8,128)(2,1)S(1)}) custom-call(s32[1]{0:T(128)} %bitcast.where, bf16[72,1536]{1,0:T(8,128)(2,1)S(1)} %collective-permute-done.2.refs_0_.refs_7_, bf16[72,1536]{1,0:T(8,128)(2,1)S(1)} %collective-permute-done.3.refs_1_.refs_8_, ...), custom_call_target="tpu_custom_call" | custom-call | flops 2038431744 | bytes 2097152 | tf_op jit(solution)/shard_map/project/pallas_call | solution.py:267
  31.5 1.5 %collective-permute-start.11 = (bf16[288,1536]{1,0:T(8,128)(2,1)S(1)}, bf16[288,1536]{1,0:T(8,128)(2,1)S(1)}, u32[]{:S(2)}, u32[]{:S(2)}) collective-permute-start(bf16[288,1536]{1,0:T(8,128)(2,1)S(1)} %get-tuple-element.42.refs_1_), channel_id=1, source_target_pairs={{0,1},{1,0},{2,3},{3,2},{4,5},{5,4},{6,7},{7,6},{8,9},{9,8},{10,11... | collective-permute-start | bytes 2654216 | tf_op jit(solution)/shard_map/ppermute | solution.py:22
  33.0 0.0 collective-permute-done.7.refs_1_.relayed_ref
  33.0 3.1 %collective-permute-start.9 = (bf16[72,1536]{1,0:T(8,128)(2,1)S(1)}, bf16[72,1536]{1,0:T(8,128)(2,1)S(1)}, u32[]{:S(2)}, u32[]{:S(2)}) collective-permute-start(bf16[72,1536]{1,0:T(8,128)(2,1)S(1)} %collective-permute-done.7.refs_1_.relayed_ref), channel_id=1, source_target_pairs={{12,14},{13,15},{14,12},{15,13},{28,30},{29,31},{30,28},{31,29}} | collective-permute-start | bytes 663560 | tf_op jit(solution)/shard_map/ppermute | solution.py:22
  36.2 0.7 %collective-permute-start.8 = (bf16[72,1536]{1,0:T(8,128)(2,1)S(1)}, bf16[72,1536]{1,0:T(8,128)(2,1)S(1)}, u32[]{:S(2)}, u32[]{:S(2)}) collective-permute-start(bf16[72,1536]{1,0:T(8,128)(2,1)S(1)} %collective-permute-done.6.refs_0_.direct_ref), channel_id=1, source_target_pairs={{8,10},{9,11},{10,8},{11,9},{24,26},{25,27},{26,24},{27,25}} | collective-permute-start | bytes 663560 | tf_op jit(solution)/shard_map/ppermute | solution.py:22
  36.9 0.3 place.1
  37.2 3.0 %collective-permute-done.9.refs_3_.relayed2_ref = bf16[72,1536]{1,0:T(8,128)(2,1)S(1)} collective-permute-done((bf16[72,1536]{1,0:T(8,128)(2,1)S(1)}, bf16[72,1536]{1,0:T(8,128)(2,1)S(1)}, u32[]{:S(2)}, u32[]{:S(2)}) %collective-permute-start.9) | collective-permute-done | bytes 221216 | tf_op jit(solution)/shard_map/ppermute | solution.py:22
  40.3 1.4 %project.5 = (bf16[144,1536]{1,0:T(8,128)(2,1)S(1)}, bf16[144,768]{1,0:T(8,128)(2,1)S(1)}) custom-call(s32[1]{0:T(128)} %bitcast.where, bf16[72,1536]{1,0:T(8,128)(2,1)S(1)} %collective-permute-done.6.refs_0_.direct_ref, bf16[72,1536]{1,0:T(8,128)(2,1)S(1)} %collective-permute-done.7.refs_1_.relayed_ref, ...), custom_call_target="tpu_custom_call" | custom-call | flops 1019215872 | bytes 2097152 | tf_op jit(solution)/shard_map/project/pallas_call | solution.py:267
  41.7 2.6 %collective-permute-start.12 = (bf16[144,1536]{1,0:T(8,128)(2,1)S(1)}, bf16[144,1536]{1,0:T(8,128)(2,1)S(1)}, u32[]{:S(2)}, u32[]{:S(2)}) collective-permute-start(bf16[144,1536]{1,0:T(8,128)(2,1)S(1)} %get-tuple-element.51.refs_2_), channel_id=1, source_target_pairs={{0,1},{1,0},{2,3},{3,2},{4,5},{5,4},{6,7},{7,6},{8,9},{9,8},{10,11... | collective-permute-start | bytes 1327112 | tf_op jit(solution)/shard_map/ppermute | solution.py:22
  44.2 3.1 %begin_first.1 = (bf16[1152,1536]{1,0:T(8,128)(2,1)S(1)}, f32[576,1536]{1,0:T(8,128)S(1)}, bf16[576,768]{1,0:T(8,128)(2,1)S(1)}, f32[6,432,128]{2,1,0:T(8,128)S(...) custom-call(s32[1]{0:T(128)} %bitcast.where, ...), custom_call_target="tpu_custom_call", output_to_operand_aliasing={{0}: (7, {}), {1}: (8, {}), {2}: (9, {})} | custom-call | flops 764411904 | bytes 2097152 | tf_op jit(solution)/shard_map/begin_first/pallas_call | solution.py:378
  47.4 7.0 %finish_first.1 = (bf16[2,72,1536]{2,1,0:T(8,128)(2,1)}, bf16[2,72,1536]{2,1,0:T(8,128)(2,1)}, bf16[432,1536]{1,0:T(8,128)(2,1)S(1)}, bf16[72,1536]{1,0:T(8,128)(2,1)S(1)}, bf16[72,1536]{1,0:T(8,128)(2,1)S(1)}) custom-call(s32[1]{0:T(128)} %bitcast.where, f32[4]{0:T(128)S(1)} %fusion.1.steps, bf16[288,1536]{1,0:T(8,128)(2,1)S(1)} %get-tuple-element.41.refs_0_.fresh_mine_ref, ...), custom_call_target="tpu_custom_call" | custom-call | flops 4076863488 | bytes 4194304 | tf_op jit(solution)/shard_map/finish_first/pallas_call | solution.py:475
  54.4 0.1 collective-permute-start.13
  54.5 1.1 %begin_second.1 = (bf16[72,768]{1,0:T(8,128)(2,1)S(1)}, f32[6,72,128]{2,1,0:T(8,128)S(1)}, f32[6,72,128]{2,1,0:T(8,128)S(1)}, f32[72,768]{1,0:T(8,128)S(1)}) custom-call(s32[1]{0:T(128)} %bitcast.where, bf16[72,1536]{1,0:T(8,128)(2,1)S(1)} %get-tuple-element.59.own_ref, bf16[1536,768]{1,0:T(8,128)(2,1)S(1)} %get-tuple-element.40.refs_7_.wq_ref, ...), custom_call_target="tpu_custom_call" | custom-call | flops 339738624 | bytes 2097152 | tf_op jit(solution)/shard_map/begin_second/pallas_call | solution.py:532
  55.6 1.9 %collective-permute-done.13.theirs_ref = bf16[432,1536]{1,0:T(8,128)(2,1)S(1)} collective-permute-done((bf16[432,1536]{1,0:T(8,128)(2,1)S(1)}, bf16[432,1536]{1,0:T(8,128)(2,1)S(1)}, u32[]{:S(2)}, u32[]{:S(2)}) %collective-permute-start.13) | collective-permute-done | bytes 1327136 | tf_op jit(solution)/shard_map/ppermute | solution.py:22
  57.5 2.7 %finish_second.1 = (bf16[2,72,1536]{2,1,0:T(8,128)(2,1)}, bf16[2,72,1536]{2,1,0:T(8,128)(2,1)}) custom-call(s32[1]{0:T(128)} %bitcast.where, f32[4]{0:T(128)S(1)} %fusion.1.steps, bf16[72,768]{1,0:T(8,128)(2,1)S(1)} %get-tuple-element.61.q_ref, f32[6,72,128]{2,1,0:T(8,128)S(1)} %get-tuple-element.62.top_ref, ...), custom_call_target="tpu_custom_call", output_to_operand_aliasing={{0}: (10, {}), {1}: (11, {})} | custom-call | flops 339738624 | bytes 4194304 | tf_op jit(solution)/shard_map/finish_second/pallas_call | solution.py:591
  (14 shorter events, 0.0 us)
Async XLA Ops:
  0.6 16.7 %collective-permute-start.4 = (bf16[72,1536]{1,0:T(8,128)(2,1)}, bf16[72,1536]{1,0:T(8,128)(2,1)S(1)}, u32[]{:S(2)}, u32[]{:S(2)}) collective-permute-start(bf16[72,1536]{1,0:T(8,128)(2,1)} %refs_5_.3), channel_id=1, source_target_pairs={{0,8},{1,9},{2,10},{3,11},{4,12},{5,13},{6,14},{7,15},{8,4},{9,5},... | collective-permute-start | bytes 663560 | tf_op jit(solution)/shard_map/ppermute | solution.py:22
  1.9 9.4 %collective-permute-start = (bf16[72,1536]{1,0:T(8,128)(2,1)}, bf16[72,1536]{1,0:T(8,128)(2,1)S(1)}, u32[]{:S(2)}, u32[]{:S(2)}) collective-permute-start(bf16[72,1536]{1,0:T(8,128)(2,1)} %refs_5_.3), channel_id=1, source_target_pairs={{0,2},{1,3},{2,0},{3,1},{4,6},{5,7},{6,4},{7,5},{8,10},{9,11},{10,... | collective-permute-start | bytes 663560 | tf_op jit(solution)/shard_map/ppermute | solution.py:22
  3.2 10.0 %collective-permute-start.1 = (bf16[72,1536]{1,0:T(8,128)(2,1)}, bf16[72,1536]{1,0:T(8,128)(2,1)S(1)}, u32[]{:S(2)}, u32[]{:S(2)}) collective-permute-start(bf16[72,1536]{1,0:T(8,128)(2,1)} %fresh_ref.1), channel_id=1, source_target_pairs={{12,14},{13,15},{14,12},{15,13},{28,30},{29,31},{30,28},{31,29}} | collective-permute-start | bytes 663560 | tf_op jit(solution)/shard_map/ppermute | solution.py:22
  7.0 6.3 %copy-start = (bf16[72,1536]{1,0:T(8,128)(2,1)S(1)}, bf16[72,1536]{1,0:T(8,128)(2,1)}, u32[]{:S(2)}) copy-start(bf16[72,1536]{1,0:T(8,128)(2,1)} %refs_5_.3) | copy-start | bytes 663556
  7.0 6.3 %copy-start.1 = (bf16[72,1536]{1,0:T(8,128)(2,1)S(1)}, bf16[72,1536]{1,0:T(8,128)(2,1)}, u32[]{:S(2)}) copy-start(bf16[72,1536]{1,0:T(8,128)(2,1)} %fresh_ref.1) | copy-start | bytes 663556
  15.8 21.1 %collective-permute-start.10 = (bf16[288,1536]{1,0:T(8,128)(2,1)S(1)}, bf16[288,1536]{1,0:T(8,128)(2,1)S(1)}, u32[]{:S(2)}, u32[]{:S(2)}) collective-permute-start(bf16[288,1536]{1,0:T(8,128)(2,1)S(1)} %get-tuple-element.41.refs_0_.fresh_mine_ref), channel_id=1, source_target_pairs={{0,1},{1,0},{2,3},{3,2},{4,5},{5,4},{6,7},{7,6},{8,9},{9,8},{10,11... | collective-permute-start | bytes 2654216 | tf_op jit(solution)/shard_map/ppermute | solution.py:22
  17.3 6.9 %collective-permute-start.2 = (bf16[72,1536]{1,0:T(8,128)(2,1)S(1)}, bf16[72,1536]{1,0:T(8,128)(2,1)S(1)}, u32[]{:S(2)}, u32[]{:S(2)}) collective-permute-start(bf16[72,1536]{1,0:T(8,128)(2,1)S(1)} %copy-done), channel_id=1, source_target_pairs={{0,4},{1,5},{2,6},{3,7},{4,0},{5,1},{6,2},{7,3},{8,12},{9,13},{10,... | collective-permute-start | bytes 663560 | tf_op jit(solution)/shard_map/ppermute | solution.py:22
  17.4 8.8 %collective-permute-start.5 = (bf16[72,1536]{1,0:T(8,128)(2,1)S(1)}, bf16[72,1536]{1,0:T(8,128)(2,1)S(1)}, u32[]{:S(2)}, u32[]{:S(2)}) collective-permute-start(bf16[72,1536]{1,0:T(8,128)(2,1)S(1)} %collective-permute-done.4.refs_2_.refs_9_), channel_id=1, source_target_pairs={{4,6},{5,7},{6,4},{7,5},{8,10},{9,11},{10,8},{11,9},{12,14},{13,15... | collective-permute-start | bytes 663560 | tf_op jit(solution)/shard_map/ppermute | solution.py:22
  20.5 8.5 %collective-permute-start.3 = (bf16[72,1536]{1,0:T(8,128)(2,1)S(1)}, bf16[72,1536]{1,0:T(8,128)(2,1)S(1)}, u32[]{:S(2)}, u32[]{:S(2)}) collective-permute-start(bf16[72,1536]{1,0:T(8,128)(2,1)S(1)} %collective-permute-done.refs_1_.refs_6_), channel_id=1, source_target_pairs={{0,4},{1,5},{2,6},{3,7},{4,0},{5,1},{6,2},{7,3},{8,12},{9,13},{10,... | collective-permute-start | bytes 663560 | tf_op jit(solution)/shard_map/ppermute | solution.py:22
  22.0 11.0 %collective-permute-start.6 = (bf16[72,1536]{1,0:T(8,128)(2,1)S(1)}, bf16[72,1536]{1,0:T(8,128)(2,1)S(1)}, u32[]{:S(2)}, u32[]{:S(2)}) collective-permute-start(bf16[72,1536]{1,0:T(8,128)(2,1)S(1)} %copy-done), channel_id=1, source_target_pairs={{4,8},{5,9},{6,10},{7,11},{20,24},{21,25},{22,26},{23,27}} | collective-permute-start | bytes 663560 | tf_op jit(solution)/shard_map/ppermute | solution.py:22
  24.3 8.8 %collective-permute-start.7 = (bf16[72,1536]{1,0:T(8,128)(2,1)S(1)}, bf16[72,1536]{1,0:T(8,128)(2,1)S(1)}, u32[]{:S(2)}, u32[]{:S(2)}) collective-permute-start(bf16[72,1536]{1,0:T(8,128)(2,1)S(1)} %collective-permute-done.4.refs_2_.refs_9_), channel_id=1, source_target_pairs={{8,12},{9,13},{10,14},{11,15},{24,28},{25,29},{26,30},{27,31}} | collective-permute-start | bytes 663560 | tf_op jit(solution)/shard_map/ppermute | solution.py:22
  31.5 12.8 %collective-permute-start.11 = (bf16[288,1536]{1,0:T(8,128)(2,1)S(1)}, bf16[288,1536]{1,0:T(8,128)(2,1)S(1)}, u32[]{:S(2)}, u32[]{:S(2)}) collective-permute-start(bf16[288,1536]{1,0:T(8,128)(2,1)S(1)} %get-tuple-element.42.refs_1_), channel_id=1, source_target_pairs={{0,1},{1,0},{2,3},{3,2},{4,5},{5,4},{6,7},{7,6},{8,9},{9,8},{10,11... | collective-permute-start | bytes 2654216 | tf_op jit(solution)/shard_map/ppermute | solution.py:22
  33.0 7.2 %collective-permute-start.9 = (bf16[72,1536]{1,0:T(8,128)(2,1)S(1)}, bf16[72,1536]{1,0:T(8,128)(2,1)S(1)}, u32[]{:S(2)}, u32[]{:S(2)}) collective-permute-start(bf16[72,1536]{1,0:T(8,128)(2,1)S(1)} %collective-permute-done.7.refs_1_.relayed_ref), channel_id=1, source_target_pairs={{12,14},{13,15},{14,12},{15,13},{28,30},{29,31},{30,28},{31,29}} | collective-permute-start | bytes 663560 | tf_op jit(solution)/shard_map/ppermute | solution.py:22
  36.2 4.1 %collective-permute-start.8 = (bf16[72,1536]{1,0:T(8,128)(2,1)S(1)}, bf16[72,1536]{1,0:T(8,128)(2,1)S(1)}, u32[]{:S(2)}, u32[]{:S(2)}) collective-permute-start(bf16[72,1536]{1,0:T(8,128)(2,1)S(1)} %collective-permute-done.6.refs_0_.direct_ref), channel_id=1, source_target_pairs={{8,10},{9,11},{10,8},{11,9},{24,26},{25,27},{26,24},{27,25}} | collective-permute-start | bytes 663560 | tf_op jit(solution)/shard_map/ppermute | solution.py:22
  41.7 5.7 %collective-permute-start.12 = (bf16[144,1536]{1,0:T(8,128)(2,1)S(1)}, bf16[144,1536]{1,0:T(8,128)(2,1)S(1)}, u32[]{:S(2)}, u32[]{:S(2)}) collective-permute-start(bf16[144,1536]{1,0:T(8,128)(2,1)S(1)} %get-tuple-element.51.refs_2_), channel_id=1, source_target_pairs={{0,1},{1,0},{2,3},{3,2},{4,5},{5,4},{6,7},{7,6},{8,9},{9,8},{10,11... | collective-permute-start | bytes 1327112 | tf_op jit(solution)/shard_map/ppermute | solution.py:22
  54.4 3.1 %collective-permute-start.13 = (bf16[432,1536]{1,0:T(8,128)(2,1)S(1)}, bf16[432,1536]{1,0:T(8,128)(2,1)S(1)}, u32[]{:S(2)}, u32[]{:S(2)}) collective-permute-start(bf16[432,1536]{1,0:T(8,128)(2,1)S(1)} %get-tuple-element.60.mine_ref), channel_id=1, source_target_pairs={{0,1},{1,0},{2,3},{3,2},{4,5},{5,4},{6,7},{7,6},{8,9},{9,8},{10,11... | collective-permute-start | bytes 3981320 | tf_op jit(solution)/shard_map/ppermute | solution.py:22

commit v5 on v3

--- a/solution.py
+++ b/solution.py
@@ -594,14 +594,8 @@
 
         return permuted(block, "tok", move)
 
-    def chip_swap(block, slot):
-        def move(i):
-            section = i // per_section
-            if slot is None:
-                return i ^ CORES if section == LAST else None
-            return i ^ CORES if needs(section, section ^ slot) else None
-
-        return permuted(block, "tok", move)
+    def chip_swap(block):
+        return permuted(block, "tok", lambda i: i ^ CORES)
 
     def core_swap(block):
         return permuted(block, "tok", lambda i: i ^ 1)
@@ -621,7 +615,7 @@
     own = {0: latents, None: fresh_noise}
     for slot in (3, 1, 2):
         own[slot] = from_section(latents, slot)
-    parts = {slot: [own[slot], chip_swap(own[slot], slot)] for slot in (0, None, 3)}
+    parts = {slot: [own[slot], chip_swap(own[slot])] for slot in (0, None, 3)}
     parts[1] = [own[1], from_section(parts[0][1], 1)]
     mine, theirs, q = {}, {}, {}
 
@@ -631,7 +625,7 @@
 
     work(groups[0])
     own[2] = after(own[2], own[3], mine[groups[0]])
-    parts[2] = [own[2], chip_swap(own[2], 2)]
+    parts[2] = [own[2], chip_swap(own[2])]
     work(groups[1])
     early = groups[:-1]
     placed = place(

time: 63.6 us -> 63.7 us (level)
  the two profiles are of different devices: /device:TPU:25 before, /device:TPU:0 now
where the time goes in v5:
time: 63.7 us; the launch traced here: 63.5 us
  Pallas kernels  25.6 us (40%)
  waiting for transfers between devices  19 us (30%)
  starting transfers between devices  16.4 us (26%)
  other arithmetic  1.6 us (3%)
  between operations  0.94 us (1%)
    ppermute x12, waiting for transfers between devices, permuted(): return lax.ppermute(block, axis, route)  19 us
    ppermute x12, starting transfers between devices, permuted(): return lax.ppermute(block, axis, route)  16.4 us
    pallas_call x1, Pallas kernels, finish_first(): pl.pallas_call(functools.partial(finish_kernel, groups=groups), out_shape...  8.09 us
    pallas_call x3, Pallas kernels, project(): pl.pallas_call(functools.partial(project_kernel, slots=slots, counts=[len...  6.3 us
    pallas_call x1, Pallas kernels, fetch(): pl.pallas_call(functools.partial(fetch_kernel, count=len(arrays)), out_sh...  4.3 us
    pallas_call x1, Pallas kernels, begin_first(): pl.pallas_call(functools.partial(begin_kernel, groups=groups), out_shape=...  3.1 us
    pallas_call x1, Pallas kernels, finish_second(): pl.pallas_call(finish_second_kernel, out_shape=(pair, pair), in_specs=[SM...  2.41 us
  transfers between devices with their start and end apart: 12, of which 6 were waited for; matrix products, arithmetic and copies ran while one was open for 3% of the time, Pallas kernels for 24%

profile of v5, /device:TPU:0, one launch (start us, length us, event | category | flops | bytes accessed | tf_op | source)
XLA Modules:
  0.0 63.5 jit_solution(12819065097175527950)
XLA Ops:
  0.6 7.0 %collective-permute-start.4 = (bf16[72,1536]{1,0:T(8,128)(2,1)}, bf16[72,1536]{1,0:T(8,128)(2,1)S(1)}, u32[]{:S(2)}, u32[]{:S(2)}) collective-permute-start(bf16[72,1536]{1,0:T(8,128)(2,1)} %refs_5_.3), channel_id=1, source_target_pairs={{0,12},{1,13},{2,14},{3,15},{4,8},{5,9},{6,10},{7,11},{8,4},{9,5},... | collective-permute-start | bytes 663560 | tf_op jit(solution)/shard_map/ppermute | solution.py:22
  7.6 1.6 %collective-permute-start = (bf16[72,1536]{1,0:T(8,128)(2,1)}, bf16[72,1536]{1,0:T(8,128)(2,1)S(1)}, u32[]{:S(2)}, u32[]{:S(2)}) collective-permute-start(bf16[72,1536]{1,0:T(8,128)(2,1)} %refs_5_.3), channel_id=1, source_target_pairs={{0,2},{1,3},{2,0},{3,1},{4,6},{5,7},{6,4},{7,5},{8,10},{9,11},{10,... | collective-permute-start | bytes 663560 | tf_op jit(solution)/shard_map/ppermute | solution.py:22
  9.2 0.5 collective-permute-start.1
  9.7 0.7 %convert_element_type.6 = f32[4]{0:T(128)S(1)} convert(s32[4]{0:T(128)} %param.10) | non-fusion elementwise | flops 4 | bytes 32 | tf_op jit(solution)/shard_map/convert_element_type | solution.py:27
  10.4 0.1 multiply_cosine_fusion
  10.5 0.8 %fusion.1.steps = f32[4]{0:T(128)S(1)} fusion(s32[4]{0:T(128)} %param.10, s32[3]{0:T(128)} %bitcast.2, s32[1]{0:T(128)} %constant.28.clone.1), kind=kLoop, calls=%fused_computation.5 | loop fusion | flops 16 | bytes 48 | tf_op jit(solution)/shard_map/div | solution.py:41
  11.3 4.3 %fetch.1 = (bf16[1536,768]{1,0:T(8,128)(2,1)S(1)}, bf16[1536,768]{1,0:T(8,128)(2,1)S(1)}, bf16[1536,768]{1,0:T(8,128)(2,1)S(1)}, bf16[768,1536]{1,0:T(8,128)(2,1)S(1)}, f32[4,3072]{1,0:T(4,128)S(1)}) custom-call(bf16[1536,768]{1,0:T(8,128)(2,1)} %refs_0_.2, bf16[1536,768]{1,0:T(8,128)(2,1)} %refs_1_.1, bf16[1536,768]{1,0:T(8,128)(2,1)} %refs_2_.2, ...), custom_call_target="tpu_custom_call" | custom-call | bytes 9437184 | tf_op jit(solution)/shard_map/fetch/pallas_call | solution.py:199
  15.6 0.6 collective-permute-done.refs_1_.refs_6_
  16.2 3.3 %collective-permute-done.1.refs_3_ = bf16[72,1536]{1,0:T(8,128)(2,1)S(1)} collective-permute-done((bf16[72,1536]{1,0:T(8,128)(2,1)}, bf16[72,1536]{1,0:T(8,128)(2,1)S(1)}, u32[]{:S(2)}, u32[]{:S(2)}) %collective-permute-start.1) | collective-permute-done | bytes 221216 | tf_op jit(solution)/shard_map/ppermute | solution.py:22
  19.5 2.5 %project.3 = (bf16[288,1536]{1,0:T(8,128)(2,1)S(1)}, bf16[288,768]{1,0:T(8,128)(2,1)S(1)}) custom-call(s32[1]{0:T(128)} %bitcast.where, bf16[72,1536]{1,0:T(8,128)(2,1)S(1)} %copy-done, bf16[72,1536]{1,0:T(8,128)(2,1)S(1)} %collective-permute-done.refs_1_.refs_6_, bf16[72,1536]{1,0:T(8,128)(2,1)S(1)} %copy-done.1, ...), custom_call_target="tpu_custom_call" | custom-call | flops 2038431744 | bytes 2097152 | tf_op jit(solution)/shard_map/project/pallas_call | solution.py:238
  22.0 0.1 collective-permute-start.8
  22.1 0.1 collective-permute-start.2
  22.2 1.6 %collective-permute-start.5 = (bf16[72,1536]{1,0:T(8,128)(2,1)S(1)}, bf16[72,1536]{1,0:T(8,128)(2,1)S(1)}, u32[]{:S(2)}, u32[]{:S(2)}) collective-permute-start(bf16[72,1536]{1,0:T(8,128)(2,1)S(1)} %collective-permute-done.4.refs_2_.refs_9_), channel_id=1, source_target_pairs={{0,2},{1,3},{2,0},{3,1},{4,6},{5,7},{6,4},{7,5},{8,10},{9,11},{10,... | collective-permute-start | bytes 663560 | tf_op jit(solution)/shard_map/ppermute | solution.py:22
  23.8 1.9 %collective-permute-start.3 = (bf16[72,1536]{1,0:T(8,128)(2,1)S(1)}, bf16[72,1536]{1,0:T(8,128)(2,1)S(1)}, u32[]{:S(2)}, u32[]{:S(2)}) collective-permute-start(bf16[72,1536]{1,0:T(8,128)(2,1)S(1)} %collective-permute-done.refs_1_.refs_6_), channel_id=1, source_target_pairs={{0,4},{1,5},{2,6},{3,7},{4,0},{5,1},{6,2},{7,3},{8,12},{9,13},{10,... | collective-permute-start | bytes 663560 | tf_op jit(solution)/shard_map/ppermute | solution.py:22
  25.7 1.3 %collective-permute-start.6 = (bf16[72,1536]{1,0:T(8,128)(2,1)S(1)}, bf16[72,1536]{1,0:T(8,128)(2,1)S(1)}, u32[]{:S(2)}, u32[]{:S(2)}) collective-permute-start(bf16[72,1536]{1,0:T(8,128)(2,1)S(1)} %copy-done), channel_id=1, source_target_pairs={{0,8},{1,9},{2,10},{3,11},{4,12},{5,13},{6,14},{7,15},{16,24},{17,... | collective-permute-start | bytes 663560 | tf_op jit(solution)/shard_map/ppermute | solution.py:22
  27.1 3.4 %collective-permute-done.2.refs_0_.refs_7_ = bf16[72,1536]{1,0:T(8,128)(2,1)S(1)} collective-permute-done((bf16[72,1536]{1,0:T(8,128)(2,1)S(1)}, bf16[72,1536]{1,0:T(8,128)(2,1)S(1)}, u32[]{:S(2)}, u32[]{:S(2)}) %collective-permute-start.2) | collective-permute-done | bytes 221216 | tf_op jit(solution)/shard_map/ppermute | solution.py:22
  30.5 0.0 collective-permute-done.5.refs_3_.refs_10_
  30.5 4.2 %collective-permute-done.3.refs_1_.refs_8_ = bf16[72,1536]{1,0:T(8,128)(2,1)S(1)} collective-permute-done((bf16[72,1536]{1,0:T(8,128)(2,1)S(1)}, bf16[72,1536]{1,0:T(8,128)(2,1)S(1)}, u32[]{:S(2)}, u32[]{:S(2)}) %collective-permute-start.3) | collective-permute-done | bytes 221216 | tf_op jit(solution)/shard_map/ppermute | solution.py:22
  34.7 2.5 %project.4 = (bf16[288,1536]{1,0:T(8,128)(2,1)S(1)}, bf16[288,768]{1,0:T(8,128)(2,1)S(1)}) custom-call(s32[1]{0:T(128)} %bitcast.where, bf16[72,1536]{1,0:T(8,128)(2,1)S(1)} %collective-permute-done.2.refs_0_.refs_7_, bf16[72,1536]{1,0:T(8,128)(2,1)S(1)} %collective-permute-done.3.refs_1_.refs_8_, ...), custom_call_target="tpu_custom_call" | custom-call | flops 2038431744 | bytes 2097152 | tf_op jit(solution)/shard_map/project/pallas_call | solution.py:238
  37.2 0.1 collective-permute-start.9
  37.2 0.0 collective-permute-done.6.refs_0_.own_ref
  37.3 1.6 %collective-permute-start.7 = (bf16[72,1536]{1,0:T(8,128)(2,1)S(1)}, bf16[72,1536]{1,0:T(8,128)(2,1)S(1)}, u32[]{:S(2)}, u32[]{:S(2)}) collective-permute-start(bf16[72,1536]{1,0:T(8,128)(2,1)S(1)} %collective-permute-done.6.refs_0_.own_ref), channel_id=1, source_target_pairs={{0,2},{1,3},{2,0},{3,1},{4,6},{5,7},{6,4},{7,5},{8,10},{9,11},{10,... | collective-permute-start | bytes 663560 | tf_op jit(solution)/shard_map/ppermute | solution.py:22
  38.8 0.3 place.1
  39.2 5.9 %collective-permute-done.7.refs_1_.across_ref = bf16[72,1536]{1,0:T(8,128)(2,1)S(1)} collective-permute-done((bf16[72,1536]{1,0:T(8,128)(2,1)S(1)}, bf16[72,1536]{1,0:T(8,128)(2,1)S(1)}, u32[]{:S(2)}, u32[]{:S(2)}) %collective-permute-start.7) | collective-permute-done | bytes 221216 | tf_op jit(solution)/shard_map/ppermute | solution.py:22
  45.1 1.3 %project.5 = (bf16[144,1536]{1,0:T(8,128)(2,1)S(1)}, bf16[144,768]{1,0:T(8,128)(2,1)S(1)}) custom-call(s32[1]{0:T(128)} %bitcast.where, bf16[72,1536]{1,0:T(8,128)(2,1)S(1)} %collective-permute-done.6.refs_0_.own_ref, bf16[72,1536]{1,0:T(8,128)(2,1)S(1)} %collective-permute-done.7.refs_1_.across_ref, ...), custom_call_target="tpu_custom_call" | custom-call | flops 1019215872 | bytes 2097152 | tf_op jit(solution)/shard_map/project/pallas_call | solution.py:238
  46.4 0.1 collective-permute-start.10
  46.5 3.1 %begin_first.1 = (bf16[1152,1536]{1,0:T(8,128)(2,1)S(1)}, f32[576,1536]{1,0:T(8,128)S(1)}, bf16[576,768]{1,0:T(8,128)(2,1)S(1)}, f32[6,432,128]{2,1,0:T(8,128)S(...) custom-call(s32[1]{0:T(128)} %bitcast.where, ...), custom_call_target="tpu_custom_call", output_to_operand_aliasing={{0}: (5, {}), {1}: (6, {}), {2}: (7, {})} | custom-call | flops 764411904 | bytes 2097152 | tf_op jit(solution)/shard_map/begin_first/pallas_call | solution.py:349
  49.6 8.1 %finish_first.1 = (bf16[2,72,1536]{2,1,0:T(8,128)(2,1)}, bf16[2,72,1536]{2,1,0:T(8,128)(2,1)}, bf16[432,1536]{1,0:T(8,128)(2,1)S(1)}, bf16[72,1536]{1,0:T(8,128)(2,1)S(1)}, bf16[72,1536]{1,0:T(8,128)(2,1)S(1)}) custom-call(s32[1]{0:T(128)} %bitcast.where, f32[4]{0:T(128)S(1)} %fusion.1.steps, bf16[288,1536]{1,0:T(8,128)(2,1)S(1)} %get-tuple-element.40.refs_0_.fresh_mine_ref, ...), custom_call_target="tpu_custom_call" | custom-call | flops 4076863488 | bytes 4194304 | tf_op jit(solution)/shard_map/finish_first/pallas_call | solution.py:446
  57.7 0.5 collective-permute-start.11
  58.3 1.1 %begin_second.1 = (bf16[72,768]{1,0:T(8,128)(2,1)S(1)}, f32[6,72,128]{2,1,0:T(8,128)S(1)}, f32[6,72,128]{2,1,0:T(8,128)S(1)}, f32[72,768]{1,0:T(8,128)S(1)}) custom-call(s32[1]{0:T(128)} %bitcast.where, bf16[72,1536]{1,0:T(8,128)(2,1)S(1)} %get-tuple-element.57.own_ref, bf16[1536,768]{1,0:T(8,128)(2,1)S(1)} %get-tuple-element.39.refs_7_.refs_5_.wq_ref, ...), custom_call_target="tpu_custom_call" | custom-call | flops 339738624 | bytes 2097152 | tf_op jit(solution)/shard_map/begin_second/pallas_call | solution.py:503
  59.3 1.6 %collective-permute-done.11.theirs_ref = bf16[432,1536]{1,0:T(8,128)(2,1)S(1)} collective-permute-done((bf16[432,1536]{1,0:T(8,128)(2,1)S(1)}, bf16[432,1536]{1,0:T(8,128)(2,1)S(1)}, u32[]{:S(2)}, u32[]{:S(2)}) %collective-permute-start.11) | collective-permute-done | bytes 1327136 | tf_op jit(solution)/shard_map/ppermute | solution.py:22
  61.0 2.4 %finish_second.1 = (bf16[2,72,1536]{2,1,0:T(8,128)(2,1)}, bf16[2,72,1536]{2,1,0:T(8,128)(2,1)}) custom-call(s32[1]{0:T(128)} %bitcast.where, f32[4]{0:T(128)S(1)} %fusion.1.steps, bf16[72,768]{1,0:T(8,128)(2,1)S(1)} %get-tuple-element.59.q_ref, f32[6,72,128]{2,1,0:T(8,128)S(1)} %get-tuple-element.60.top_ref, ...), custom_call_target="tpu_custom_call", output_to_operand_aliasing={{0}: (10, {}), {1}: (11, {})} | custom-call | flops 339738624 | bytes 4194304 | tf_op jit(solution)/shard_map/finish_second/pallas_call | solution.py:562
  (10 shorter events, 0.0 us)
Async XLA Ops:
  0.6 21.6 %collective-permute-start.4 = (bf16[72,1536]{1,0:T(8,128)(2,1)}, bf16[72,1536]{1,0:T(8,128)(2,1)S(1)}, u32[]{:S(2)}, u32[]{:S(2)}) collective-permute-start(bf16[72,1536]{1,0:T(8,128)(2,1)} %refs_5_.3), channel_id=1, source_target_pairs={{0,12},{1,13},{2,14},{3,15},{4,8},{5,9},{6,10},{7,11},{8,4},{9,5},... | collective-permute-start | bytes 663560 | tf_op jit(solution)/shard_map/ppermute | solution.py:22
  7.6 8.6 %collective-permute-start = (bf16[72,1536]{1,0:T(8,128)(2,1)}, bf16[72,1536]{1,0:T(8,128)(2,1)S(1)}, u32[]{:S(2)}, u32[]{:S(2)}) collective-permute-start(bf16[72,1536]{1,0:T(8,128)(2,1)} %refs_5_.3), channel_id=1, source_target_pairs={{0,2},{1,3},{2,0},{3,1},{4,6},{5,7},{6,4},{7,5},{8,10},{9,11},{10,... | collective-permute-start | bytes 663560 | tf_op jit(solution)/shard_map/ppermute | solution.py:22
  9.2 10.3 %collective-permute-start.1 = (bf16[72,1536]{1,0:T(8,128)(2,1)}, bf16[72,1536]{1,0:T(8,128)(2,1)S(1)}, u32[]{:S(2)}, u32[]{:S(2)}) collective-permute-start(bf16[72,1536]{1,0:T(8,128)(2,1)} %fresh_ref.1), channel_id=1, source_target_pairs={{0,2},{1,3},{2,0},{3,1},{4,6},{5,7},{6,4},{7,5},{8,10},{9,11},{10,... | collective-permute-start | bytes 663560 | tf_op jit(solution)/shard_map/ppermute | solution.py:22
  11.3 8.2 %copy-start = (bf16[72,1536]{1,0:T(8,128)(2,1)S(1)}, bf16[72,1536]{1,0:T(8,128)(2,1)}, u32[]{:S(2)}) copy-start(bf16[72,1536]{1,0:T(8,128)(2,1)} %refs_5_.3) | copy-start | bytes 663556
  11.3 8.2 %copy-start.1 = (bf16[72,1536]{1,0:T(8,128)(2,1)S(1)}, bf16[72,1536]{1,0:T(8,128)(2,1)}, u32[]{:S(2)}) copy-start(bf16[72,1536]{1,0:T(8,128)(2,1)} %fresh_ref.1) | copy-start | bytes 663556
  22.0 16.8 %collective-permute-start.8 = (bf16[288,1536]{1,0:T(8,128)(2,1)S(1)}, bf16[288,1536]{1,0:T(8,128)(2,1)S(1)}, u32[]{:S(2)}, u32[]{:S(2)}) collective-permute-start(bf16[288,1536]{1,0:T(8,128)(2,1)S(1)} %get-tuple-element.40.refs_0_.fresh_mine_ref), channel_id=1, source_target_pairs={{0,1},{1,0},{2,3},{3,2},{4,5},{5,4},{6,7},{7,6},{8,9},{9,8},{10,11... | collective-permute-start | bytes 2654216 | tf_op jit(solution)/shard_map/ppermute | solution.py:22
  22.1 8.4 %collective-permute-start.2 = (bf16[72,1536]{1,0:T(8,128)(2,1)S(1)}, bf16[72,1536]{1,0:T(8,128)(2,1)S(1)}, u32[]{:S(2)}, u32[]{:S(2)}) collective-permute-start(bf16[72,1536]{1,0:T(8,128)(2,1)S(1)} %copy-done), channel_id=1, source_target_pairs={{0,4},{1,5},{2,6},{3,7},{4,0},{5,1},{6,2},{7,3},{8,12},{9,13},{10,... | collective-permute-start | bytes 663560 | tf_op jit(solution)/shard_map/ppermute | solution.py:22
  22.2 8.3 %collective-permute-start.5 = (bf16[72,1536]{1,0:T(8,128)(2,1)S(1)}, bf16[72,1536]{1,0:T(8,128)(2,1)S(1)}, u32[]{:S(2)}, u32[]{:S(2)}) collective-permute-start(bf16[72,1536]{1,0:T(8,128)(2,1)S(1)} %collective-permute-done.4.refs_2_.refs_9_), channel_id=1, source_target_pairs={{0,2},{1,3},{2,0},{3,1},{4,6},{5,7},{6,4},{7,5},{8,10},{9,11},{10,... | collective-permute-start | bytes 663560 | tf_op jit(solution)/shard_map/ppermute | solution.py:22
  23.8 10.9 %collective-permute-start.3 = (bf16[72,1536]{1,0:T(8,128)(2,1)S(1)}, bf16[72,1536]{1,0:T(8,128)(2,1)S(1)}, u32[]{:S(2)}, u32[]{:S(2)}) collective-permute-start(bf16[72,1536]{1,0:T(8,128)(2,1)S(1)} %collective-permute-done.refs_1_.refs_6_), channel_id=1, source_target_pairs={{0,4},{1,5},{2,6},{3,7},{4,0},{5,1},{6,2},{7,3},{8,12},{9,13},{10,... | collective-permute-start | bytes 663560 | tf_op jit(solution)/shard_map/ppermute | solution.py:22
  25.7 11.5 %collective-permute-start.6 = (bf16[72,1536]{1,0:T(8,128)(2,1)S(1)}, bf16[72,1536]{1,0:T(8,128)(2,1)S(1)}, u32[]{:S(2)}, u32[]{:S(2)}) collective-permute-start(bf16[72,1536]{1,0:T(8,128)(2,1)S(1)} %copy-done), channel_id=1, source_target_pairs={{0,8},{1,9},{2,10},{3,11},{4,12},{5,13},{6,14},{7,15},{16,24},{17,... | collective-permute-start | bytes 663560 | tf_op jit(solution)/shard_map/ppermute | solution.py:22
  37.2 9.4 %collective-permute-start.9 = (bf16[288,1536]{1,0:T(8,128)(2,1)S(1)}, bf16[288,1536]{1,0:T(8,128)(2,1)S(1)}, u32[]{:S(2)}, u32[]{:S(2)}) collective-permute-start(bf16[288,1536]{1,0:T(8,128)(2,1)S(1)} %get-tuple-element.41.refs_1_), channel_id=1, source_target_pairs={{0,1},{1,0},{2,3},{3,2},{4,5},{5,4},{6,7},{7,6},{8,9},{9,8},{10,11... | collective-permute-start | bytes 2654216 | tf_op jit(solution)/shard_map/ppermute | solution.py:22
  37.3 7.8 %collective-permute-start.7 = (bf16[72,1536]{1,0:T(8,128)(2,1)S(1)}, bf16[72,1536]{1,0:T(8,128)(2,1)S(1)}, u32[]{:S(2)}, u32[]{:S(2)}) collective-permute-start(bf16[72,1536]{1,0:T(8,128)(2,1)S(1)} %collective-permute-done.6.refs_0_.own_ref), channel_id=1, source_target_pairs={{0,2},{1,3},{2,0},{3,1},{4,6},{5,7},{6,4},{7,5},{8,10},{9,11},{10,... | collective-permute-start | bytes 663560 | tf_op jit(solution)/shard_map/ppermute | solution.py:22
  46.4 3.2 %collective-permute-start.10 = (bf16[144,1536]{1,0:T(8,128)(2,1)S(1)}, bf16[144,1536]{1,0:T(8,128)(2,1)S(1)}, u32[]{:S(2)}, u32[]{:S(2)}) collective-permute-start(bf16[144,1536]{1,0:T(8,128)(2,1)S(1)} %get-tuple-element.49.refs_2_), channel_id=1, source_target_pairs={{0,1},{1,0},{2,3},{3,2},{4,5},{5,4},{6,7},{7,6},{8,9},{9,8},{10,11... | collective-permute-start | bytes 1327112 | tf_op jit(solution)/shard_map/ppermute | solution.py:22
  57.7 3.2 %collective-permute-start.11 = (bf16[432,1536]{1,0:T(8,128)(2,1)S(1)}, bf16[432,1536]{1,0:T(8,128)(2,1)S(1)}, u32[]{:S(2)}, u32[]{:S(2)}) collective-permute-start(bf16[432,1536]{1,0:T(8,128)(2,1)S(1)} %get-tuple-element.58.mine_ref), channel_id=1, source_target_pairs={{0,1},{1,0},{2,3},{3,2},{4,5},{5,4},{6,7},{7,6},{8,9},{9,8},{10,11... | collective-permute-start | bytes 3981320 | tf_op jit(solution)/shard_map/ppermute | solution.py:22

commit v6 on v3

--- a/solution.py
+++ b/solution.py
@@ -597,9 +597,8 @@
     def chip_swap(block, slot):
         def move(i):
             section = i // per_section
-            if slot is None:
-                return i ^ CORES if section == LAST else None
-            return i ^ CORES if needs(section, section ^ slot) else None
+            needed = section == LAST if slot is None else needs(section, section ^ slot)
+            return i ^ CORES if needed else i
 
         return permuted(block, "tok", move)
 

time: 63.6 us -> 63.2 us (level)
  the two profiles are of different devices: /device:TPU:25 before, /device:TPU:27 now
where the time goes in v6:
time: 63.2 us; the launch traced here: 63 us
  Pallas kernels  24.9 us (39%)
  starting transfers between devices  18.4 us (29%)
  waiting for transfers between devices  17.1 us (27%)
  other arithmetic  1.6 us (3%)
  between operations  0.94 us (1%)
    ppermute x12, starting transfers between devices, permuted(): return lax.ppermute(block, axis, route)  18.4 us
    ppermute x12, waiting for transfers between devices, permuted(): return lax.ppermute(block, axis, route)  17.1 us
    pallas_call x1, Pallas kernels, finish_first(): pl.pallas_call(functools.partial(finish_kernel, groups=groups), out_shape...  6.98 us
    pallas_call x3, Pallas kernels, project(): pl.pallas_call(functools.partial(project_kernel, slots=slots, counts=[len...  6.31 us
    pallas_call x1, Pallas kernels, fetch(): pl.pallas_call(functools.partial(fetch_kernel, count=len(arrays)), out_sh...  4.3 us
    pallas_call x1, Pallas kernels, begin_first(): pl.pallas_call(functools.partial(begin_kernel, groups=groups), out_shape=...  3.09 us
    pallas_call x1, Pallas kernels, finish_second(): pl.pallas_call(finish_second_kernel, out_shape=(pair, pair), in_specs=[SM...  2.71 us
  transfers between devices with their start and end apart: 12, of which 7 were waited for; matrix products, arithmetic and copies ran while one was open for 3% of the time, Pallas kernels for 24%

profile of v6, /device:TPU:27, one launch (start us, length us, event | category | flops | bytes accessed | tf_op | source)
XLA Modules:
  0.0 63.0 jit_solution(2545909344121977718)
XLA Ops:
  0.6 1.3 %collective-permute-start.4 = (bf16[72,1536]{1,0:T(8,128)(2,1)}, bf16[72,1536]{1,0:T(8,128)(2,1)S(1)}, u32[]{:S(2)}, u32[]{:S(2)}) collective-permute-start(bf16[72,1536]{1,0:T(8,128)(2,1)} %refs_5_.3), channel_id=1, source_target_pairs={{0,12},{1,13},{2,14},{3,15},{4,8},{5,9},{6,10},{7,11},{8,4},{9,5},... | collective-permute-start | bytes 663560 | tf_op jit(solution)/shard_map/ppermute | solution.py:22
  1.9 1.3 %collective-permute-start = (bf16[72,1536]{1,0:T(8,128)(2,1)}, bf16[72,1536]{1,0:T(8,128)(2,1)S(1)}, u32[]{:S(2)}, u32[]{:S(2)}) collective-permute-start(bf16[72,1536]{1,0:T(8,128)(2,1)} %refs_5_.3), channel_id=1, source_target_pairs={{0,2},{1,3},{2,0},{3,1},{4,6},{5,7},{6,4},{7,5},{8,10},{9,11},{10,... | collective-permute-start | bytes 663560 | tf_op jit(solution)/shard_map/ppermute | solution.py:22
  3.2 2.1 %collective-permute-start.1 = (bf16[72,1536]{1,0:T(8,128)(2,1)}, bf16[72,1536]{1,0:T(8,128)(2,1)S(1)}, u32[]{:S(2)}, u32[]{:S(2)}) collective-permute-start(bf16[72,1536]{1,0:T(8,128)(2,1)} %fresh_ref.1), channel_id=1, source_target_pairs={{0,0},{1,1},{2,2},{3,3},{4,4},{5,5},{6,6},{7,7},{8,8},{9,9},{10,10... | collective-permute-start | bytes 663560 | tf_op jit(solution)/shard_map/ppermute | solution.py:22
  5.4 0.7 %convert_element_type.6 = f32[4]{0:T(128)S(1)} convert(s32[4]{0:T(128)} %param.10) | non-fusion elementwise | flops 4 | bytes 32 | tf_op jit(solution)/shard_map/convert_element_type | solution.py:27
  6.1 0.1 multiply_cosine_fusion
  6.2 0.8 %fusion.1.steps = f32[4]{0:T(128)S(1)} fusion(s32[4]{0:T(128)} %param.10, s32[3]{0:T(128)} %bitcast.2, s32[1]{0:T(128)} %constant.28.clone.1), kind=kLoop, calls=%fused_computation.5 | loop fusion | flops 16 | bytes 48 | tf_op jit(solution)/shard_map/div | solution.py:41
  7.0 4.3 %fetch.1 = (bf16[1536,768]{1,0:T(8,128)(2,1)S(1)}, bf16[1536,768]{1,0:T(8,128)(2,1)S(1)}, bf16[1536,768]{1,0:T(8,128)(2,1)S(1)}, bf16[768,1536]{1,0:T(8,128)(2,1)S(1)}, f32[4,3072]{1,0:T(4,128)S(1)}) custom-call(bf16[1536,768]{1,0:T(8,128)(2,1)} %refs_0_.2, bf16[1536,768]{1,0:T(8,128)(2,1)} %refs_1_.1, bf16[1536,768]{1,0:T(8,128)(2,1)} %refs_2_.2, ...), custom_call_target="tpu_custom_call" | custom-call | bytes 9437184 | tf_op jit(solution)/shard_map/fetch/pallas_call | solution.py:199
  11.3 1.9 %collective-permute-done.1.refs_3_ = bf16[72,1536]{1,0:T(8,128)(2,1)S(1)} collective-permute-done((bf16[72,1536]{1,0:T(8,128)(2,1)}, bf16[72,1536]{1,0:T(8,128)(2,1)S(1)}, u32[]{:S(2)}, u32[]{:S(2)}) %collective-permute-start.1) | collective-permute-done | bytes 221216 | tf_op jit(solution)/shard_map/ppermute | solution.py:22
  13.3 2.5 %project.3 = (bf16[288,1536]{1,0:T(8,128)(2,1)S(1)}, bf16[288,768]{1,0:T(8,128)(2,1)S(1)}) custom-call(s32[1]{0:T(128)} %bitcast.where, bf16[72,1536]{1,0:T(8,128)(2,1)S(1)} %copy-done, bf16[72,1536]{1,0:T(8,128)(2,1)S(1)} %collective-permute-done.refs_1_.refs_6_, bf16[72,1536]{1,0:T(8,128)(2,1)S(1)} %copy-done.1, ...), custom_call_target="tpu_custom_call" | custom-call | flops 2038431744 | bytes 2097152 | tf_op jit(solution)/shard_map/project/pallas_call | solution.py:238
  15.8 1.6 %collective-permute-start.8 = (bf16[288,1536]{1,0:T(8,128)(2,1)S(1)}, bf16[288,1536]{1,0:T(8,128)(2,1)S(1)}, u32[]{:S(2)}, u32[]{:S(2)}) collective-permute-start(bf16[288,1536]{1,0:T(8,128)(2,1)S(1)} %get-tuple-element.40.refs_0_.fresh_mine_ref), channel_id=1, source_target_pairs={{0,1},{1,0},{2,3},{3,2},{4,5},{5,4},{6,7},{7,6},{8,9},{9,8},{10,11... | collective-permute-start | bytes 2654216 | tf_op jit(solution)/shard_map/ppermute | solution.py:22
  17.4 3.1 %collective-permute-start.5 = (bf16[72,1536]{1,0:T(8,128)(2,1)S(1)}, bf16[72,1536]{1,0:T(8,128)(2,1)S(1)}, u32[]{:S(2)}, u32[]{:S(2)}) collective-permute-start(bf16[72,1536]{1,0:T(8,128)(2,1)S(1)} %collective-permute-done.4.refs_2_.refs_9_), channel_id=1, source_target_pairs={{0,0},{1,1},{2,2},{3,3},{4,6},{5,7},{6,4},{7,5},{8,10},{9,11},{10,... | collective-permute-start | bytes 663560 | tf_op jit(solution)/shard_map/ppermute | solution.py:22
  20.5 1.5 %collective-permute-start.3 = (bf16[72,1536]{1,0:T(8,128)(2,1)S(1)}, bf16[72,1536]{1,0:T(8,128)(2,1)S(1)}, u32[]{:S(2)}, u32[]{:S(2)}) collective-permute-start(bf16[72,1536]{1,0:T(8,128)(2,1)S(1)} %collective-permute-done.refs_1_.refs_6_), channel_id=1, source_target_pairs={{0,4},{1,5},{2,6},{3,7},{4,0},{5,1},{6,2},{7,3},{8,12},{9,13},{10,... | collective-permute-start | bytes 663560 | tf_op jit(solution)/shard_map/ppermute | solution.py:22
  22.0 1.3 %collective-permute-start.6 = (bf16[72,1536]{1,0:T(8,128)(2,1)S(1)}, bf16[72,1536]{1,0:T(8,128)(2,1)S(1)}, u32[]{:S(2)}, u32[]{:S(2)}) collective-permute-start(bf16[72,1536]{1,0:T(8,128)(2,1)S(1)} %copy-done), channel_id=1, source_target_pairs={{0,8},{1,9},{2,10},{3,11},{4,12},{5,13},{6,14},{7,15},{16,24},{17,... | collective-permute-start | bytes 663560 | tf_op jit(solution)/shard_map/ppermute | solution.py:22
  23.3 0.9 %collective-permute-done.2.refs_0_.refs_7_ = bf16[72,1536]{1,0:T(8,128)(2,1)S(1)} collective-permute-done((bf16[72,1536]{1,0:T(8,128)(2,1)S(1)}, bf16[72,1536]{1,0:T(8,128)(2,1)S(1)}, u32[]{:S(2)}, u32[]{:S(2)}) %collective-permute-start.2) | collective-permute-done | bytes 221216 | tf_op jit(solution)/shard_map/ppermute | solution.py:22
  24.3 1.9 %collective-permute-done.5.refs_3_.refs_10_ = bf16[72,1536]{1,0:T(8,128)(2,1)S(1)} collective-permute-done((bf16[72,1536]{1,0:T(8,128)(2,1)S(1)}, bf16[72,1536]{1,0:T(8,128)(2,1)S(1)}, u32[]{:S(2)}, u32[]{:S(2)}) %collective-permute-start.5) | collective-permute-done | bytes 221216 | tf_op jit(solution)/shard_map/ppermute | solution.py:22
  26.1 4.6 %collective-permute-done.3.refs_1_.refs_8_ = bf16[72,1536]{1,0:T(8,128)(2,1)S(1)} collective-permute-done((bf16[72,1536]{1,0:T(8,128)(2,1)S(1)}, bf16[72,1536]{1,0:T(8,128)(2,1)S(1)}, u32[]{:S(2)}, u32[]{:S(2)}) %collective-permute-start.3) | collective-permute-done | bytes 221216 | tf_op jit(solution)/shard_map/ppermute | solution.py:22
  30.7 2.5 %project.4 = (bf16[288,1536]{1,0:T(8,128)(2,1)S(1)}, bf16[288,768]{1,0:T(8,128)(2,1)S(1)}) custom-call(s32[1]{0:T(128)} %bitcast.where, bf16[72,1536]{1,0:T(8,128)(2,1)S(1)} %collective-permute-done.2.refs_0_.refs_7_, bf16[72,1536]{1,0:T(8,128)(2,1)S(1)} %collective-permute-done.3.refs_1_.refs_8_, ...), custom_call_target="tpu_custom_call" | custom-call | flops 2038431744 | bytes 2097152 | tf_op jit(solution)/shard_map/project/pallas_call | solution.py:238
  33.2 1.0 %collective-permute-start.9 = (bf16[288,1536]{1,0:T(8,128)(2,1)S(1)}, bf16[288,1536]{1,0:T(8,128)(2,1)S(1)}, u32[]{:S(2)}, u32[]{:S(2)}) collective-permute-start(bf16[288,1536]{1,0:T(8,128)(2,1)S(1)} %get-tuple-element.41.refs_1_), channel_id=1, source_target_pairs={{0,1},{1,0},{2,3},{3,2},{4,5},{5,4},{6,7},{7,6},{8,9},{9,8},{10,11... | collective-permute-start | bytes 2654216 | tf_op jit(solution)/shard_map/ppermute | solution.py:22
  34.2 1.5 %collective-permute-done.6.refs_0_.own_ref = bf16[72,1536]{1,0:T(8,128)(2,1)S(1)} collective-permute-done((bf16[72,1536]{1,0:T(8,128)(2,1)S(1)}, bf16[72,1536]{1,0:T(8,128)(2,1)S(1)}, u32[]{:S(2)}, u32[]{:S(2)}) %collective-permute-start.6) | collective-permute-done | bytes 221216 | tf_op jit(solution)/shard_map/ppermute | solution.py:22
  35.7 2.4 %collective-permute-start.7 = (bf16[72,1536]{1,0:T(8,128)(2,1)S(1)}, bf16[72,1536]{1,0:T(8,128)(2,1)S(1)}, u32[]{:S(2)}, u32[]{:S(2)}) collective-permute-start(bf16[72,1536]{1,0:T(8,128)(2,1)S(1)} %collective-permute-done.6.refs_0_.own_ref), channel_id=1, source_target_pairs={{0,0},{1,1},{2,2},{3,3},{4,4},{5,5},{6,6},{7,7},{8,10},{9,11},{10,... | collective-permute-start | bytes 663560 | tf_op jit(solution)/shard_map/ppermute | solution.py:22
  38.1 0.0 collective-permute-done.8.refs_2_.refs_3_.fresh_theirs_ref
  38.1 0.3 place.1
  38.5 4.4 %collective-permute-done.7.refs_1_.across_ref = bf16[72,1536]{1,0:T(8,128)(2,1)S(1)} collective-permute-done((bf16[72,1536]{1,0:T(8,128)(2,1)S(1)}, bf16[72,1536]{1,0:T(8,128)(2,1)S(1)}, u32[]{:S(2)}, u32[]{:S(2)}) %collective-permute-start.7) | collective-permute-done | bytes 221216 | tf_op jit(solution)/shard_map/ppermute | solution.py:22
  42.9 1.3 %project.5 = (bf16[144,1536]{1,0:T(8,128)(2,1)S(1)}, bf16[144,768]{1,0:T(8,128)(2,1)S(1)}) custom-call(s32[1]{0:T(128)} %bitcast.where, bf16[72,1536]{1,0:T(8,128)(2,1)S(1)} %collective-permute-done.6.refs_0_.own_ref, bf16[72,1536]{1,0:T(8,128)(2,1)S(1)} %collective-permute-done.7.refs_1_.across_ref, ...), custom_call_target="tpu_custom_call" | custom-call | flops 1019215872 | bytes 2097152 | tf_op jit(solution)/shard_map/project/pallas_call | solution.py:238
  44.2 2.6 %collective-permute-start.10 = (bf16[144,1536]{1,0:T(8,128)(2,1)S(1)}, bf16[144,1536]{1,0:T(8,128)(2,1)S(1)}, u32[]{:S(2)}, u32[]{:S(2)}) collective-permute-start(bf16[144,1536]{1,0:T(8,128)(2,1)S(1)} %get-tuple-element.49.refs_2_), channel_id=1, source_target_pairs={{0,1},{1,0},{2,3},{3,2},{4,5},{5,4},{6,7},{7,6},{8,9},{9,8},{10,11... | collective-permute-start | bytes 1327112 | tf_op jit(solution)/shard_map/ppermute | solution.py:22
  46.9 0.0 collective-permute-done.9.theirs_ref.refs_4_
  46.9 3.1 %begin_first.1 = (bf16[1152,1536]{1,0:T(8,128)(2,1)S(1)}, f32[576,1536]{1,0:T(8,128)S(1)}, bf16[576,768]{1,0:T(8,128)(2,1)S(1)}, f32[6,432,128]{2,1,0:T(8,128)S(...) custom-call(s32[1]{0:T(128)} %bitcast.where, ...), custom_call_target="tpu_custom_call", output_to_operand_aliasing={{0}: (5, {}), {1}: (6, {}), {2}: (7, {})} | custom-call | flops 764411904 | bytes 2097152 | tf_op jit(solution)/shard_map/begin_first/pallas_call | solution.py:349
  50.0 7.0 %finish_first.1 = (bf16[2,72,1536]{2,1,0:T(8,128)(2,1)}, bf16[2,72,1536]{2,1,0:T(8,128)(2,1)}, bf16[432,1536]{1,0:T(8,128)(2,1)S(1)}, bf16[72,1536]{1,0:T(8,128)(2,1)S(1)}, bf16[72,1536]{1,0:T(8,128)(2,1)S(1)}) custom-call(s32[1]{0:T(128)} %bitcast.where, f32[4]{0:T(128)S(1)} %fusion.1.steps, bf16[288,1536]{1,0:T(8,128)(2,1)S(1)} %get-tuple-element.40.refs_0_.fresh_mine_ref, ...), custom_call_target="tpu_custom_call" | custom-call | flops 4076863488 | bytes 4194304 | tf_op jit(solution)/shard_map/finish_first/pallas_call | solution.py:446
  57.0 0.1 collective-permute-start.11
  57.1 1.1 %begin_second.1 = (bf16[72,768]{1,0:T(8,128)(2,1)S(1)}, f32[6,72,128]{2,1,0:T(8,128)S(1)}, f32[6,72,128]{2,1,0:T(8,128)S(1)}, f32[72,768]{1,0:T(8,128)S(1)}) custom-call(s32[1]{0:T(128)} %bitcast.where, bf16[72,1536]{1,0:T(8,128)(2,1)S(1)} %get-tuple-element.57.own_ref, bf16[1536,768]{1,0:T(8,128)(2,1)S(1)} %get-tuple-element.39.refs_7_.refs_5_.wq_ref, ...), custom_call_target="tpu_custom_call" | custom-call | flops 339738624 | bytes 2097152 | tf_op jit(solution)/shard_map/begin_second/pallas_call | solution.py:503
  58.2 1.9 %collective-permute-done.11.theirs_ref = bf16[432,1536]{1,0:T(8,128)(2,1)S(1)} collective-permute-done((bf16[432,1536]{1,0:T(8,128)(2,1)S(1)}, bf16[432,1536]{1,0:T(8,128)(2,1)S(1)}, u32[]{:S(2)}, u32[]{:S(2)}) %collective-permute-start.11) | collective-permute-done | bytes 1327136 | tf_op jit(solution)/shard_map/ppermute | solution.py:22
  60.1 2.7 %finish_second.1 = (bf16[2,72,1536]{2,1,0:T(8,128)(2,1)}, bf16[2,72,1536]{2,1,0:T(8,128)(2,1)}) custom-call(s32[1]{0:T(128)} %bitcast.where, f32[4]{0:T(128)S(1)} %fusion.1.steps, bf16[72,768]{1,0:T(8,128)(2,1)S(1)} %get-tuple-element.59.q_ref, f32[6,72,128]{2,1,0:T(8,128)S(1)} %get-tuple-element.60.top_ref, ...), custom_call_target="tpu_custom_call", output_to_operand_aliasing={{0}: (10, {}), {1}: (11, {})} | custom-call | flops 339738624 | bytes 4194304 | tf_op jit(solution)/shard_map/finish_second/pallas_call | solution.py:562
  (10 shorter events, 0.0 us)
Async XLA Ops:
  0.6 16.7 %collective-permute-start.4 = (bf16[72,1536]{1,0:T(8,128)(2,1)}, bf16[72,1536]{1,0:T(8,128)(2,1)S(1)}, u32[]{:S(2)}, u32[]{:S(2)}) collective-permute-start(bf16[72,1536]{1,0:T(8,128)(2,1)} %refs_5_.3), channel_id=1, source_target_pairs={{0,12},{1,13},{2,14},{3,15},{4,8},{5,9},{6,10},{7,11},{8,4},{9,5},... | collective-permute-start | bytes 663560 | tf_op jit(solution)/shard_map/ppermute | solution.py:22
  1.9 9.4 %collective-permute-start = (bf16[72,1536]{1,0:T(8,128)(2,1)}, bf16[72,1536]{1,0:T(8,128)(2,1)S(1)}, u32[]{:S(2)}, u32[]{:S(2)}) collective-permute-start(bf16[72,1536]{1,0:T(8,128)(2,1)} %refs_5_.3), channel_id=1, source_target_pairs={{0,2},{1,3},{2,0},{3,1},{4,6},{5,7},{6,4},{7,5},{8,10},{9,11},{10,... | collective-permute-start | bytes 663560 | tf_op jit(solution)/shard_map/ppermute | solution.py:22
  3.2 10.0 %collective-permute-start.1 = (bf16[72,1536]{1,0:T(8,128)(2,1)}, bf16[72,1536]{1,0:T(8,128)(2,1)S(1)}, u32[]{:S(2)}, u32[]{:S(2)}) collective-permute-start(bf16[72,1536]{1,0:T(8,128)(2,1)} %fresh_ref.1), channel_id=1, source_target_pairs={{0,0},{1,1},{2,2},{3,3},{4,4},{5,5},{6,6},{7,7},{8,8},{9,9},{10,10... | collective-permute-start | bytes 663560 | tf_op jit(solution)/shard_map/ppermute | solution.py:22
  7.0 6.3 %copy-start = (bf16[72,1536]{1,0:T(8,128)(2,1)S(1)}, bf16[72,1536]{1,0:T(8,128)(2,1)}, u32[]{:S(2)}) copy-start(bf16[72,1536]{1,0:T(8,128)(2,1)} %refs_5_.3) | copy-start | bytes 663556
  7.0 6.3 %copy-start.1 = (bf16[72,1536]{1,0:T(8,128)(2,1)S(1)}, bf16[72,1536]{1,0:T(8,128)(2,1)}, u32[]{:S(2)}) copy-start(bf16[72,1536]{1,0:T(8,128)(2,1)} %fresh_ref.1) | copy-start | bytes 663556
  15.8 22.4 %collective-permute-start.8 = (bf16[288,1536]{1,0:T(8,128)(2,1)S(1)}, bf16[288,1536]{1,0:T(8,128)(2,1)S(1)}, u32[]{:S(2)}, u32[]{:S(2)}) collective-permute-start(bf16[288,1536]{1,0:T(8,128)(2,1)S(1)} %get-tuple-element.40.refs_0_.fresh_mine_ref), channel_id=1, source_target_pairs={{0,1},{1,0},{2,3},{3,2},{4,5},{5,4},{6,7},{7,6},{8,9},{9,8},{10,11... | collective-permute-start | bytes 2654216 | tf_op jit(solution)/shard_map/ppermute | solution.py:22
  17.3 6.9 %collective-permute-start.2 = (bf16[72,1536]{1,0:T(8,128)(2,1)S(1)}, bf16[72,1536]{1,0:T(8,128)(2,1)S(1)}, u32[]{:S(2)}, u32[]{:S(2)}) collective-permute-start(bf16[72,1536]{1,0:T(8,128)(2,1)S(1)} %copy-done), channel_id=1, source_target_pairs={{0,4},{1,5},{2,6},{3,7},{4,0},{5,1},{6,2},{7,3},{8,12},{9,13},{10,... | collective-permute-start | bytes 663560 | tf_op jit(solution)/shard_map/ppermute | solution.py:22
  17.4 8.8 %collective-permute-start.5 = (bf16[72,1536]{1,0:T(8,128)(2,1)S(1)}, bf16[72,1536]{1,0:T(8,128)(2,1)S(1)}, u32[]{:S(2)}, u32[]{:S(2)}) collective-permute-start(bf16[72,1536]{1,0:T(8,128)(2,1)S(1)} %collective-permute-done.4.refs_2_.refs_9_), channel_id=1, source_target_pairs={{0,0},{1,1},{2,2},{3,3},{4,6},{5,7},{6,4},{7,5},{8,10},{9,11},{10,... | collective-permute-start | bytes 663560 | tf_op jit(solution)/shard_map/ppermute | solution.py:22
  20.5 10.2 %collective-permute-start.3 = (bf16[72,1536]{1,0:T(8,128)(2,1)S(1)}, bf16[72,1536]{1,0:T(8,128)(2,1)S(1)}, u32[]{:S(2)}, u32[]{:S(2)}) collective-permute-start(bf16[72,1536]{1,0:T(8,128)(2,1)S(1)} %collective-permute-done.refs_1_.refs_6_), channel_id=1, source_target_pairs={{0,4},{1,5},{2,6},{3,7},{4,0},{5,1},{6,2},{7,3},{8,12},{9,13},{10,... | collective-permute-start | bytes 663560 | tf_op jit(solution)/shard_map/ppermute | solution.py:22
  22.0 13.7 %collective-permute-start.6 = (bf16[72,1536]{1,0:T(8,128)(2,1)S(1)}, bf16[72,1536]{1,0:T(8,128)(2,1)S(1)}, u32[]{:S(2)}, u32[]{:S(2)}) collective-permute-start(bf16[72,1536]{1,0:T(8,128)(2,1)S(1)} %copy-done), channel_id=1, source_target_pairs={{0,8},{1,9},{2,10},{3,11},{4,12},{5,13},{6,14},{7,15},{16,24},{17,... | collective-permute-start | bytes 663560 | tf_op jit(solution)/shard_map/ppermute | solution.py:22
  33.2 13.7 %collective-permute-start.9 = (bf16[288,1536]{1,0:T(8,128)(2,1)S(1)}, bf16[288,1536]{1,0:T(8,128)(2,1)S(1)}, u32[]{:S(2)}, u32[]{:S(2)}) collective-permute-start(bf16[288,1536]{1,0:T(8,128)(2,1)S(1)} %get-tuple-element.41.refs_1_), channel_id=1, source_target_pairs={{0,1},{1,0},{2,3},{3,2},{4,5},{5,4},{6,7},{7,6},{8,9},{9,8},{10,11... | collective-permute-start | bytes 2654216 | tf_op jit(solution)/shard_map/ppermute | solution.py:22
  35.7 7.1 %collective-permute-start.7 = (bf16[72,1536]{1,0:T(8,128)(2,1)S(1)}, bf16[72,1536]{1,0:T(8,128)(2,1)S(1)}, u32[]{:S(2)}, u32[]{:S(2)}) collective-permute-start(bf16[72,1536]{1,0:T(8,128)(2,1)S(1)} %collective-permute-done.6.refs_0_.own_ref), channel_id=1, source_target_pairs={{0,0},{1,1},{2,2},{3,3},{4,4},{5,5},{6,6},{7,7},{8,10},{9,11},{10,... | collective-permute-start | bytes 663560 | tf_op jit(solution)/shard_map/ppermute | solution.py:22
  44.2 5.7 %collective-permute-start.10 = (bf16[144,1536]{1,0:T(8,128)(2,1)S(1)}, bf16[144,1536]{1,0:T(8,128)(2,1)S(1)}, u32[]{:S(2)}, u32[]{:S(2)}) collective-permute-start(bf16[144,1536]{1,0:T(8,128)(2,1)S(1)} %get-tuple-element.49.refs_2_), channel_id=1, source_target_pairs={{0,1},{1,0},{2,3},{3,2},{4,5},{5,4},{6,7},{7,6},{8,9},{9,8},{10,11... | collective-permute-start | bytes 1327112 | tf_op jit(solution)/shard_map/ppermute | solution.py:22
  57.0 3.1 %collective-permute-start.11 = (bf16[432,1536]{1,0:T(8,128)(2,1)S(1)}, bf16[432,1536]{1,0:T(8,128)(2,1)S(1)}, u32[]{:S(2)}, u32[]{:S(2)}) collective-permute-start(bf16[432,1536]{1,0:T(8,128)(2,1)S(1)} %get-tuple-element.58.mine_ref), channel_id=1, source_target_pairs={{0,1},{1,0},{2,3},{3,2},{4,5},{5,4},{6,7},{7,6},{8,9},{9,8},{10,11... | collective-permute-start | bytes 3981320 | tf_op jit(solution)/shard_map/ppermute | solution.py:22

commit v7 on v5

--- a/solution.py
+++ b/solution.py
@@ -299,6 +299,11 @@
             if g < swapped:
                 set_keys(kv_ref, section, slot, half, kv_theirs[g][rows, :])
 
+    @pl.when(section == 0)
+    def _():
+        q_ref[LAST * half :, :] = q_ref[0:half, :]
+        x_ref[LAST * half :, :] = x_ref[0:half, :]
+
 
 def place(where, groups, kv_mine, kv_theirs, q, parts):
     local, depth = parts[0][0].shape
@@ -342,6 +347,13 @@
             jobs.append((queries, [(view(kv_ref, seen, cols), view(kv_ref, seen, v_cols))], None, emit))
     attend_all(jobs)
 
+    @pl.when(section == 0)
+    def _():
+        rows = slice((LAST - 1) * half, LAST * half)
+        top_ref[:, rows, :] = jnp.full((width // HEAD_DIM, half, HEAD_DIM), -1e30, jnp.float32)
+        total_ref[:, rows, :] = jnp.zeros((width // HEAD_DIM, half, HEAD_DIM), jnp.float32)
+        sum_ref[rows, :] = jnp.zeros((half, width), jnp.float32)
+
 
 def begin_first(where, groups, placed, theirs, late_q, late_parts):
     half, width = placed[2].shape[0] // SECTIONS, late_q.shape[1]
@@ -385,42 +397,31 @@
     pl.when(section == LAST)(functools.partial(set_late, LAST ^ 1))
 
     everything = slice(None)
-
-    def late_jobs(queries, into, with_state):
-        for head, (cols, v_cols) in enumerate(head_columns(width)):
-
-            def emit(_, total, summed, cols=cols):
-                o_ref[into, cols] = (summed / total).astype(jnp.bfloat16)
-
-            def state(head=head, cols=cols):
-                return top_ref[head, into], total_ref[head, into], sum_ref[into, cols]
-
-            pairs = [(view(late_ref, everything, cols), view(late_ref, everything, v_cols))]
-            yield view(q_ref, queries, cols), pairs, state if with_state else None, emit
-
-    attend_all(list(late_jobs(slice(half, SECTIONS * half), slice(0, LAST * half), True)))
+    jobs = []
+    for head, (cols, v_cols) in enumerate(head_columns(width)):
+
+        def emit(_, total, summed, cols=cols):
+            o_ref[:, cols] = (summed / total).astype(jnp.bfloat16)
+
+        def state(head=head, cols=cols):
+            return top_ref[head], total_ref[head], sum_ref[:, cols]
+
+        pairs = [(view(late_ref, everything, cols), view(late_ref, everything, v_cols))]
+        jobs.append((view(q_ref, slice(half, SECTIONS * half), cols), pairs, state, emit))
+    attend_all(jobs)
     v_ref[...] = dot(o_ref[...], wo_ref[...])
     for s in range(1, SECTIONS):
         rows = slice((s - 1) * half, s * half)
-        stepped = (x_ref[s * half : (s + 1) * half, :] + steps[s] * v_ref[rows, :]).astype(jnp.bfloat16)
+        step = steps[jnp.where(section == 0, 0, LAST)] if s == LAST else steps[s]
+        stepped = (x_ref[s * half : (s + 1) * half, :] + step * v_ref[rows, :]).astype(jnp.bfloat16)
         st_ref[rows, :] = stepped
         hid_ref[rows, :] = modulate(
             stepped.astype(jnp.float32), mods_ref[s - 1 : s, depth:], mods_ref[s - 1 : s, :depth]
         )
 
-    @pl.when(section == 0)
-    def _():
-        attend_all(list(late_jobs(slice(0, local), slice(0, local), False)))
-        moving = dot(o_ref[0:local, :], wo_ref[...])
-        out_ref[0] = (x_ref[0:local, :] + steps[0] * moving).astype(jnp.bfloat16)
-        out_ref[1] = moving.astype(jnp.bfloat16)
-
-    @pl.when(section > 0)
-    def _():
-        base = pl.multiple_of((section - 1) * half, half)
-        out_ref[0] = st_ref[pl.ds(base, half), :][:local]
-        out_ref[1] = v_ref[pl.ds(base, half), :][:local].astype(jnp.bfloat16)
-
+    base = pl.multiple_of((jnp.where(section == 0, LAST, section) - 1) * half, half)
+    out_ref[0] = st_ref[pl.ds(base, half), :][:local]
+    out_ref[1] = v_ref[pl.ds(base, half), :][:local].astype(jnp.bfloat16)
     copies = [
         pltpu.make_async_copy(out_ref.at[0], stepped_hbm.at[0], sem.at[0]),
         pltpu.make_async_copy(out_ref.at[1], velocity_hbm.at[0], sem.at[1]),
@@ -616,7 +617,7 @@
     for slot in (3, 1, 2):
         own[slot] = from_section(latents, slot)
     parts = {slot: [own[slot], chip_swap(own[slot])] for slot in (0, None, 3)}
-    parts[1] = [own[1], from_section(parts[0][1], 1)]
+    parts[1] = [own[1], chip_swap(own[1])]
     mine, theirs, q = {}, {}, {}
 
     def work(group):

time: 63.7 us -> 62.9 us (0.987)
  waiting for transfers between devices: 19 us -> 20.1 us
  starting transfers between devices: 16.4 us -> 15.4 us
  Pallas kernels: 25.6 us -> 24.8 us
    ppermute x12, waiting for transfers between devices: 19 us -> 20.1 us  [permuted(): return lax.ppermute(block, axis, route)]
    ppermute x12, starting transfers between devices: 16.4 us -> 15.4 us  [permuted(): return lax.ppermute(block, axis, route)]
    pallas_call x1, Pallas kernels: 8.09 us -> 7.14 us  [finish_first(): pl.pallas_call(functools.partial(finish_kernel, groups=groups), out_shape...]
where the time goes in v7:
time: 62.9 us; the launch traced here: 62.7 us
  Pallas kernels  24.8 us (39%)
  waiting for transfers between devices  20.1 us (32%)
  starting transfers between devices  15.4 us (24%)
  other arithmetic  1.6 us (3%)
  between operations  0.94 us (1%)
    ppermute x12, waiting for transfers between devices, permuted(): return lax.ppermute(block, axis, route)  20.1 us
    ppermute x12, starting transfers between devices, permuted(): return lax.ppermute(block, axis, route)  15.4 us
    pallas_call x1, Pallas kernels, finish_first(): pl.pallas_call(functools.partial(finish_kernel, groups=groups), out_shape...  7.14 us
    pallas_call x3, Pallas kernels, project(): pl.pallas_call(functools.partial(project_kernel, slots=slots, counts=[len...  6.3 us
    pallas_call x1, Pallas kernels, fetch(): pl.pallas_call(functools.partial(fetch_kernel, count=len(arrays)), out_sh...  4.3 us
    pallas_call x1, Pallas kernels, begin_first(): pl.pallas_call(functools.partial(begin_kernel, groups=groups), out_shape=...  3.16 us
    pallas_call x1, Pallas kernels, finish_second(): pl.pallas_call(finish_second_kernel, out_shape=(pair, pair), in_specs=[SM...  2.41 us
  transfers between devices with their start and end apart: 12, of which 6 were waited for; matrix products, arithmetic and copies ran while one was open for 3% of the time, Pallas kernels for 24%

profile of v7, /device:TPU:0, one launch (start us, length us, event | category | flops | bytes accessed | tf_op | source)
XLA Modules:
  0.0 62.7 jit_solution(8331389193657378471)
XLA Ops:
  0.6 7.0 %collective-permute-start.4 = (bf16[72,1536]{1,0:T(8,128)(2,1)}, bf16[72,1536]{1,0:T(8,128)(2,1)S(1)}, u32[]{:S(2)}, u32[]{:S(2)}) collective-permute-start(bf16[72,1536]{1,0:T(8,128)(2,1)} %refs_5_.3), channel_id=1, source_target_pairs={{0,12},{1,13},{2,14},{3,15},{4,8},{5,9},{6,10},{7,11},{8,4},{9,5},... | collective-permute-start | bytes 663560 | tf_op jit(solution)/shard_map/ppermute | solution.py:22
  7.6 0.1 collective-permute-start.2
  7.7 1.6 %collective-permute-start = (bf16[72,1536]{1,0:T(8,128)(2,1)}, bf16[72,1536]{1,0:T(8,128)(2,1)S(1)}, u32[]{:S(2)}, u32[]{:S(2)}) collective-permute-start(bf16[72,1536]{1,0:T(8,128)(2,1)} %refs_5_.3), channel_id=1, source_target_pairs={{0,2},{1,3},{2,0},{3,1},{4,6},{5,7},{6,4},{7,5},{8,10},{9,11},{10,... | collective-permute-start | bytes 663560 | tf_op jit(solution)/shard_map/ppermute | solution.py:22
  9.3 0.5 collective-permute-start.1
  9.8 0.7 %convert_element_type.6 = f32[4]{0:T(128)S(1)} convert(s32[4]{0:T(128)} %param.10) | non-fusion elementwise | flops 4 | bytes 32 | tf_op jit(solution)/shard_map/convert_element_type | solution.py:27
  10.5 0.1 multiply_cosine_fusion
  10.6 0.8 %fusion.1.steps = f32[4]{0:T(128)S(1)} fusion(s32[4]{0:T(128)} %param.10, s32[3]{0:T(128)} %bitcast.2, s32[1]{0:T(128)} %constant.28.clone.1), kind=kLoop, calls=%fused_computation.5 | loop fusion | flops 16 | bytes 48 | tf_op jit(solution)/shard_map/div | solution.py:41
  11.4 4.3 %fetch.1 = (bf16[1536,768]{1,0:T(8,128)(2,1)S(1)}, bf16[1536,768]{1,0:T(8,128)(2,1)S(1)}, bf16[1536,768]{1,0:T(8,128)(2,1)S(1)}, bf16[768,1536]{1,0:T(8,128)(2,1)S(1)}, f32[4,3072]{1,0:T(4,128)S(1)}) custom-call(bf16[1536,768]{1,0:T(8,128)(2,1)} %refs_0_.2, bf16[1536,768]{1,0:T(8,128)(2,1)} %refs_1_.1, bf16[1536,768]{1,0:T(8,128)(2,1)} %refs_2_.2, ...), custom_call_target="tpu_custom_call" | custom-call | bytes 9437184 | tf_op jit(solution)/shard_map/fetch/pallas_call | solution.py:199
  15.7 0.6 collective-permute-done.refs_1_.refs_6_
  16.3 3.3 %collective-permute-done.1.refs_3_ = bf16[72,1536]{1,0:T(8,128)(2,1)S(1)} collective-permute-done((bf16[72,1536]{1,0:T(8,128)(2,1)}, bf16[72,1536]{1,0:T(8,128)(2,1)S(1)}, u32[]{:S(2)}, u32[]{:S(2)}) %collective-permute-start.1) | collective-permute-done | bytes 221216 | tf_op jit(solution)/shard_map/ppermute | solution.py:22
  19.6 2.5 %project.3 = (bf16[288,1536]{1,0:T(8,128)(2,1)S(1)}, bf16[288,768]{1,0:T(8,128)(2,1)S(1)}) custom-call(s32[1]{0:T(128)} %bitcast.where, bf16[72,1536]{1,0:T(8,128)(2,1)S(1)} %copy-done, bf16[72,1536]{1,0:T(8,128)(2,1)S(1)} %collective-permute-done.refs_1_.refs_6_, bf16[72,1536]{1,0:T(8,128)(2,1)S(1)} %copy-done.1, ...), custom_call_target="tpu_custom_call" | custom-call | flops 2038431744 | bytes 2097152 | tf_op jit(solution)/shard_map/project/pallas_call | solution.py:238
  22.1 0.1 collective-permute-start.8
  22.2 0.0 collective-permute-done.4.refs_2_.refs_9_
  22.2 1.6 %collective-permute-start.5 = (bf16[72,1536]{1,0:T(8,128)(2,1)S(1)}, bf16[72,1536]{1,0:T(8,128)(2,1)S(1)}, u32[]{:S(2)}, u32[]{:S(2)}) collective-permute-start(bf16[72,1536]{1,0:T(8,128)(2,1)S(1)} %collective-permute-done.4.refs_2_.refs_9_), channel_id=1, source_target_pairs={{0,2},{1,3},{2,0},{3,1},{4,6},{5,7},{6,4},{7,5},{8,10},{9,11},{10,... | collective-permute-start | bytes 663560 | tf_op jit(solution)/shard_map/ppermute | solution.py:22
  23.8 0.5 collective-permute-start.3
  24.3 1.8 %collective-permute-start.6 = (bf16[72,1536]{1,0:T(8,128)(2,1)S(1)}, bf16[72,1536]{1,0:T(8,128)(2,1)S(1)}, u32[]{:S(2)}, u32[]{:S(2)}) collective-permute-start(bf16[72,1536]{1,0:T(8,128)(2,1)S(1)} %copy-done), channel_id=1, source_target_pairs={{0,8},{1,9},{2,10},{3,11},{4,12},{5,13},{6,14},{7,15},{16,24},{17,... | collective-permute-start | bytes 663560 | tf_op jit(solution)/shard_map/ppermute | solution.py:22
  26.1 4.5 %collective-permute-done.5.refs_3_.refs_10_ = bf16[72,1536]{1,0:T(8,128)(2,1)S(1)} collective-permute-done((bf16[72,1536]{1,0:T(8,128)(2,1)S(1)}, bf16[72,1536]{1,0:T(8,128)(2,1)S(1)}, u32[]{:S(2)}, u32[]{:S(2)}) %collective-permute-start.5) | collective-permute-done | bytes 221216 | tf_op jit(solution)/shard_map/ppermute | solution.py:22
  30.6 4.2 %collective-permute-done.3.refs_1_.refs_8_ = bf16[72,1536]{1,0:T(8,128)(2,1)S(1)} collective-permute-done((bf16[72,1536]{1,0:T(8,128)(2,1)S(1)}, bf16[72,1536]{1,0:T(8,128)(2,1)S(1)}, u32[]{:S(2)}, u32[]{:S(2)}) %collective-permute-start.3) | collective-permute-done | bytes 221216 | tf_op jit(solution)/shard_map/ppermute | solution.py:22
  34.8 2.5 %project.4 = (bf16[288,1536]{1,0:T(8,128)(2,1)S(1)}, bf16[288,768]{1,0:T(8,128)(2,1)S(1)}) custom-call(s32[1]{0:T(128)} %bitcast.where, bf16[72,1536]{1,0:T(8,128)(2,1)S(1)} %collective-permute-done.2.refs_0_.refs_7_, bf16[72,1536]{1,0:T(8,128)(2,1)S(1)} %collective-permute-done.3.refs_1_.refs_8_, ...), custom_call_target="tpu_custom_call" | custom-call | flops 2038431744 | bytes 2097152 | tf_op jit(solution)/shard_map/project/pallas_call | solution.py:238
  37.2 0.1 collective-permute-start.9
  37.3 0.0 collective-permute-done.6.refs_0_.own_ref
  37.3 1.6 %collective-permute-start.7 = (bf16[72,1536]{1,0:T(8,128)(2,1)S(1)}, bf16[72,1536]{1,0:T(8,128)(2,1)S(1)}, u32[]{:S(2)}, u32[]{:S(2)}) collective-permute-start(bf16[72,1536]{1,0:T(8,128)(2,1)S(1)} %collective-permute-done.6.refs_0_.own_ref), channel_id=1, source_target_pairs={{0,2},{1,3},{2,0},{3,1},{4,6},{5,7},{6,4},{7,5},{8,10},{9,11},{10,... | collective-permute-start | bytes 663560 | tf_op jit(solution)/shard_map/ppermute | solution.py:22
  38.9 0.4 place.1
  39.3 5.8 %collective-permute-done.7.refs_1_.across_ref = bf16[72,1536]{1,0:T(8,128)(2,1)S(1)} collective-permute-done((bf16[72,1536]{1,0:T(8,128)(2,1)S(1)}, bf16[72,1536]{1,0:T(8,128)(2,1)S(1)}, u32[]{:S(2)}, u32[]{:S(2)}) %collective-permute-start.7) | collective-permute-done | bytes 221216 | tf_op jit(solution)/shard_map/ppermute | solution.py:22
  45.2 1.3 %project.5 = (bf16[144,1536]{1,0:T(8,128)(2,1)S(1)}, bf16[144,768]{1,0:T(8,128)(2,1)S(1)}) custom-call(s32[1]{0:T(128)} %bitcast.where, bf16[72,1536]{1,0:T(8,128)(2,1)S(1)} %collective-permute-done.6.refs_0_.own_ref, bf16[72,1536]{1,0:T(8,128)(2,1)S(1)} %collective-permute-done.7.refs_1_.across_ref, ...), custom_call_target="tpu_custom_call" | custom-call | flops 1019215872 | bytes 2097152 | tf_op jit(solution)/shard_map/project/pallas_call | solution.py:238
  46.5 0.1 collective-permute-start.10
  46.6 3.2 %begin_first.1 = (bf16[1152,1536]{1,0:T(8,128)(2,1)S(1)}, f32[576,1536]{1,0:T(8,128)S(1)}, bf16[576,768]{1,0:T(8,128)(2,1)S(1)}, f32[6,432,128]{2,1,0:T(8,128)S(...) custom-call(s32[1]{0:T(128)} %bitcast.where, ...), custom_call_target="tpu_custom_call", output_to_operand_aliasing={{0}: (5, {}), {1}: (6, {}), {2}: (7, {})} | custom-call | flops 764411904 | bytes 2097152 | tf_op jit(solution)/shard_map/begin_first/pallas_call | solution.py:361
  49.8 7.1 %finish_first.1 = (bf16[2,72,1536]{2,1,0:T(8,128)(2,1)}, bf16[2,72,1536]{2,1,0:T(8,128)(2,1)}, bf16[432,1536]{1,0:T(8,128)(2,1)S(1)}, bf16[72,1536]{1,0:T(8,128)(2,1)S(1)}, bf16[72,1536]{1,0:T(8,128)(2,1)S(1)}) custom-call(s32[1]{0:T(128)} %bitcast.where, f32[4]{0:T(128)S(1)} %fusion.1.steps, bf16[288,1536]{1,0:T(8,128)(2,1)S(1)} %get-tuple-element.40.refs_0_.fresh_mine_ref, ...), custom_call_target="tpu_custom_call" | custom-call | flops 4076863488 | bytes 4194304 | tf_op jit(solution)/shard_map/finish_first/pallas_call | solution.py:447
  56.9 0.6 collective-permute-start.11
  57.5 1.1 %begin_second.1 = (bf16[72,768]{1,0:T(8,128)(2,1)S(1)}, f32[6,72,128]{2,1,0:T(8,128)S(1)}, f32[6,72,128]{2,1,0:T(8,128)S(1)}, f32[72,768]{1,0:T(8,128)S(1)}) custom-call(s32[1]{0:T(128)} %bitcast.where, bf16[72,1536]{1,0:T(8,128)(2,1)S(1)} %get-tuple-element.57.own_ref, bf16[1536,768]{1,0:T(8,128)(2,1)S(1)} %get-tuple-element.39.refs_7_.refs_5_.wq_ref, ...), custom_call_target="tpu_custom_call" | custom-call | flops 339738624 | bytes 2097152 | tf_op jit(solution)/shard_map/begin_second/pallas_call | solution.py:504
  58.5 1.6 %collective-permute-done.11.theirs_ref = bf16[432,1536]{1,0:T(8,128)(2,1)S(1)} collective-permute-done((bf16[432,1536]{1,0:T(8,128)(2,1)S(1)}, bf16[432,1536]{1,0:T(8,128)(2,1)S(1)}, u32[]{:S(2)}, u32[]{:S(2)}) %collective-permute-start.11) | collective-permute-done | bytes 1327136 | tf_op jit(solution)/shard_map/ppermute | solution.py:22
  60.2 2.4 %finish_second.1 = (bf16[2,72,1536]{2,1,0:T(8,128)(2,1)}, bf16[2,72,1536]{2,1,0:T(8,128)(2,1)}) custom-call(s32[1]{0:T(128)} %bitcast.where, f32[4]{0:T(128)S(1)} %fusion.1.steps, bf16[72,768]{1,0:T(8,128)(2,1)S(1)} %get-tuple-element.59.q_ref, f32[6,72,128]{2,1,0:T(8,128)S(1)} %get-tuple-element.60.top_ref, ...), custom_call_target="tpu_custom_call", output_to_operand_aliasing={{0}: (10, {}), {1}: (11, {})} | custom-call | flops 339738624 | bytes 4194304 | tf_op jit(solution)/shard_map/finish_second/pallas_call | solution.py:563
  (10 shorter events, 0.0 us)
Async XLA Ops:
  0.6 21.6 %collective-permute-start.4 = (bf16[72,1536]{1,0:T(8,128)(2,1)}, bf16[72,1536]{1,0:T(8,128)(2,1)S(1)}, u32[]{:S(2)}, u32[]{:S(2)}) collective-permute-start(bf16[72,1536]{1,0:T(8,128)(2,1)} %refs_5_.3), channel_id=1, source_target_pairs={{0,12},{1,13},{2,14},{3,15},{4,8},{5,9},{6,10},{7,11},{8,4},{9,5},... | collective-permute-start | bytes 663560 | tf_op jit(solution)/shard_map/ppermute | solution.py:22
  7.6 16.2 %collective-permute-start.2 = (bf16[72,1536]{1,0:T(8,128)(2,1)}, bf16[72,1536]{1,0:T(8,128)(2,1)S(1)}, u32[]{:S(2)}, u32[]{:S(2)}) collective-permute-start(bf16[72,1536]{1,0:T(8,128)(2,1)} %refs_5_.3), channel_id=1, source_target_pairs={{0,4},{1,5},{2,6},{3,7},{4,0},{5,1},{6,2},{7,3},{8,12},{9,13},{10,... | collective-permute-start | bytes 663560 | tf_op jit(solution)/shard_map/ppermute | solution.py:22
  7.7 8.6 %collective-permute-start = (bf16[72,1536]{1,0:T(8,128)(2,1)}, bf16[72,1536]{1,0:T(8,128)(2,1)S(1)}, u32[]{:S(2)}, u32[]{:S(2)}) collective-permute-start(bf16[72,1536]{1,0:T(8,128)(2,1)} %refs_5_.3), channel_id=1, source_target_pairs={{0,2},{1,3},{2,0},{3,1},{4,6},{5,7},{6,4},{7,5},{8,10},{9,11},{10,... | collective-permute-start | bytes 663560 | tf_op jit(solution)/shard_map/ppermute | solution.py:22
  9.3 10.3 %collective-permute-start.1 = (bf16[72,1536]{1,0:T(8,128)(2,1)}, bf16[72,1536]{1,0:T(8,128)(2,1)S(1)}, u32[]{:S(2)}, u32[]{:S(2)}) collective-permute-start(bf16[72,1536]{1,0:T(8,128)(2,1)} %fresh_ref.1), channel_id=1, source_target_pairs={{0,2},{1,3},{2,0},{3,1},{4,6},{5,7},{6,4},{7,5},{8,10},{9,11},{10,... | collective-permute-start | bytes 663560 | tf_op jit(solution)/shard_map/ppermute | solution.py:22
  11.4 8.2 %copy-start = (bf16[72,1536]{1,0:T(8,128)(2,1)S(1)}, bf16[72,1536]{1,0:T(8,128)(2,1)}, u32[]{:S(2)}) copy-start(bf16[72,1536]{1,0:T(8,128)(2,1)} %refs_5_.3) | copy-start | bytes 663556
  11.4 8.2 %copy-start.1 = (bf16[72,1536]{1,0:T(8,128)(2,1)S(1)}, bf16[72,1536]{1,0:T(8,128)(2,1)}, u32[]{:S(2)}) copy-start(bf16[72,1536]{1,0:T(8,128)(2,1)} %fresh_ref.1) | copy-start | bytes 663556
  22.1 16.8 %collective-permute-start.8 = (bf16[288,1536]{1,0:T(8,128)(2,1)S(1)}, bf16[288,1536]{1,0:T(8,128)(2,1)S(1)}, u32[]{:S(2)}, u32[]{:S(2)}) collective-permute-start(bf16[288,1536]{1,0:T(8,128)(2,1)S(1)} %get-tuple-element.40.refs_0_.fresh_mine_ref), channel_id=1, source_target_pairs={{0,1},{1,0},{2,3},{3,2},{4,5},{5,4},{6,7},{7,6},{8,9},{9,8},{10,11... | collective-permute-start | bytes 2654216 | tf_op jit(solution)/shard_map/ppermute | solution.py:22
  22.2 8.4 %collective-permute-start.5 = (bf16[72,1536]{1,0:T(8,128)(2,1)S(1)}, bf16[72,1536]{1,0:T(8,128)(2,1)S(1)}, u32[]{:S(2)}, u32[]{:S(2)}) collective-permute-start(bf16[72,1536]{1,0:T(8,128)(2,1)S(1)} %collective-permute-done.4.refs_2_.refs_9_), channel_id=1, source_target_pairs={{0,2},{1,3},{2,0},{3,1},{4,6},{5,7},{6,4},{7,5},{8,10},{9,11},{10,... | collective-permute-start | bytes 663560 | tf_op jit(solution)/shard_map/ppermute | solution.py:22
  23.8 11.0 %collective-permute-start.3 = (bf16[72,1536]{1,0:T(8,128)(2,1)S(1)}, bf16[72,1536]{1,0:T(8,128)(2,1)S(1)}, u32[]{:S(2)}, u32[]{:S(2)}) collective-permute-start(bf16[72,1536]{1,0:T(8,128)(2,1)S(1)} %collective-permute-done.2.refs_0_.refs_7_), channel_id=1, source_target_pairs={{0,2},{1,3},{2,0},{3,1},{4,6},{5,7},{6,4},{7,5},{8,10},{9,11},{10,... | collective-permute-start | bytes 663560 | tf_op jit(solution)/shard_map/ppermute | solution.py:22
  24.3 13.0 %collective-permute-start.6 = (bf16[72,1536]{1,0:T(8,128)(2,1)S(1)}, bf16[72,1536]{1,0:T(8,128)(2,1)S(1)}, u32[]{:S(2)}, u32[]{:S(2)}) collective-permute-start(bf16[72,1536]{1,0:T(8,128)(2,1)S(1)} %copy-done), channel_id=1, source_target_pairs={{0,8},{1,9},{2,10},{3,11},{4,12},{5,13},{6,14},{7,15},{16,24},{17,... | collective-permute-start | bytes 663560 | tf_op jit(solution)/shard_map/ppermute | solution.py:22
  37.2 9.4 %collective-permute-start.9 = (bf16[288,1536]{1,0:T(8,128)(2,1)S(1)}, bf16[288,1536]{1,0:T(8,128)(2,1)S(1)}, u32[]{:S(2)}, u32[]{:S(2)}) collective-permute-start(bf16[288,1536]{1,0:T(8,128)(2,1)S(1)} %get-tuple-element.41.refs_1_), channel_id=1, source_target_pairs={{0,1},{1,0},{2,3},{3,2},{4,5},{5,4},{6,7},{7,6},{8,9},{9,8},{10,11... | collective-permute-start | bytes 2654216 | tf_op jit(solution)/shard_map/ppermute | solution.py:22
  37.3 7.8 %collective-permute-start.7 = (bf16[72,1536]{1,0:T(8,128)(2,1)S(1)}, bf16[72,1536]{1,0:T(8,128)(2,1)S(1)}, u32[]{:S(2)}, u32[]{:S(2)}) collective-permute-start(bf16[72,1536]{1,0:T(8,128)(2,1)S(1)} %collective-permute-done.6.refs_0_.own_ref), channel_id=1, source_target_pairs={{0,2},{1,3},{2,0},{3,1},{4,6},{5,7},{6,4},{7,5},{8,10},{9,11},{10,... | collective-permute-start | bytes 663560 | tf_op jit(solution)/shard_map/ppermute | solution.py:22
  46.5 3.3 %collective-permute-start.10 = (bf16[144,1536]{1,0:T(8,128)(2,1)S(1)}, bf16[144,1536]{1,0:T(8,128)(2,1)S(1)}, u32[]{:S(2)}, u32[]{:S(2)}) collective-permute-start(bf16[144,1536]{1,0:T(8,128)(2,1)S(1)} %get-tuple-element.49.refs_2_), channel_id=1, source_target_pairs={{0,1},{1,0},{2,3},{3,2},{4,5},{5,4},{6,7},{7,6},{8,9},{9,8},{10,11... | collective-permute-start | bytes 1327112 | tf_op jit(solution)/shard_map/ppermute | solution.py:22
  56.9 3.2 %collective-permute-start.11 = (bf16[432,1536]{1,0:T(8,128)(2,1)S(1)}, bf16[432,1536]{1,0:T(8,128)(2,1)S(1)}, u32[]{:S(2)}, u32[]{:S(2)}) collective-permute-start(bf16[432,1536]{1,0:T(8,128)(2,1)S(1)} %get-tuple-element.58.mine_ref), channel_id=1, source_target_pairs={{0,1},{1,0},{2,3},{3,2},{4,5},{5,4},{6,7},{7,6},{8,9},{9,8},{10,11... | collective-permute-start | bytes 3981320 | tf_op jit(solution)/shard_map/ppermute | solution.py:22

commit v8 on v7

--- a/solution.py
+++ b/solution.py
@@ -150,7 +150,7 @@
     return top, total, summed
 
 
-AHEAD = 3
+AHEAD = 4
 
 
 def attend_all(jobs):
@@ -398,16 +398,18 @@
 
     everything = slice(None)
     jobs = []
-    for head, (cols, v_cols) in enumerate(head_columns(width)):
-
-        def emit(_, total, summed, cols=cols):
-            o_ref[:, cols] = (summed / total).astype(jnp.bfloat16)
-
-        def state(head=head, cols=cols):
-            return top_ref[head], total_ref[head], sum_ref[:, cols]
-
-        pairs = [(view(late_ref, everything, cols), view(late_ref, everything, v_cols))]
-        jobs.append((view(q_ref, slice(half, SECTIONS * half), cols), pairs, state, emit))
+    for s in range(1, SECTIONS):
+        rows = slice((s - 1) * half, s * half)
+        for head, (cols, v_cols) in enumerate(head_columns(width)):
+
+            def emit(_, total, summed, cols=cols, rows=rows):
+                o_ref[rows, cols] = (summed / total).astype(jnp.bfloat16)
+
+            def state(head=head, cols=cols, rows=rows):
+                return top_ref[head, rows, :], total_ref[head, rows, :], sum_ref[rows, cols]
+
+            pairs = [(view(late_ref, everything, cols), view(late_ref, everything, v_cols))]
+            jobs.append((view(q_ref, slice(s * half, (s + 1) * half), cols), pairs, state, emit))
     attend_all(jobs)
     v_ref[...] = dot(o_ref[...], wo_ref[...])
     for s in range(1, SECTIONS):
@@ -617,7 +619,7 @@
     for slot in (3, 1, 2):
         own[slot] = from_section(latents, slot)
     parts = {slot: [own[slot], chip_swap(own[slot])] for slot in (0, None, 3)}
-    parts[1] = [own[1], chip_swap(own[1])]
+    parts[1] = [own[1], from_section(parts[0][1], 1)]
     mine, theirs, q = {}, {}, {}
 
     def work(group):

time: 62.9 us -> 62.8 us (level)
  waiting for transfers between devices: 20.1 us -> 19 us
  starting transfers between devices: 15.4 us -> 16.4 us
    ppermute x12, waiting for transfers between devices: 20.1 us -> 19 us  [permuted(): return lax.ppermute(block, axis, route)]
    ppermute x12, starting transfers between devices: 15.4 us -> 16.4 us  [permuted(): return lax.ppermute(block, axis, route)]
where the time goes in v8:
time: 62.8 us; the launch traced here: 62.6 us
  Pallas kernels  24.7 us (39%)
  waiting for transfers between devices  19 us (30%)
  starting transfers between devices  16.4 us (26%)
  other arithmetic  1.6 us (3%)
  between operations  0.94 us (1%)
    ppermute x12, waiting for transfers between devices, permuted(): return lax.ppermute(block, axis, route)  19 us
    ppermute x12, starting transfers between devices, permuted(): return lax.ppermute(block, axis, route)  16.4 us
    pallas_call x1, Pallas kernels, finish_first(): pl.pallas_call(functools.partial(finish_kernel, groups=groups), out_shape...  6.98 us
    pallas_call x3, Pallas kernels, project(): pl.pallas_call(functools.partial(project_kernel, slots=slots, counts=[len...  6.3 us
    pallas_call x1, Pallas kernels, fetch(): pl.pallas_call(functools.partial(fetch_kernel, count=len(arrays)), out_sh...  4.3 us
    pallas_call x1, Pallas kernels, begin_first(): pl.pallas_call(functools.partial(begin_kernel, groups=groups), out_shape=...  3.16 us
    pallas_call x1, Pallas kernels, finish_second(): pl.pallas_call(finish_second_kernel, out_shape=(pair, pair), in_specs=[SM...  2.54 us
  transfers between devices with their start and end apart: 12, of which 6 were waited for; matrix products, arithmetic and copies ran while one was open for 3% of the time, Pallas kernels for 24%

profile of v8, /device:TPU:0, one launch (start us, length us, event | category | flops | bytes accessed | tf_op | source)
XLA Modules:
  0.0 62.6 jit_solution(4247174157284353275)
XLA Ops:
  0.6 7.0 %collective-permute-start.4 = (bf16[72,1536]{1,0:T(8,128)(2,1)}, bf16[72,1536]{1,0:T(8,128)(2,1)S(1)}, u32[]{:S(2)}, u32[]{:S(2)}) collective-permute-start(bf16[72,1536]{1,0:T(8,128)(2,1)} %refs_5_.3), channel_id=1, source_target_pairs={{0,12},{1,13},{2,14},{3,15},{4,8},{5,9},{6,10},{7,11},{8,4},{9,5},... | collective-permute-start | bytes 663560 | tf_op jit(solution)/shard_map/ppermute | solution.py:22
  7.6 1.6 %collective-permute-start = (bf16[72,1536]{1,0:T(8,128)(2,1)}, bf16[72,1536]{1,0:T(8,128)(2,1)S(1)}, u32[]{:S(2)}, u32[]{:S(2)}) collective-permute-start(bf16[72,1536]{1,0:T(8,128)(2,1)} %refs_5_.3), channel_id=1, source_target_pairs={{0,2},{1,3},{2,0},{3,1},{4,6},{5,7},{6,4},{7,5},{8,10},{9,11},{10,... | collective-permute-start | bytes 663560 | tf_op jit(solution)/shard_map/ppermute | solution.py:22
  9.2 0.5 collective-permute-start.1
  9.7 0.7 %convert_element_type.6 = f32[4]{0:T(128)S(1)} convert(s32[4]{0:T(128)} %param.10) | non-fusion elementwise | flops 4 | bytes 32 | tf_op jit(solution)/shard_map/convert_element_type | solution.py:27
  10.4 0.1 multiply_cosine_fusion
  10.5 0.8 %fusion.1.steps = f32[4]{0:T(128)S(1)} fusion(s32[4]{0:T(128)} %param.10, s32[3]{0:T(128)} %bitcast.2, s32[1]{0:T(128)} %constant.28.clone.1), kind=kLoop, calls=%fused_computation.5 | loop fusion | flops 16 | bytes 48 | tf_op jit(solution)/shard_map/div | solution.py:41
  11.3 4.3 %fetch.1 = (bf16[1536,768]{1,0:T(8,128)(2,1)S(1)}, bf16[1536,768]{1,0:T(8,128)(2,1)S(1)}, bf16[1536,768]{1,0:T(8,128)(2,1)S(1)}, bf16[768,1536]{1,0:T(8,128)(2,1)S(1)}, f32[4,3072]{1,0:T(4,128)S(1)}) custom-call(bf16[1536,768]{1,0:T(8,128)(2,1)} %refs_0_.2, bf16[1536,768]{1,0:T(8,128)(2,1)} %refs_1_.1, bf16[1536,768]{1,0:T(8,128)(2,1)} %refs_2_.2, ...), custom_call_target="tpu_custom_call" | custom-call | bytes 9437184 | tf_op jit(solution)/shard_map/fetch/pallas_call | solution.py:199
  15.6 0.6 collective-permute-done.refs_1_.refs_6_
  16.2 3.3 %collective-permute-done.1.refs_3_ = bf16[72,1536]{1,0:T(8,128)(2,1)S(1)} collective-permute-done((bf16[72,1536]{1,0:T(8,128)(2,1)}, bf16[72,1536]{1,0:T(8,128)(2,1)S(1)}, u32[]{:S(2)}, u32[]{:S(2)}) %collective-permute-start.1) | collective-permute-done | bytes 221216 | tf_op jit(solution)/shard_map/ppermute | solution.py:22
  19.5 2.5 %project.3 = (bf16[288,1536]{1,0:T(8,128)(2,1)S(1)}, bf16[288,768]{1,0:T(8,128)(2,1)S(1)}) custom-call(s32[1]{0:T(128)} %bitcast.where, bf16[72,1536]{1,0:T(8,128)(2,1)S(1)} %copy-done, bf16[72,1536]{1,0:T(8,128)(2,1)S(1)} %collective-permute-done.refs_1_.refs_6_, bf16[72,1536]{1,0:T(8,128)(2,1)S(1)} %copy-done.1, ...), custom_call_target="tpu_custom_call" | custom-call | flops 2038431744 | bytes 2097152 | tf_op jit(solution)/shard_map/project/pallas_call | solution.py:238
  22.0 0.1 collective-permute-start.8
  22.1 0.1 collective-permute-start.2
  22.2 1.6 %collective-permute-start.5 = (bf16[72,1536]{1,0:T(8,128)(2,1)S(1)}, bf16[72,1536]{1,0:T(8,128)(2,1)S(1)}, u32[]{:S(2)}, u32[]{:S(2)}) collective-permute-start(bf16[72,1536]{1,0:T(8,128)(2,1)S(1)} %collective-permute-done.4.refs_2_.refs_9_), channel_id=1, source_target_pairs={{0,2},{1,3},{2,0},{3,1},{4,6},{5,7},{6,4},{7,5},{8,10},{9,11},{10,... | collective-permute-start | bytes 663560 | tf_op jit(solution)/shard_map/ppermute | solution.py:22
  23.8 1.9 %collective-permute-start.3 = (bf16[72,1536]{1,0:T(8,128)(2,1)S(1)}, bf16[72,1536]{1,0:T(8,128)(2,1)S(1)}, u32[]{:S(2)}, u32[]{:S(2)}) collective-permute-start(bf16[72,1536]{1,0:T(8,128)(2,1)S(1)} %collective-permute-done.refs_1_.refs_6_), channel_id=1, source_target_pairs={{0,4},{1,5},{2,6},{3,7},{4,0},{5,1},{6,2},{7,3},{8,12},{9,13},{10,... | collective-permute-start | bytes 663560 | tf_op jit(solution)/shard_map/ppermute | solution.py:22
  25.7 1.3 %collective-permute-start.6 = (bf16[72,1536]{1,0:T(8,128)(2,1)S(1)}, bf16[72,1536]{1,0:T(8,128)(2,1)S(1)}, u32[]{:S(2)}, u32[]{:S(2)}) collective-permute-start(bf16[72,1536]{1,0:T(8,128)(2,1)S(1)} %copy-done), channel_id=1, source_target_pairs={{0,8},{1,9},{2,10},{3,11},{4,12},{5,13},{6,14},{7,15},{16,24},{17,... | collective-permute-start | bytes 663560 | tf_op jit(solution)/shard_map/ppermute | solution.py:22
  27.1 3.4 %collective-permute-done.2.refs_0_.refs_7_ = bf16[72,1536]{1,0:T(8,128)(2,1)S(1)} collective-permute-done((bf16[72,1536]{1,0:T(8,128)(2,1)S(1)}, bf16[72,1536]{1,0:T(8,128)(2,1)S(1)}, u32[]{:S(2)}, u32[]{:S(2)}) %collective-permute-start.2) | collective-permute-done | bytes 221216 | tf_op jit(solution)/shard_map/ppermute | solution.py:22
  30.5 0.0 collective-permute-done.5.refs_3_.refs_10_
  30.5 4.2 %collective-permute-done.3.refs_1_.refs_8_ = bf16[72,1536]{1,0:T(8,128)(2,1)S(1)} collective-permute-done((bf16[72,1536]{1,0:T(8,128)(2,1)S(1)}, bf16[72,1536]{1,0:T(8,128)(2,1)S(1)}, u32[]{:S(2)}, u32[]{:S(2)}) %collective-permute-start.3) | collective-permute-done | bytes 221216 | tf_op jit(solution)/shard_map/ppermute | solution.py:22
  34.7 2.5 %project.4 = (bf16[288,1536]{1,0:T(8,128)(2,1)S(1)}, bf16[288,768]{1,0:T(8,128)(2,1)S(1)}) custom-call(s32[1]{0:T(128)} %bitcast.where, bf16[72,1536]{1,0:T(8,128)(2,1)S(1)} %collective-permute-done.2.refs_0_.refs_7_, bf16[72,1536]{1,0:T(8,128)(2,1)S(1)} %collective-permute-done.3.refs_1_.refs_8_, ...), custom_call_target="tpu_custom_call" | custom-call | flops 2038431744 | bytes 2097152 | tf_op jit(solution)/shard_map/project/pallas_call | solution.py:238
  37.2 0.1 collective-permute-start.9
  37.2 0.0 collective-permute-done.6.refs_0_.own_ref
  37.3 1.6 %collective-permute-start.7 = (bf16[72,1536]{1,0:T(8,128)(2,1)S(1)}, bf16[72,1536]{1,0:T(8,128)(2,1)S(1)}, u32[]{:S(2)}, u32[]{:S(2)}) collective-permute-start(bf16[72,1536]{1,0:T(8,128)(2,1)S(1)} %collective-permute-done.6.refs_0_.own_ref), channel_id=1, source_target_pairs={{0,2},{1,3},{2,0},{3,1},{4,6},{5,7},{6,4},{7,5},{8,10},{9,11},{10,... | collective-permute-start | bytes 663560 | tf_op jit(solution)/shard_map/ppermute | solution.py:22
  38.8 0.4 place.1
  39.3 5.8 %collective-permute-done.7.refs_1_.across_ref = bf16[72,1536]{1,0:T(8,128)(2,1)S(1)} collective-permute-done((bf16[72,1536]{1,0:T(8,128)(2,1)S(1)}, bf16[72,1536]{1,0:T(8,128)(2,1)S(1)}, u32[]{:S(2)}, u32[]{:S(2)}) %collective-permute-start.7) | collective-permute-done | bytes 221216 | tf_op jit(solution)/shard_map/ppermute | solution.py:22
  45.1 1.3 %project.5 = (bf16[144,1536]{1,0:T(8,128)(2,1)S(1)}, bf16[144,768]{1,0:T(8,128)(2,1)S(1)}) custom-call(s32[1]{0:T(128)} %bitcast.where, bf16[72,1536]{1,0:T(8,128)(2,1)S(1)} %collective-permute-done.6.refs_0_.own_ref, bf16[72,1536]{1,0:T(8,128)(2,1)S(1)} %collective-permute-done.7.refs_1_.across_ref, ...), custom_call_target="tpu_custom_call" | custom-call | flops 1019215872 | bytes 2097152 | tf_op jit(solution)/shard_map/project/pallas_call | solution.py:238
  46.4 0.1 collective-permute-start.10
  46.5 3.2 %begin_first.1 = (bf16[1152,1536]{1,0:T(8,128)(2,1)S(1)}, f32[576,1536]{1,0:T(8,128)S(1)}, bf16[576,768]{1,0:T(8,128)(2,1)S(1)}, f32[6,432,128]{2,1,0:T(8,128)S(...) custom-call(s32[1]{0:T(128)} %bitcast.where, ...), custom_call_target="tpu_custom_call", output_to_operand_aliasing={{0}: (5, {}), {1}: (6, {}), {2}: (7, {})} | custom-call | flops 764411904 | bytes 2097152 | tf_op jit(solution)/shard_map/begin_first/pallas_call | solution.py:361
  49.7 7.0 %finish_first.1 = (bf16[2,72,1536]{2,1,0:T(8,128)(2,1)}, bf16[2,72,1536]{2,1,0:T(8,128)(2,1)}, bf16[432,1536]{1,0:T(8,128)(2,1)S(1)}, bf16[72,1536]{1,0:T(8,128)(2,1)S(1)}, bf16[72,1536]{1,0:T(8,128)(2,1)S(1)}) custom-call(s32[1]{0:T(128)} %bitcast.where, f32[4]{0:T(128)S(1)} %fusion.1.steps, bf16[288,1536]{1,0:T(8,128)(2,1)S(1)} %get-tuple-element.40.refs_0_.fresh_mine_ref, ...), custom_call_target="tpu_custom_call" | custom-call | flops 4076863488 | bytes 4194304 | tf_op jit(solution)/shard_map/finish_first/pallas_call | solution.py:449
  56.7 0.5 collective-permute-start.11
  57.2 1.0 %begin_second.1 = (bf16[72,768]{1,0:T(8,128)(2,1)S(1)}, f32[6,72,128]{2,1,0:T(8,128)S(1)}, f32[6,72,128]{2,1,0:T(8,128)S(1)}, f32[72,768]{1,0:T(8,128)S(1)}) custom-call(s32[1]{0:T(128)} %bitcast.where, bf16[72,1536]{1,0:T(8,128)(2,1)S(1)} %get-tuple-element.57.own_ref, bf16[1536,768]{1,0:T(8,128)(2,1)S(1)} %get-tuple-element.39.refs_7_.refs_5_.wq_ref, ...), custom_call_target="tpu_custom_call" | custom-call | flops 339738624 | bytes 2097152 | tf_op jit(solution)/shard_map/begin_second/pallas_call | solution.py:506
  58.2 1.7 %collective-permute-done.11.theirs_ref = bf16[432,1536]{1,0:T(8,128)(2,1)S(1)} collective-permute-done((bf16[432,1536]{1,0:T(8,128)(2,1)S(1)}, bf16[432,1536]{1,0:T(8,128)(2,1)S(1)}, u32[]{:S(2)}, u32[]{:S(2)}) %collective-permute-start.11) | collective-permute-done | bytes 1327136 | tf_op jit(solution)/shard_map/ppermute | solution.py:22
  59.9 2.5 %finish_second.1 = (bf16[2,72,1536]{2,1,0:T(8,128)(2,1)}, bf16[2,72,1536]{2,1,0:T(8,128)(2,1)}) custom-call(s32[1]{0:T(128)} %bitcast.where, f32[4]{0:T(128)S(1)} %fusion.1.steps, bf16[72,768]{1,0:T(8,128)(2,1)S(1)} %get-tuple-element.59.q_ref, f32[6,72,128]{2,1,0:T(8,128)S(1)} %get-tuple-element.60.top_ref, ...), custom_call_target="tpu_custom_call", output_to_operand_aliasing={{0}: (10, {}), {1}: (11, {})} | custom-call | flops 339738624 | bytes 4194304 | tf_op jit(solution)/shard_map/finish_second/pallas_call | solution.py:565
  (10 shorter events, 0.0 us)
Async XLA Ops:
  0.6 21.6 %collective-permute-start.4 = (bf16[72,1536]{1,0:T(8,128)(2,1)}, bf16[72,1536]{1,0:T(8,128)(2,1)S(1)}, u32[]{:S(2)}, u32[]{:S(2)}) collective-permute-start(bf16[72,1536]{1,0:T(8,128)(2,1)} %refs_5_.3), channel_id=1, source_target_pairs={{0,12},{1,13},{2,14},{3,15},{4,8},{5,9},{6,10},{7,11},{8,4},{9,5},... | collective-permute-start | bytes 663560 | tf_op jit(solution)/shard_map/ppermute | solution.py:22
  7.6 8.6 %collective-permute-start = (bf16[72,1536]{1,0:T(8,128)(2,1)}, bf16[72,1536]{1,0:T(8,128)(2,1)S(1)}, u32[]{:S(2)}, u32[]{:S(2)}) collective-permute-start(bf16[72,1536]{1,0:T(8,128)(2,1)} %refs_5_.3), channel_id=1, source_target_pairs={{0,2},{1,3},{2,0},{3,1},{4,6},{5,7},{6,4},{7,5},{8,10},{9,11},{10,... | collective-permute-start | bytes 663560 | tf_op jit(solution)/shard_map/ppermute | solution.py:22
  9.2 10.3 %collective-permute-start.1 = (bf16[72,1536]{1,0:T(8,128)(2,1)}, bf16[72,1536]{1,0:T(8,128)(2,1)S(1)}, u32[]{:S(2)}, u32[]{:S(2)}) collective-permute-start(bf16[72,1536]{1,0:T(8,128)(2,1)} %fresh_ref.1), channel_id=1, source_target_pairs={{0,2},{1,3},{2,0},{3,1},{4,6},{5,7},{6,4},{7,5},{8,10},{9,11},{10,... | collective-permute-start | bytes 663560 | tf_op jit(solution)/shard_map/ppermute | solution.py:22
  11.3 8.2 %copy-start = (bf16[72,1536]{1,0:T(8,128)(2,1)S(1)}, bf16[72,1536]{1,0:T(8,128)(2,1)}, u32[]{:S(2)}) copy-start(bf16[72,1536]{1,0:T(8,128)(2,1)} %refs_5_.3) | copy-start | bytes 663556
  11.3 8.2 %copy-start.1 = (bf16[72,1536]{1,0:T(8,128)(2,1)S(1)}, bf16[72,1536]{1,0:T(8,128)(2,1)}, u32[]{:S(2)}) copy-start(bf16[72,1536]{1,0:T(8,128)(2,1)} %fresh_ref.1) | copy-start | bytes 663556
  22.0 16.8 %collective-permute-start.8 = (bf16[288,1536]{1,0:T(8,128)(2,1)S(1)}, bf16[288,1536]{1,0:T(8,128)(2,1)S(1)}, u32[]{:S(2)}, u32[]{:S(2)}) collective-permute-start(bf16[288,1536]{1,0:T(8,128)(2,1)S(1)} %get-tuple-element.40.refs_0_.fresh_mine_ref), channel_id=1, source_target_pairs={{0,1},{1,0},{2,3},{3,2},{4,5},{5,4},{6,7},{7,6},{8,9},{9,8},{10,11... | collective-permute-start | bytes 2654216 | tf_op jit(solution)/shard_map/ppermute | solution.py:22
  22.1 8.4 %collective-permute-start.2 = (bf16[72,1536]{1,0:T(8,128)(2,1)S(1)}, bf16[72,1536]{1,0:T(8,128)(2,1)S(1)}, u32[]{:S(2)}, u32[]{:S(2)}) collective-permute-start(bf16[72,1536]{1,0:T(8,128)(2,1)S(1)} %copy-done), channel_id=1, source_target_pairs={{0,4},{1,5},{2,6},{3,7},{4,0},{5,1},{6,2},{7,3},{8,12},{9,13},{10,... | collective-permute-start | bytes 663560 | tf_op jit(solution)/shard_map/ppermute | solution.py:22
  22.2 8.3 %collective-permute-start.5 = (bf16[72,1536]{1,0:T(8,128)(2,1)S(1)}, bf16[72,1536]{1,0:T(8,128)(2,1)S(1)}, u32[]{:S(2)}, u32[]{:S(2)}) collective-permute-start(bf16[72,1536]{1,0:T(8,128)(2,1)S(1)} %collective-permute-done.4.refs_2_.refs_9_), channel_id=1, source_target_pairs={{0,2},{1,3},{2,0},{3,1},{4,6},{5,7},{6,4},{7,5},{8,10},{9,11},{10,... | collective-permute-start | bytes 663560 | tf_op jit(solution)/shard_map/ppermute | solution.py:22
  23.8 10.9 %collective-permute-start.3 = (bf16[72,1536]{1,0:T(8,128)(2,1)S(1)}, bf16[72,1536]{1,0:T(8,128)(2,1)S(1)}, u32[]{:S(2)}, u32[]{:S(2)}) collective-permute-start(bf16[72,1536]{1,0:T(8,128)(2,1)S(1)} %collective-permute-done.refs_1_.refs_6_), channel_id=1, source_target_pairs={{0,4},{1,5},{2,6},{3,7},{4,0},{5,1},{6,2},{7,3},{8,12},{9,13},{10,... | collective-permute-start | bytes 663560 | tf_op jit(solution)/shard_map/ppermute | solution.py:22
  25.7 11.5 %collective-permute-start.6 = (bf16[72,1536]{1,0:T(8,128)(2,1)S(1)}, bf16[72,1536]{1,0:T(8,128)(2,1)S(1)}, u32[]{:S(2)}, u32[]{:S(2)}) collective-permute-start(bf16[72,1536]{1,0:T(8,128)(2,1)S(1)} %copy-done), channel_id=1, source_target_pairs={{0,8},{1,9},{2,10},{3,11},{4,12},{5,13},{6,14},{7,15},{16,24},{17,... | collective-permute-start | bytes 663560 | tf_op jit(solution)/shard_map/ppermute | solution.py:22
  37.2 9.4 %collective-permute-start.9 = (bf16[288,1536]{1,0:T(8,128)(2,1)S(1)}, bf16[288,1536]{1,0:T(8,128)(2,1)S(1)}, u32[]{:S(2)}, u32[]{:S(2)}) collective-permute-start(bf16[288,1536]{1,0:T(8,128)(2,1)S(1)} %get-tuple-element.41.refs_1_), channel_id=1, source_target_pairs={{0,1},{1,0},{2,3},{3,2},{4,5},{5,4},{6,7},{7,6},{8,9},{9,8},{10,11... | collective-permute-start | bytes 2654216 | tf_op jit(solution)/shard_map/ppermute | solution.py:22
  37.3 7.8 %collective-permute-start.7 = (bf16[72,1536]{1,0:T(8,128)(2,1)S(1)}, bf16[72,1536]{1,0:T(8,128)(2,1)S(1)}, u32[]{:S(2)}, u32[]{:S(2)}) collective-permute-start(bf16[72,1536]{1,0:T(8,128)(2,1)S(1)} %collective-permute-done.6.refs_0_.own_ref), channel_id=1, source_target_pairs={{0,2},{1,3},{2,0},{3,1},{4,6},{5,7},{6,4},{7,5},{8,10},{9,11},{10,... | collective-permute-start | bytes 663560 | tf_op jit(solution)/shard_map/ppermute | solution.py:22
  46.4 3.3 %collective-permute-start.10 = (bf16[144,1536]{1,0:T(8,128)(2,1)S(1)}, bf16[144,1536]{1,0:T(8,128)(2,1)S(1)}, u32[]{:S(2)}, u32[]{:S(2)}) collective-permute-start(bf16[144,1536]{1,0:T(8,128)(2,1)S(1)} %get-tuple-element.49.refs_2_), channel_id=1, source_target_pairs={{0,1},{1,0},{2,3},{3,2},{4,5},{5,4},{6,7},{7,6},{8,9},{9,8},{10,11... | collective-permute-start | bytes 1327112 | tf_op jit(solution)/shard_map/ppermute | solution.py:22
  56.7 3.2 %collective-permute-start.11 = (bf16[432,1536]{1,0:T(8,128)(2,1)S(1)}, bf16[432,1536]{1,0:T(8,128)(2,1)S(1)}, u32[]{:S(2)}, u32[]{:S(2)}) collective-permute-start(bf16[432,1536]{1,0:T(8,128)(2,1)S(1)} %get-tuple-element.58.mine_ref), channel_id=1, source_target_pairs={{0,1},{1,0},{2,3},{3,2},{4,5},{5,4},{6,7},{7,6},{8,9},{9,8},{10,11... | collective-permute-start | bytes 3981320 | tf_op jit(solution)/shard_map/ppermute | solution.py:22
